TPU v7x, 32 devices: a whole 2x2x4 slice. The times are simulated.
32 devices in a mesh: seq: 8 (over z, y), tensor: 2 (over x), section: 2 (over core).
Axes of the slice: x: 2, y: 2, z: 4, core: 2. Of those that a mesh axis runs over, the one named last changes fastest.
Arguments:
- encoder_states: bfloat16 [12288, 4096], P(('seq', 'section'), 'tensor'), may hold values from -6 to 6
- key_weight: bfloat16 [4096, 4096], P(None, 'tensor'), may hold values from -0.125 to 0.125
- value_weight: bfloat16 [4096, 4096], P(None, 'tensor'), may hold values from -0.125 to 0.125
- queries: bfloat16 [4096, 4096], P(('seq', 'section'), 'tensor'), may hold values from -400 to 400
- out_grad: bfloat16 [4096, 4096], P(('seq', 'section'), 'tensor'), may hold values from -6 to 6
- band_blocks: int32 [32, 2], P(('seq', 'section')), may hold values from 0 to 95, as said below
Outputs:
- query_grad: bfloat16 [4096, 4096], P(('seq', 'section'), 'tensor')
- encoder_grad: bfloat16 [12288, 4096], P(('seq', 'section'), 'tensor')
Inputs may be any that keep to these rules, and one draw needn't show every extreme that they name: band_blocks[b] holds the first and the last encoder block (inclusive, blocks of 128 frames) that decoder block b attends to; both rise with b; the first lies in 3 * b - 2 to 3 * b - 1 and the last in 3 * b + 3 to 3 * b + 4, each clipped to the encoder's blocks; some band spans exactly 7 encoder blocks.
All inputs are finite; a program needn't handle non-finite values.
Results may differ from a plain program's by a relative error of at most 0.006.
The roundings to bfloat16 on the way count: a program that leaves them out, or rounds other values in their place, can miss the bound.
Values may be sent and summed in bfloat16 or wider, within the bound.
No kernel may reach another device: no remote copies, remote signals or barrier semaphores. Data moves between devices by JAX's collectives and lax.ppermute only.
A program may use at most 192 MiB of HBM per device.

v0:
```python
import functools
import math

import jax
import jax.numpy as jnp
from jax import lax
from jax.experimental import pallas as pl
from jax.experimental.pallas import tpu as pltpu
from jax.sharding import PartitionSpec as P


DH = 128
BLOCK = 128
RATIO = 3
HALO_BLK = 2
NEG = -1e30
WINDOW = 3
PER_STATS = 4
PER_GRADIENTS = 4
ROWS = ("seq", "section")
NT = (((1,), (1,)), ((), ()))
TN = (((0,), (0,)), ((), ()))
F32 = jnp.float32
BF16 = jnp.bfloat16


ANYWHERE = pl.BlockSpec(memory_space=pltpu.HBM)
HERE = pl.BlockSpec(memory_space=pltpu.VMEM)
SCALARS = pl.BlockSpec(memory_space=pltpu.SMEM)


def call(body, in_specs, out_specs, out_shape, scratch, flops, moved, aliases=None):
    return pl.pallas_call(
        body,
        in_specs=in_specs,
        out_specs=out_specs,
        out_shape=out_shape,
        scratch_shapes=scratch,
        input_output_aliases=aliases or {},
        compiler_params=pltpu.CompilerParams(vmem_limit_bytes=limit_of(scratch)),
        cost_estimate=pl.CostEstimate(flops=flops, bytes_accessed=moved, transcendentals=0),
    )


def limit_of(scratch):
    held = 0
    for item in scratch:
        if item.dtype in (BF16, F32):
            held += math.prod(item.shape) * jnp.dtype(item.dtype).itemsize
    return held + 3 * 2**20


def lanes_at(step, wide):
    return pl.ds(pl.multiple_of(step * wide, wide), wide)


class Weights:
    def __init__(self, key_weight, by_columns, group):
        rows, columns = key_weight.shape
        self.features = rows // group
        self.by_columns = by_columns
        if by_columns:
            self.step = min(256, columns)
            self.steps = columns // self.step
            self.block = (self.features, self.step)
        else:
            self.step = min(256, self.features)
            self.steps = self.features // self.step
            self.block = (self.step, columns)

    def buffer_shape(self, count):
        return (count, 2, self.steps) + self.block

    def scratch(self, count):
        return pltpu.VMEM(self.buffer_shape(count), BF16)

    def semaphores(self, count):
        return pltpu.SemaphoreType.DMA((count, 2, self.steps))

    def copy(self, refs, buffer, sems, owner, at, which, step):
        if self.by_columns:
            first = pl.multiple_of(owner * self.features, self.features)
            source = refs[which].at[pl.ds(first, self.features), lanes_at(step, self.step)]
        else:
            first = pl.multiple_of(owner * self.features + step * self.step, self.step)
            source = refs[which].at[pl.ds(first, self.step), :]
        return pltpu.make_async_copy(
            source, buffer.at[at, which, step], sems.at[at, which, step]
        )

    def start_step(self, refs, buffer, sems, owners, step):
        for at, owner in enumerate(owners):
            for which in range(2):
                self.copy(refs, buffer, sems, owner, at, which, step).start()

    def start(self, refs, buffer, sems, owners, window=None):
        for step in range(min(self.steps, window or self.steps)):
            self.start_step(refs, buffer, sems, owners, step)

    def wait(self, refs, buffer, sems, owners, step):
        for at, owner in enumerate(owners):
            for which in range(2):
                self.copy(refs, buffer, sems, owner, at, which, step).wait()

    def advance(self, refs, buffer, sems, owners, step):
        self.wait(refs, buffer, sems, owners, step)

        @pl.when(step + WINDOW < self.steps)
        def _():
            self.start_step(refs, buffer, sems, owners, step + WINDOW)


def sources(group):
    me = lax.axis_index("tensor")
    return [lax.rem(me - k + group, group) for k in range(group)]


def targets(group):
    me = lax.axis_index("tensor")
    return [lax.rem(me + k, group) for k in range(group)]


def take_rows(states, cuts):
    def body(states_ref, *refs):
        outs, sems = refs[:-1], refs[-1]
        copies = []
        for i, (first, last) in enumerate(cuts):
            copies.append(
                pltpu.make_async_copy(states_ref.at[pl.ds(first, last - first), :], outs[i], sems.at[i])
            )
            copies[-1].start()
        for copy in copies:
            copy.wait()

    shapes = [jax.ShapeDtypeStruct((last - first, states.shape[1]), BF16) for first, last in cuts]
    return call(
        body,
        [ANYWHERE],
        [HERE] * len(cuts),
        shapes,
        [pltpu.SemaphoreType.DMA((len(cuts),))],
        0,
        4 * sum(math.prod(shape.shape) for shape in shapes),
    )(pltpu.with_memory_space_constraint(states, pltpu.HBM))


def project_own(states, queries, grads, key_weight, value_weight, cuts, group):
    rows, depth = states.shape
    columns = key_weight.shape[1]
    tokens = queries.shape[0]
    weights = Weights(key_weight, True, group)
    count = len(cuts)

    def body(states_ref, query_ref, grad_ref, key_ref, value_ref, *refs):
        outs = refs[: 2 * count]
        up_ref, down_ref = refs[2 * count : 2 * count + 2]
        buffer, sems = refs[2 * count + 2 :]
        owners = sources(group)[:1]
        both = (key_ref, value_ref)
        weights.start(both, buffer, sems, owners, WINDOW)
        for at, ref in enumerate((query_ref, grad_ref)):
            lanes = slice(at * columns, (at + 1) * columns)
            up_ref[:, lanes] = ref[tokens - BLOCK :, :]
            down_ref[:, lanes] = ref[:BLOCK, :]

        def step(j, carry):
            weights.advance(both, buffer, sems, owners, j)
            for which in range(2):
                product = jnp.dot(
                    states_ref[...], buffer[0, which, j], preferred_element_type=F32
                )
                for piece_at, (first, last) in enumerate(cuts):
                    outs[2 * piece_at + which][:, lanes_at(j, weights.step)] = product[first:last]
            return carry

        lax.fori_loop(0, weights.steps, step, 0)

    shapes = []
    for first, last in cuts:
        shapes += [jax.ShapeDtypeStruct((last - first, columns), F32)] * 2
    edge = jax.ShapeDtypeStruct((BLOCK, 2 * columns), BF16)
    out = call(
        body,
        [HERE] * 3 + [ANYWHERE] * 2,
        [HERE] * (len(shapes) + 2),
        shapes + [edge, edge],
        [weights.scratch(1), weights.semaphores(1)],
        4 * rows * depth * columns,
        2 * rows * depth + 4 * depth * columns,
    )(states, queries, grads, key_weight, value_weight)
    return [(out[2 * i], out[2 * i + 1]) for i in range(count)], out[-2], out[-1]


def project_rest(partial, arrived, key_weight, value_weight, held, group):
    rows, columns = partial[0].shape
    depth = arrived[0].shape[1]
    count = len(arrived)
    weights = Weights(key_weight, True, group)
    loads = held is None

    def body(key_part, value_part, *refs):
        pieces, refs = refs[:count], refs[count:]
        if loads:
            both, outs, (buffer, sems) = refs[:2], refs[2:4], refs[4:]
            owners = sources(group)[1:]
            weights.start(both, buffer, sems, owners, WINDOW)
        else:
            buffer, outs = refs[0], refs[1:]

        def step(j, carry):
            if loads:
                weights.advance(both, buffer, sems, owners, j)
            here = lanes_at(j, weights.step)
            for which, part_ref in enumerate((key_part, value_part)):
                total = part_ref[:, here]
                for at in range(count):
                    total = total + jnp.dot(
                        pieces[at][...], buffer[at, which, j], preferred_element_type=F32
                    )
                outs[which][:, here] = total.astype(BF16)
            return carry

        lax.fori_loop(0, weights.steps, step, 0)

    shapes = [jax.ShapeDtypeStruct((rows, columns), BF16)] * 2
    if loads:
        shapes.append(jax.ShapeDtypeStruct(weights.buffer_shape(count), BF16))
    out = call(
        body,
        [HERE] * (2 + count) + ([ANYWHERE] * 2 if loads else [HERE]),
        [HERE] * len(shapes),
        shapes,
        [weights.semaphores(count)] if loads else [],
        4 * rows * depth * columns * count,
        4 * depth * columns * count if loads else 2 * rows * columns,
    )(*partial, *arrived, *((key_weight, value_weight) if loads else (held,)))
    return (out[0], out[1]), (out[2] if loads else held)


def certain(token, frame):
    return RATIO * token - 1 <= frame <= RATIO * token + RATIO


def reaches(token, frame):
    return RATIO * token - HALO_BLK <= frame <= RATIO * token + RATIO - 1 + HALO_BLK


class Tiles:
    def __init__(self, tokens, first, last, halo):
        self.first, self.last, self.tokens = first, last, tokens
        low, high = (-1, tokens + 1) if halo else (0, tokens)
        touched = [
            t for t in range(low, high) if any(reaches(t, f) for f in range(first, last))
        ]
        whole = [t for t in touched if all(reaches(t, f) for f in range(first, last))]
        self.groups = []
        if whole:
            self.groups.append((whole, first, last))
        for t in touched:
            if t not in whole:
                frames = [f for f in range(first, last) if reaches(t, f)]
                self.groups.append(([t], frames[0], frames[-1] + 1))
        self.touched = touched


class Tokens:
    def __init__(self, own_count, columns, refs):
        self.own_count, self.columns = own_count, columns
        self.query_ref, self.grad_ref = refs[:2]
        self.below_ref, self.above_ref = refs[2:] if len(refs) > 2 else (None, None)

    def rows(self, tokens, head, grads):
        own_ref = self.grad_ref if grads else self.query_ref
        lanes = lanes_at(head, DH)
        halo = lanes_at(head + (self.columns // DH if grads else 0), DH)
        pieces = []
        for t in tokens:
            if t < 0:
                pieces.append(self.below_ref[:, halo])
            elif t >= self.own_count:
                pieces.append(self.above_ref[:, halo])
            else:
                pieces.append(own_ref[t * BLOCK : (t + 1) * BLOCK, lanes])
        return pieces[0] if len(pieces) == 1 else jnp.concatenate(pieces, axis=0)


class Bands:
    def __init__(self, refs, own_count):
        self.below_ref, self.own_ref, self.above_ref = refs
        self.own_count = own_count
        self.place, self.places = lax.axis_index(ROWS), lax.axis_size(ROWS)

    def allowed(self, token, frame):
        inside = None
        if token < 0:
            ref, row = self.below_ref, self.own_count + token
            inside = self.place > 0
        elif token >= self.own_count:
            ref, row = self.above_ref, token - self.own_count
            inside = self.place < self.places - 1
        elif certain(token, frame):
            return None
        else:
            ref, row = self.own_ref, token
        at = self.place * (RATIO * self.own_count) + frame
        held = (ref[row, 0] <= at) & (at <= ref[row, 1])
        return held if inside is None else held & inside


def head_tiles(tiles, tokens, key_ref, value_ref, head):
    lanes = lanes_at(head, DH)
    for group, first, last in tiles.groups:
        rows = slice((first - tiles.first) * BLOCK, (last - tiles.first) * BLOCK)
        keys, values = key_ref[rows, lanes], value_ref[rows, lanes]
        query_rows = tokens.rows(group, head, False)
        grad_rows = tokens.rows(group, head, True)
        scores = lax.dot_general(keys, query_rows, NT, preferred_element_type=F32)
        slopes = lax.dot_general(values, grad_rows, NT, preferred_element_type=F32)
        yield group, first, last, keys, query_rows, grad_rows, scores, slopes


def piece(array, frame, position):
    return array[frame * BLOCK : (frame + 1) * BLOCK, position * BLOCK : (position + 1) * BLOCK]


def fold(stats, rate):
    tops = [jnp.where(total > 0, top, NEG) for top, total, _ in stats]
    top = functools.reduce(jnp.maximum, tops)
    gains = [jnp.exp2((t - top) * rate) for t in tops]
    total = sum(g * s[1] for g, s in zip(gains, stats))
    weighted = sum(g * s[2] for g, s in zip(gains, stats))
    return top, total, weighted


def tile_stats(bands, tiles_list, tokens, kv_refs, head, rate):
    found = {}
    for tiles, (key_ref, value_ref) in zip(tiles_list, kv_refs):
        for group, first, last, _, _, _, scores, slopes in head_tiles(
            tiles, tokens, key_ref, value_ref, head
        ):
            for position, t in enumerate(group):
                for f in range(first, last):
                    allowed = bands.allowed(t, f)
                    found.setdefault(t, []).append(
                        (allowed, piece(scores, f - first, position), piece(slopes, f - first, position))
                    )
    stats = {}
    for t, entries in found.items():
        shown = [s if a is None else jnp.where(a, s, NEG) for a, s, _ in entries]
        top = jnp.max(functools.reduce(jnp.maximum, shown), axis=0, keepdims=True)
        total = weighted = None
        for (allowed, _, slope), s in zip(entries, shown):
            e = jnp.exp2((s - top) * rate)
            if allowed is not None:
                e = jnp.where(allowed, e, 0.0)
            total = e if total is None else total + e
            weighted = e * slope if weighted is None else weighted + e * slope
        stats[t] = (
            top,
            jnp.sum(total, axis=0, keepdims=True),
            jnp.sum(weighted, axis=0, keepdims=True),
        )
    return stats


def read_stats(ref, head, row):
    return tuple(ref[head, row + i : row + i + 1, :] for i in range(3))


def stat_depth(own_count):
    return -(-3 * (own_count + 2) // 8) * 8


def row_stats(
    band, tiles_list, kvs, queries, grads, below, above, earlier, last, rate
):
    own_count = queries.shape[0] // BLOCK
    columns = queries.shape[1]
    heads = columns // DH
    per = min(PER_STATS, heads)
    depth = stat_depth(own_count)
    count = len(kvs)
    halo = any(t < 0 or t >= own_count for tiles in tiles_list for t in tiles.touched)
    shared = (queries, grads) + ((below, above) if halo else ())
    extra = [] if earlier is None else [earlier]

    def body(*refs):
        bands, refs = Bands(refs[:3], own_count), refs[3:]
        tokens = Tokens(own_count, columns, refs[: len(shared)])
        refs = refs[len(shared) :]
        kv_refs = [refs[2 * i : 2 * i + 2] for i in range(count)]
        rest = refs[2 * count :]
        out_ref = rest[len(extra)]
        even = lax.rem(lax.axis_index(ROWS), 2) == 0

        def step(pair, carry):
            for k in range(per):
                head = pair * per + k
                stats = tile_stats(bands, tiles_list, tokens, kv_refs, head, rate)
                results = []
                for t in range(-1, own_count + 1):
                    mine = [stats[t]] if t in stats else []
                    if extra:
                        mine.append(read_stats(rest[0], head, 3 * (t + 1)))
                    results += mine[0] if len(mine) == 1 else fold(mine, rate)
                blank = [jnp.zeros((1, BLOCK), F32)]
                out_ref[head] = jnp.concatenate(
                    results + blank * (depth - len(results)), axis=0
                )
                if last:
                    lower, upper = results[:6], results[-6:]
                    for ref, flag in zip(rest[len(extra) + 1 :], (even, jnp.logical_not(even))):
                        picked = [jnp.where(flag, u, d) for u, d in zip(upper, lower)]
                        ref[head] = jnp.concatenate(picked + blank * 2, axis=0)
            return carry

        lax.fori_loop(0, heads // per, step, 0)

    frames = sum(kv[0].shape[0] for kv in kvs)
    flat = [array for kv in kvs for array in kv]
    shapes = [jax.ShapeDtypeStruct((heads, depth, BLOCK), F32)]
    if last:
        shapes += [jax.ShapeDtypeStruct((heads, 8, BLOCK), F32)] * 2
    return call(
        body,
        [SCALARS] * 3
        + [HERE] * len(shared)
        + [HERE] * (len(flat) + len(extra)),
        [HERE] * len(shapes),
        shapes,
        [],
        8 * frames * 2 * BLOCK * columns,
        4 * frames * columns + 8 * queries.size,
    )(*band, *shared, *flat, *extra)


def term_block(buffer, at, step, key_ref, value_ref, rows, out_ref):
    term = lax.dot_general(
        key_ref[rows, :], buffer[at, 0, step], NT, preferred_element_type=F32
    ) + lax.dot_general(value_ref[rows, :], buffer[at, 1, step], NT, preferred_element_type=F32)
    out_ref[:, lanes_at(step, buffer.shape[3])] = term.astype(BF16)


def gradients(
    band,
    tiles,
    kv,
    queries,
    grads,
    below,
    above,
    stats,
    swaps,
    key_weight,
    value_weight,
    held,
    deferred,
    totals,
    rate,
    scale,
    group,
):
    own_count = queries.shape[0] // BLOCK
    columns = queries.shape[1]
    heads = columns // DH
    per = min(PER_GRADIENTS, heads)
    frames = kv[0].shape[0]
    touched = tiles.touched
    halo_touched = [t for t in touched if not 0 <= t < own_count]
    shared = (queries, grads) + ((below, above) if halo_touched else ())
    weights = Weights(key_weight, False, group)
    steps, features = weights.steps, weights.features
    loads = held is None
    sources_in = [key_weight, value_weight] if loads else [held]
    defer = not halo_touched
    extra = [] if defer else list(deferred)
    earlier = [] if totals is None else list(totals)
    base = tiles.first * BLOCK
    ahead = min(4, weights.steps)

    def body(*refs):
        bands, refs = Bands(refs[:3], own_count), refs[3:]
        tokens = Tokens(own_count, columns, refs[: len(shared)])
        refs = refs[len(shared) :]
        key_ref, value_ref, stat_ref, even_ref, odd_ref = refs[:5]
        both, refs = refs[5 : 5 + len(sources_in)], refs[5 + len(sources_in) :]
        extra_refs, refs = refs[: len(extra)], refs[len(extra) + len(earlier) :]
        if loads:
            buffer, sems, refs = refs[-2], refs[-1], refs[:-2]
            owners = targets(group)[1:]
            weights.start(both, buffer, sems, owners, ahead)
        else:
            buffer = both[0]
        key_out, value_out, own_out = refs[:3]
        term_outs = refs[3 : 2 + group]
        halo_outs = refs[2 + group :]
        even = lax.rem(lax.axis_index(ROWS), 2) == 0

        def one(head):
            lanes = lanes_at(head, DH)
            rows = {}
            for t in touched:
                parts = [read_stats(stat_ref, head, 3 * (t + 1))]
                if t <= 0:
                    row = 3 * (t + 1)
                    first, second = read_stats(odd_ref, head, row), read_stats(even_ref, head, row)
                    parts.append([jnp.where(even, a, b) for a, b in zip(first, second)])
                if t >= own_count - 1:
                    row = 3 * (t - own_count + 1)
                    first, second = read_stats(even_ref, head, row), read_stats(odd_ref, head, row)
                    parts.append([jnp.where(even, a, b) for a, b in zip(first, second)])
                top, total, weighted = fold(parts, rate)
                rows[t] = (top * rate + jnp.log2(total), weighted / total)
            key_sum = [None] * (tiles.last - tiles.first)
            value_sum = [None] * (tiles.last - tiles.first)
            query_sum = {}
            if extra:
                query_part = lax.dot_general(
                    extra_refs[1][head], extra_refs[0][:, lanes], TN, preferred_element_type=F32
                )
                for t in range(own_count):
                    query_sum[t] = query_part[t * BLOCK : (t + 1) * BLOCK]
            for group_tokens, first, last, keys, query_rows, grad_rows, scores, slopes in head_tiles(
                tiles, tokens, key_ref, value_ref, head
            ):
                low, slope_low = [], []
                for f in range(first, last):
                    low_row, slope_row = [], []
                    for position, t in enumerate(group_tokens):
                        level, delta = rows[t]
                        p = jnp.exp2(piece(scores, f - first, position) * rate - level)
                        d = p * (piece(slopes, f - first, position) - delta) * scale
                        allowed = bands.allowed(t, f)
                        if allowed is not None:
                            p = jnp.where(allowed, p, 0.0)
                            d = jnp.where(allowed, d, 0.0)
                        low_row.append(p.astype(BF16))
                        slope_row.append(d.astype(BF16))
                    low.append(jnp.concatenate(low_row, axis=1))
                    slope_low.append(jnp.concatenate(slope_row, axis=1))
                low = jnp.concatenate(low, axis=0)
                slope_low = jnp.concatenate(slope_low, axis=0)
                key_part = jnp.dot(slope_low, query_rows, preferred_element_type=F32)
                value_part = jnp.dot(low, grad_rows, preferred_element_type=F32)
                if defer:
                    own_out[head] = slope_low
                else:
                    query_part = lax.dot_general(slope_low, keys, TN, preferred_element_type=F32)
                    for position, t in enumerate(group_tokens):
                        part = query_part[position * BLOCK : (position + 1) * BLOCK]
                        query_sum[t] = query_sum[t] + part if t in query_sum else part
                for f in range(first, last):
                    at, cut = f - tiles.first, slice((f - first) * BLOCK, (f - first + 1) * BLOCK)
                    for sums, part in ((key_sum, key_part), (value_sum, value_part)):
                        sums[at] = part[cut] if sums[at] is None else sums[at] + part[cut]
            for at in range(tiles.last - tiles.first):
                cut = slice(base + at * BLOCK, base + (at + 1) * BLOCK)
                key_out[cut, lanes] = key_sum[at].astype(BF16)
                value_out[cut, lanes] = value_sum[at].astype(BF16)
            if not defer:
                for t in range(own_count):
                    own_out[t * BLOCK : (t + 1) * BLOCK, lanes] = query_sum[t]
                for out_ref, t in zip(halo_outs, halo_touched):
                    out_ref[:, lanes] = query_sum[t]

        def step(pair, carry):
            for k in range(per):
                one(pair * per + k)
            if loads:

                @pl.when(pair + ahead < steps)
                def _():
                    weights.wait(both, buffer, sems, owners, pair)
                    weights.start_step(both, buffer, sems, owners, pair + ahead)

            return carry

        lax.fori_loop(0, heads // per, step, 0)
        done = min(heads // per, steps - ahead)
        if loads:
            for j in range(done + ahead, steps):
                weights.start_step(both, buffer, sems, owners, j)

        def term_step(j, carry):
            if loads:

                @pl.when(j >= done)
                def _():
                    weights.wait(both, buffer, sems, owners, j)

            for at, out_ref in enumerate(term_outs):
                term_block(buffer, at, j, key_out, value_out, slice(base, base + frames), out_ref)
            return carry

        lax.fori_loop(0, steps, term_step, 0)

    shapes = (
        [jax.ShapeDtypeStruct((RATIO * own_count * BLOCK, columns), BF16)] * 2
        + [
            jax.ShapeDtypeStruct((heads, frames, own_count * BLOCK), BF16)
            if defer
            else jax.ShapeDtypeStruct((own_count * BLOCK, columns), F32)
        ]
        + [jax.ShapeDtypeStruct((frames, features), BF16)] * (group - 1)
        + [jax.ShapeDtypeStruct((BLOCK, columns), F32)] * len(halo_touched)
        + ([jax.ShapeDtypeStruct(weights.buffer_shape(group - 1), BF16)] if loads else [])
    )
    out = call(
        body,
        [SCALARS] * 3
        + [HERE] * (len(shared) + 5)
        + ([ANYWHERE] * 2 if loads else [HERE])
        + [HERE] * (len(extra) + len(earlier)),
        [HERE] * len(shapes),
        shapes,
        [weights.semaphores(group - 1)] if loads else [],
        20 * frames * 2 * BLOCK * columns + 4 * frames * columns * features * (group - 1),
        8 * frames * columns,
        {8 + len(shared) + len(sources_in) + len(extra) + i: i for i in range(len(earlier))},
    )(*band, *shared, *kv, stats, *swaps, *sources_in, *extra, *earlier)
    halo = dict(zip(halo_touched, out[2 + group :]))
    return out[:2], out[2], out[3 : 2 + group], halo, out[-1] if loads else held


def own_terms(totals, key_weight, value_weight, group):
    rows, columns = totals[0].shape
    weights = Weights(key_weight, False, group)

    def body(key_grad_ref, value_grad_ref, key_ref, value_ref, out_ref, buffer, sems):
        both = key_ref, value_ref
        owners = targets(group)[:1]
        weights.start(both, buffer, sems, owners, WINDOW)

        def step(j, carry):
            weights.advance(both, buffer, sems, owners, j)
            term_block(buffer, 0, j, key_grad_ref, value_grad_ref, slice(0, rows), out_ref)
            return carry

        lax.fori_loop(0, weights.steps, step, 0)

    return call(
        body,
        [HERE] * 2 + [ANYWHERE] * 2,
        HERE,
        jax.ShapeDtypeStruct((rows, weights.features), BF16),
        [weights.scratch(1), weights.semaphores(1)],
        4 * rows * columns * weights.features,
        4 * columns * weights.features,
    )(*totals, key_weight, value_weight)


def finish_queries(low, high, from_below, from_above):
    rows, columns = low.shape
    tall = BLOCK
    steps = rows // tall

    def body(low_ref, high_ref, below_ref, above_ref, out_ref, buffer, sems):
        copies = []
        for i in range(steps):
            cut = slice(i * tall, (i + 1) * tall)
            total = low_ref[cut, :] + high_ref[cut, :]
            if i == 0:
                total = total + below_ref[...]
            if i == steps - 1:
                total = total + above_ref[...]
            buffer[i] = total.astype(BF16)
            copies.append(pltpu.make_async_copy(buffer.at[i], out_ref.at[pl.ds(i * tall, tall), :], sems.at[i]))
            copies[-1].start()
        for copy in copies:
            copy.wait()

    return call(
        body,
        [HERE] * 4,
        ANYWHERE,
        pltpu.HBM((rows, columns), BF16),
        [pltpu.VMEM((steps, tall, columns), BF16), pltpu.SemaphoreType.DMA((steps,))],
        4 * rows * columns,
        12 * rows * columns,
    )(low, high, from_below, from_above)


def add_rows(target, own, arrived, first):
    rows, features = arrived[0].shape
    tall = BLOCK // 2
    steps = rows // tall
    count = len(arrived)

    def body(own_ref, *refs):
        terms = refs[:count]
        out_ref, buffer, sems = refs[-3:]
        copies = []
        for i in range(steps):
            value = own_ref[first + i * tall : first + (i + 1) * tall, :].astype(F32)
            for ref in terms:
                value = value + ref[i * tall : (i + 1) * tall, :].astype(F32)
            buffer[i] = value.astype(BF16)
            copy = pltpu.make_async_copy(
                buffer.at[i], out_ref.at[pl.ds(first + i * tall, tall), :], sems.at[i]
            )
            copy.start()
            copies.append(copy)
        for copy in copies:
            copy.wait()

    extra = [] if target is None else [target]
    return call(
        body,
        [HERE] * (1 + count) + [ANYWHERE] * len(extra),
        ANYWHERE,
        pltpu.HBM(own.shape, own.dtype),
        [pltpu.VMEM((steps, tall, features), BF16), pltpu.SemaphoreType.DMA((steps,))],
        rows * features * count,
        2 * rows * features * (count + 2),
        {1 + count: 0} if extra else None,
    )(own, *arrived, *extra)


def shifted(value, steps):
    count = lax.axis_size(ROWS)
    first, last = (max(0, -steps), min(count, count - steps))
    return lax.ppermute(value, ROWS, [(source, source + steps) for source in range(first, last)])


def swapped(value, first):
    pairs = []
    for at in range(first, lax.axis_size(ROWS) - 1, 2):
        pairs += [(at, at + 1), (at + 1, at)]
    return lax.ppermute(value, ROWS, pairs)


def on_device(encoder_states, key_weight, value_weight, queries, out_grad, band_blocks):
    frames = encoder_states.shape[0]
    tokens = queries.shape[0]
    own_count = tokens // BLOCK
    frame_blocks = frames // BLOCK
    scale = DH ** (-0.5)
    rate = scale * math.log2(math.e)
    group = lax.axis_size("tensor")
    edge = HALO_BLK
    middle = frame_blocks // 2
    cuts = [(0, edge), (frame_blocks - edge, frame_blocks), (edge, middle), (middle, frame_blocks - edge)]
    row_cuts = [(first * BLOCK, last * BLOCK) for first, last in cuts]
    turns = [[(i, (i + k) % group) for i in range(group)] for k in range(1, group)]

    key_weight, value_weight = [
        pltpu.with_memory_space_constraint(w, pltpu.HBM) for w in (key_weight, value_weight)
    ]
    arrived = []
    for rows in take_rows(encoder_states, row_cuts[:1]) + take_rows(encoder_states, row_cuts[1:]):
        arrived.append([lax.ppermute(rows, "tensor", turn) for turn in turns])

    partial, edge_up, edge_down = project_own(
        encoder_states, queries, out_grad, key_weight, value_weight, row_cuts, group
    )
    edge_up, edge_down, band_sent = lax.optimization_barrier((edge_up, edge_down, band_blocks))
    below = shifted(edge_up, 1)
    above = shifted(edge_down, -1)
    band = (shifted(band_sent, 1), band_blocks, shifted(band_sent, -1))

    kvs, held = [], None
    for part, pieces in zip(partial, arrived):
        kv, held = project_rest(part, pieces, key_weight, value_weight, held, group)
        kvs.append(kv)

    tiles = [Tiles(own_count, first, last, i < 2) for i, (first, last) in enumerate(cuts)]
    shared = (queries, out_grad, below, above)
    (stats,) = row_stats(band, tiles[:2], kvs[:2], *shared, None, False, rate)
    (stats,) = row_stats(band, tiles[2:3], kvs[2:3], *shared, stats, False, rate)
    stats, first_swap, second_swap = row_stats(
        band, tiles[3:], kvs[3:], *shared, stats, True, rate
    )
    swaps = (swapped(first_swap, 0), swapped(second_swap, 1))

    out = [None] * 4
    sent = [None] * 4
    totals = away = None
    for i in (2, 3, 0, 1):
        deferred = (kvs[2 + i][0], out[2 + i][1]) if i < 2 else None
        out[i] = gradients(
            band,
            tiles[i],
            kvs[i],
            *shared,
            stats,
            swaps,
            key_weight,
            value_weight,
            away,
            deferred,
            totals,
            rate,
            scale,
            group,
        )
        totals, away = out[i][0], out[i][4]
        sent[i] = [lax.ppermute(term, "tensor", turn) for term, turn in zip(out[i][2], turns)]

    from_below = shifted(out[1][3][own_count], 1)
    from_above = shifted(out[0][3][-1], -1)
    own = own_terms(totals, key_weight, value_weight, group)
    query_grad = finish_queries(out[0][1], out[1][1], from_below, from_above)

    encoder_grad = None
    for i in (2, 3, 0, 1):
        encoder_grad = add_rows(encoder_grad, own, sent[i], row_cuts[i][0])
    return (query_grad, encoder_grad)


def solution(mesh):
    return jax.shard_map(
        on_device,
        mesh=mesh,
        in_specs=(
            P(ROWS, "tensor"),
            P(None, "tensor"),
            P(None, "tensor"),
            P(ROWS, "tensor"),
            P(ROWS, "tensor"),
            P(ROWS, None),
        ),
        out_specs=(P(ROWS, "tensor"), P(ROWS, "tensor")),
        check_vma=False,
    )
```

profile of v0, /device:TPU:0, one launch (start us, length us, event | category | flops | bytes accessed | tf_op | source)
XLA Modules:
  0.0 203.7 jit_solution(279349792564415716)
XLA Ops:
  0.6 0.0 copy-start.2
  0.6 0.0 copy-start.1
  0.7 0.0 copy-start
  0.7 1.4 shard_map.78
  2.1 3.0 %collective-permute-start.4 = (bf16[256,2048]{1,0:T(8,128)(2,1)S(1)}, bf16[256,2048]{1,0:T(8,128)(2,1)S(1)}, u32[]{:S(2)}, u32[]{:S(2)}) collective-permute-start(bf16[256,2048]{1,0:T(8,128)(2,1)S(1)} %shard_map.78), channel_id=1, source_target_pairs={{0,2},{2,0},{1,3},{3,1},{4,6},{6,4},{5,7},{7,5},{8,10},{10,8},{9,1... | collective-permute-start | bytes 3145736 | tf_op jit(solution)/shard_map/ppermute | solution.py:751
  5.1 1.5 shard_map.80
  6.6 0.5 collective-permute-start.5
  7.1 1.6 collective-permute-start.6
  8.7 0.4 collective-permute-start.7
  9.1 0.0 copy-done.2
  9.1 0.0 copy-done.1
  9.1 0.0 copy-done
  9.1 16.1 %shard_map.77 = (f32[256,2048]{1,0:T(8,128)S(1)}, f32[256,2048]{1,0:T(8,128)S(1)}, f32[256,2048]{1,0:T(8,128)S(1)}, f32[256,2048]{1,0:T(8,128)S(1)}, f32[128,204...) custom-call(bf16[768,2048]{1,0:T(8,128)(2,1)S(1)} %copy-done.2, ...), custom_call_target="tpu_custom_call" | custom-call | flops 12884901888 | bytes 19922944 | tf_op jit(solution)/shard_map/pallas_call | solution.py:182
  25.2 1.4 collective-permute-start.2
  26.6 2.5 %collective-permute-done.4.refs_0_ = bf16[256,2048]{1,0:T(8,128)(2,1)S(1)} collective-permute-done((bf16[256,2048]{1,0:T(8,128)(2,1)S(1)}, bf16[256,2048]{1,0:T(8,128)(2,1)S(1)}, u32[]{:S(2)}, u32[]{:S(2)}) %collective-permute-start.4) | collective-permute-done | bytes 1048608 | tf_op jit(solution)/shard_map/ppermute | solution.py:751
  29.1 1.3 collective-permute-start.3
  30.4 0.0 copy-start.3
  30.4 7.5 %shard_map.79 = (bf16[256,2048]{1,0:T(8,128)(2,1)S(1)}, bf16[256,2048]{1,0:T(8,128)(2,1)S(1)}, bf16[1,2,8,2048,256]{4,3,2,1,0:T(8,128)(2,1)S(1)}) custom-call(f32[256,2048]{1,0:T(8,128)S(1)} %get-tuple-element.54.key_part, f32[256,2048]{1,0:T(8,128)S(1)} %get-tuple-element.55.value_part, bf16[256,2048]{1,0:T(8,128)(2,1)S(1)} %collective-permute-done.4.refs_0_, ...), custom_call_target="tpu_custom_call" | custom-call | flops 4294967296 | bytes 16777216 | tf_op jit(solution)/shard_map/pallas_call | solution.py:228
  37.9 13.7 %collective-permute-done.6.refs_0_ = bf16[128,2048]{1,0:T(8,128)(2,1)S(1)} collective-permute-done((bf16[128,2048]{1,0:T(8,128)(2,1)S(1)}, bf16[128,2048]{1,0:T(8,128)(2,1)S(1)}, u32[]{:S(2)}, u32[]{:S(2)}) %collective-permute-start.6) | collective-permute-done | bytes 524320 | tf_op jit(solution)/shard_map/ppermute | solution.py:751
  51.6 0.0 copy-done.3
  51.6 1.3 collective-permute-start.1
  52.9 3.7 %shard_map.82 = (bf16[128,2048]{1,0:T(8,128)(2,1)S(1)}, bf16[128,2048]{1,0:T(8,128)(2,1)S(1)}) custom-call(f32[128,2048]{1,0:T(8,128)S(1)} %get-tuple-element.64.key_part, f32[128,2048]{1,0:T(8,128)S(1)} %get-tuple-element.65.value_part, bf16[128,2048]{1,0:T(8,128)(2,1)S(1)} %collective-permute-done.6.refs_0_, ...), custom_call_target="tpu_custom_call" | custom-call | flops 2147483648 | bytes 524288 | tf_op jit(solution)/shard_map/pallas_call | solution.py:228
  56.5 0.0 collective-permute-done.5.refs_0_
  56.5 3.0 %collective-permute-start = (s32[2,2]{1,0:T(2,128)S(1)}, s32[2,2]{1,0:T(2,128)S(1)}, u32[]{:S(2)}, u32[]{:S(2)}) collective-permute-start(s32[2,2]{1,0:T(2,128)S(1)} %copy-done.3), channel_id=1, source_target_pairs={{0,1},{1,4},{4,5},{5,8},{8,9},{9,12},{12,13},{13,16},{16,17},{17,2... | collective-permute-start | bytes 56 | tf_op jit(solution)/shard_map/ppermute | solution.py:722
  59.6 3.6 %shard_map.81 = (bf16[128,2048]{1,0:T(8,128)(2,1)S(1)}, bf16[128,2048]{1,0:T(8,128)(2,1)S(1)}) custom-call(f32[128,2048]{1,0:T(8,128)S(1)} %get-tuple-element.58.key_part, f32[128,2048]{1,0:T(8,128)S(1)} %get-tuple-element.59.value_part, bf16[128,2048]{1,0:T(8,128)(2,1)S(1)} %collective-permute-done.5.refs_0_, ...), custom_call_target="tpu_custom_call" | custom-call | flops 2147483648 | bytes 524288 | tf_op jit(solution)/shard_map/pallas_call | solution.py:228
  63.2 10.0 %collective-permute-done.7.refs_0_ = bf16[256,2048]{1,0:T(8,128)(2,1)S(1)} collective-permute-done((bf16[256,2048]{1,0:T(8,128)(2,1)S(1)}, bf16[256,2048]{1,0:T(8,128)(2,1)S(1)}, u32[]{:S(2)}, u32[]{:S(2)}) %collective-permute-start.7) | collective-permute-done | bytes 1048608 | tf_op jit(solution)/shard_map/ppermute | solution.py:751
  73.2 5.8 %shard_map.83 = (bf16[256,2048]{1,0:T(8,128)(2,1)S(1)}, bf16[256,2048]{1,0:T(8,128)(2,1)S(1)}) custom-call(f32[256,2048]{1,0:T(8,128)S(1)} %get-tuple-element.69.key_part, f32[256,2048]{1,0:T(8,128)S(1)} %get-tuple-element.70.value_part, bf16[256,2048]{1,0:T(8,128)(2,1)S(1)} %collective-permute-done.7.refs_0_, ...), custom_call_target="tpu_custom_call" | custom-call | flops 4294967296 | bytes 1048576 | tf_op jit(solution)/shard_map/pallas_call | solution.py:228
  79.0 0.0 collective-permute-done.1.refs_2_
  79.0 0.0 collective-permute-done.refs_0_
  79.0 0.0 collective-permute-done.2.refs_5_
  79.0 0.0 collective-permute-done.3.refs_6_
  79.0 6.8 %shard_map.84.refs_7_ = f32[16,16,128]{2,1,0:T(8,128)S(1)} custom-call(s32[2,2]{1,0:T(2,128)S(1)} %collective-permute-done.refs_0_, s32[2,2]{1,0:T(2,128)S(1)} %copy-done.3, s32[2,2]{1,0:T(2,128)S(1)} %collective-permute-done.1.refs_2_, bf16[256,2048]{1,0:T(8,128)(2,1)S(1)} %copy-done, bf16[256,2048]{1,0:T(8,128)(2,1)S(1)} %copy-done.1, ...), custom_call_target="tpu_custom_call" | custom-call | flops 2147483648 | bytes 8388608 | tf_op jit(solution)/shard_map/pallas_call | solution.py:424
  85.8 2.3 %shard_map.85.refs_7_ = f32[16,16,128]{2,1,0:T(8,128)S(1)} custom-call(s32[2,2]{1,0:T(2,128)S(1)} %collective-permute-done.refs_0_, s32[2,2]{1,0:T(2,128)S(1)} %copy-done.3, s32[2,2]{1,0:T(2,128)S(1)} %collective-permute-done.1.refs_2_, bf16[256,2048]{1,0:T(8,128)(2,1)S(1)} %copy-done, bf16[256,2048]{1,0:T(8,128)(2,1)S(1)} %copy-done.1, ...), custom_call_target="tpu_custom_call" | custom-call | flops 536870912 | bytes 5242880 | tf_op jit(solution)/shard_map/pallas_call | solution.py:424
  88.1 2.4 %shard_map.86 = (f32[16,16,128]{2,1,0:T(8,128)S(1)}, f32[16,8,128]{2,1,0:T(8,128)S(1)}, f32[16,8,128]{2,1,0:T(8,128)S(1)}) custom-call(s32[2,2]{1,0:T(2,128)S(1)} %collective-permute-done.refs_0_, s32[2,2]{1,0:T(2,128)S(1)} %copy-done.3, s32[2,2]{1,0:T(2,128)S(1)} %collective-permute-done.1.refs_2_, bf16[256,2048]{1,0:T(8,128)(2,1)S(1)} %copy-done, ...), custom_call_target="tpu_custom_call" | custom-call | flops 536870912 | bytes 5242880 | tf_op jit(solution)/shard_map/pallas_call | solution.py:424
  90.5 0.1 collective-permute-start.8
  90.6 0.8 collective-permute-start.9
  91.5 0.4 collective-permute-done.8.refs_8_.refs_10_
  91.9 0.0 collective-permute-done.9.refs_9_.refs_11_
  91.9 11.7 %shard_map.87 = (bf16[768,2048]{1,0:T(8,128)(2,1)S(1)}, bf16[768,2048]{1,0:T(8,128)(2,1)S(1)}, bf16[16,128,256]{2,1,0:T(8,128)(2,1)S(1)}, bf16[128,2048]{1,0:T(8,128)(2,1)S(1)}, bf16[1,2,8,256,2048]{4,3,2,1,0:T(8,128)(2,1)S(1)}) custom-call(s32[2,2]{1,0:T(2,128)S(1)} %collective-permute-done.refs_0_, s32[2,2]{1,0:T(2,128)S(1)} %copy-done.3, ...), custom_call_target="tpu_custom_call" | custom-call | flops 3489660928 | bytes 2097152 | tf_op jit(solution)/shard_map/pallas_call | solution.py:608
  103.5 1.8 collective-permute-start.15
  105.3 11.0 %shard_map.88 = (bf16[768,2048]{1,0:T(8,128)(2,1)S(1)}, bf16[768,2048]{1,0:T(8,128)(2,1)S(1)}, bf16[16,128,256]{2,1,0:T(8,128)(2,1)S(1)}, bf16[128,2048]{1,0:T(8,128)(2,1)S(1)}) custom-call(s32[2,2]{1,0:T(2,128)S(1)} %collective-permute-done.refs_0_, s32[2,2]{1,0:T(2,128)S(1)} %copy-done.3, ...), custom_call_target="tpu_custom_call", output_to_operand_aliasing={{0}: (11, {}), {1}: (12, {})} | custom-call | flops 3489660928 | bytes 2097152 | tf_op jit(solution)/shard_map/pallas_call | solution.py:608
  116.4 0.3 collective-permute-start.14
  116.7 14.6 %shard_map.89 = (bf16[768,2048]{1,0:T(8,128)(2,1)S(1)}, bf16[768,2048]{1,0:T(8,128)(2,1)S(1)}, f32[256,2048]{1,0:T(8,128)S(1)}, bf16[256,2048]{1,0:T(8,128)(2,1)S(1)}, f32[128,2048]{1,0:T(8,128)S(1)}) custom-call(s32[2,2]{1,0:T(2,128)S(1)} %collective-permute-done.refs_0_, s32[2,2]{1,0:T(2,128)S(1)} %copy-done.3, ...), custom_call_target="tpu_custom_call", output_to_operand_aliasing={{0}: (15, {}), {1}: (16, {})} | custom-call | flops 6979321856 | bytes 4194304 | tf_op jit(solution)/shard_map/pallas_call | solution.py:608
  131.2 14.7 %shard_map.90 = (bf16[768,2048]{1,0:T(8,128)(2,1)S(1)}, bf16[768,2048]{1,0:T(8,128)(2,1)S(1)}, f32[256,2048]{1,0:T(8,128)S(1)}, bf16[256,2048]{1,0:T(8,128)(2,1)S(1)}, f32[128,2048]{1,0:T(8,128)S(1)}) custom-call(s32[2,2]{1,0:T(2,128)S(1)} %collective-permute-done.refs_0_, s32[2,2]{1,0:T(2,128)S(1)} %copy-done.3, ...), custom_call_target="tpu_custom_call", output_to_operand_aliasing={{0}: (15, {}), {1}: (16, {})} | custom-call | flops 6979321856 | bytes 4194304 | tf_op jit(solution)/shard_map/pallas_call | solution.py:608
  146.0 6.3 %collective-permute-start.10 = (f32[128,2048]{1,0:T(8,128)S(1)}, f32[128,2048]{1,0:T(8,128)S(1)}, u32[]{:S(2)}, u32[]{:S(2)}) collective-permute-start(f32[128,2048]{1,0:T(8,128)S(1)} %get-tuple-element.88), channel_id=1, source_target_pairs={{0,1},{1,4},{4,5},{5,8},{8,9},{9,12},{12,13},{13,16},{16,17},{17,2... | collective-permute-start | bytes 3145736 | tf_op jit(solution)/shard_map/ppermute | solution.py:722
  152.3 1.8 collective-permute-start.12
  154.1 1.3 collective-permute-start.11
  155.3 0.0 collective-permute-done.15.refs_0_
  155.4 0.4 collective-permute-start.13
  155.7 16.3 %shard_map.92.own_ref = bf16[768,2048]{1,0:T(8,128)(2,1)S(1)} custom-call(bf16[768,2048]{1,0:T(8,128)(2,1)S(1)} %get-tuple-element.90.key_grad_ref, bf16[768,2048]{1,0:T(8,128)(2,1)S(1)} %get-tuple-element.91.value_grad_ref, bf16[4096,2048]{1,0:T(8,128)(2,1)} %key_ref.3, bf16[4096,2048]{1,0:T(8,128)(2,1)} %value_ref.3), custom_call_target="tpu_custom_call" | custom-call | flops 12884901888 | bytes 16777216 | tf_op jit(solution)/shard_map/pallas_call | solution.py:641
  172.0 0.9 shard_map.93.refs_1_
  172.9 0.0 collective-permute-done.14.refs_0_
  172.9 0.9 shard_map.94.refs_1_
  173.8 26.2 %collective-permute-done.13.refs_0_ = bf16[256,2048]{1,0:T(8,128)(2,1)S(1)} collective-permute-done((bf16[256,2048]{1,0:T(8,128)(2,1)S(1)}, bf16[256,2048]{1,0:T(8,128)(2,1)S(1)}, u32[]{:S(2)}, u32[]{:S(2)}) %collective-permute-start.13) | collective-permute-done | bytes 1048608 | tf_op jit(solution)/shard_map/ppermute | solution.py:797
  200.0 1.1 shard_map.95.refs_1_
  201.0 0.0 collective-permute-done.12.refs_0_
  201.1 1.1 shard_map.96
  202.1 0.0 collective-permute-done.10.below_ref
  202.1 0.0 collective-permute-done.11.above_ref
  202.1 1.4 shard_map.91
Async XLA Ops:
  0.6 8.5 %copy-start.2 = (bf16[768,2048]{1,0:T(8,128)(2,1)S(1)}, bf16[768,2048]{1,0:T(8,128)(2,1)}, u32[]{:S(2)}) copy-start(bf16[768,2048]{1,0:T(8,128)(2,1)} %states_ref.5) | copy-start | bytes 9437188
  0.6 8.5 %copy-start.1 = (bf16[256,2048]{1,0:T(8,128)(2,1)S(1)}, bf16[256,2048]{1,0:T(8,128)(2,1)}, u32[]{:S(2)}) copy-start(bf16[256,2048]{1,0:T(8,128)(2,1)} %refs_4_.13) | copy-start | bytes 3145732
  0.7 8.5 %copy-start = (bf16[256,2048]{1,0:T(8,128)(2,1)S(1)}, bf16[256,2048]{1,0:T(8,128)(2,1)}, u32[]{:S(2)}) copy-start(bf16[256,2048]{1,0:T(8,128)(2,1)} %refs_3_.13) | copy-start | bytes 3145732
  2.1 27.0 %collective-permute-start.4 = (bf16[256,2048]{1,0:T(8,128)(2,1)S(1)}, bf16[256,2048]{1,0:T(8,128)(2,1)S(1)}, u32[]{:S(2)}, u32[]{:S(2)}) collective-permute-start(bf16[256,2048]{1,0:T(8,128)(2,1)S(1)} %shard_map.78), channel_id=1, source_target_pairs={{0,2},{2,0},{1,3},{3,1},{4,6},{6,4},{5,7},{7,5},{8,10},{10,8},{9,1... | collective-permute-start | bytes 3145736 | tf_op jit(solution)/shard_map/ppermute | solution.py:751
  6.6 49.9 %collective-permute-start.5 = (bf16[128,2048]{1,0:T(8,128)(2,1)S(1)}, bf16[128,2048]{1,0:T(8,128)(2,1)S(1)}, u32[]{:S(2)}, u32[]{:S(2)}) collective-permute-start(bf16[128,2048]{1,0:T(8,128)(2,1)S(1)} %get-tuple-element.60), channel_id=1, source_target_pairs={{0,2},{2,0},{1,3},{3,1},{4,6},{6,4},{5,7},{7,5},{8,10},{10,8},{9,1... | collective-permute-start | bytes 1572872 | tf_op jit(solution)/shard_map/ppermute | solution.py:751
  7.1 44.5 %collective-permute-start.6 = (bf16[128,2048]{1,0:T(8,128)(2,1)S(1)}, bf16[128,2048]{1,0:T(8,128)(2,1)S(1)}, u32[]{:S(2)}, u32[]{:S(2)}) collective-permute-start(bf16[128,2048]{1,0:T(8,128)(2,1)S(1)} %get-tuple-element.66), channel_id=1, source_target_pairs={{0,2},{2,0},{1,3},{3,1},{4,6},{6,4},{5,7},{7,5},{8,10},{10,8},{9,1... | collective-permute-start | bytes 1572872 | tf_op jit(solution)/shard_map/ppermute | solution.py:751
  8.7 64.5 %collective-permute-start.7 = (bf16[256,2048]{1,0:T(8,128)(2,1)S(1)}, bf16[256,2048]{1,0:T(8,128)(2,1)S(1)}, u32[]{:S(2)}, u32[]{:S(2)}) collective-permute-start(bf16[256,2048]{1,0:T(8,128)(2,1)S(1)} %get-tuple-element.71), channel_id=1, source_target_pairs={{0,2},{2,0},{1,3},{3,1},{4,6},{6,4},{5,7},{7,5},{8,10},{10,8},{9,1... | collective-permute-start | bytes 3145736 | tf_op jit(solution)/shard_map/ppermute | solution.py:751
  25.2 53.8 %collective-permute-start.2 = (bf16[128,4096]{1,0:T(8,128)(2,1)S(1)}, bf16[128,4096]{1,0:T(8,128)(2,1)S(1)}, u32[]{:S(2)}, u32[]{:S(2)}) collective-permute-start(bf16[128,4096]{1,0:T(8,128)(2,1)S(1)} %get-tuple-element.52), channel_id=1, source_target_pairs={{0,1},{1,4},{4,5},{5,8},{8,9},{9,12},{12,13},{13,16},{16,17},{17,2... | collective-permute-start | bytes 3145736 | tf_op jit(solution)/shard_map/ppermute | solution.py:722
  29.1 49.9 %collective-permute-start.3 = (bf16[128,4096]{1,0:T(8,128)(2,1)S(1)}, bf16[128,4096]{1,0:T(8,128)(2,1)S(1)}, u32[]{:S(2)}, u32[]{:S(2)}) collective-permute-start(bf16[128,4096]{1,0:T(8,128)(2,1)S(1)} %get-tuple-element.53), channel_id=1, source_target_pairs={{1,0},{4,1},{5,4},{8,5},{9,8},{12,9},{13,12},{16,13},{17,16},{20,1... | collective-permute-start | bytes 3145736 | tf_op jit(solution)/shard_map/ppermute | solution.py:722
  30.4 21.2 %copy-start.3 = (s32[2,2]{1,0:T(2,128)S(1)}, s32[2,2]{1,0:T(2,128)}, u32[]{:S(2)}) copy-start(s32[2,2]{1,0:T(2,128)} %refs_1_.15) | copy-start | bytes 52
  51.6 27.4 %collective-permute-start.1 = (s32[2,2]{1,0:T(2,128)S(1)}, s32[2,2]{1,0:T(2,128)S(1)}, u32[]{:S(2)}, u32[]{:S(2)}) collective-permute-start(s32[2,2]{1,0:T(2,128)S(1)} %copy-done.3), channel_id=1, source_target_pairs={{1,0},{4,1},{5,4},{8,5},{9,8},{12,9},{13,12},{16,13},{17,16},{20,1... | collective-permute-start | bytes 56 | tf_op jit(solution)/shard_map/ppermute | solution.py:722
  56.5 22.5 %collective-permute-start = (s32[2,2]{1,0:T(2,128)S(1)}, s32[2,2]{1,0:T(2,128)S(1)}, u32[]{:S(2)}, u32[]{:S(2)}) collective-permute-start(s32[2,2]{1,0:T(2,128)S(1)} %copy-done.3), channel_id=1, source_target_pairs={{0,1},{1,4},{4,5},{5,8},{8,9},{9,12},{12,13},{13,16},{16,17},{17,2... | collective-permute-start | bytes 56 | tf_op jit(solution)/shard_map/ppermute | solution.py:722
  90.5 1.3 collective-permute-start.8
  90.6 1.2 collective-permute-start.9
  103.5 51.8 %collective-permute-start.15 = (bf16[128,2048]{1,0:T(8,128)(2,1)S(1)}, bf16[128,2048]{1,0:T(8,128)(2,1)S(1)}, u32[]{:S(2)}, u32[]{:S(2)}) collective-permute-start(bf16[128,2048]{1,0:T(8,128)(2,1)S(1)} %get-tuple-element.95), channel_id=1, source_target_pairs={{0,2},{2,0},{1,3},{3,1},{4,6},{6,4},{5,7},{7,5},{8,10},{10,8},{9,1... | collective-permute-start | bytes 1572872 | tf_op jit(solution)/shard_map/ppermute | solution.py:797
  116.4 56.5 %collective-permute-start.14 = (bf16[128,2048]{1,0:T(8,128)(2,1)S(1)}, bf16[128,2048]{1,0:T(8,128)(2,1)S(1)}, u32[]{:S(2)}, u32[]{:S(2)}) collective-permute-start(bf16[128,2048]{1,0:T(8,128)(2,1)S(1)} %get-tuple-element.94), channel_id=1, source_target_pairs={{0,2},{2,0},{1,3},{3,1},{4,6},{6,4},{5,7},{7,5},{8,10},{10,8},{9,1... | collective-permute-start | bytes 1572872 | tf_op jit(solution)/shard_map/ppermute | solution.py:797
  146.0 56.2 %collective-permute-start.10 = (f32[128,2048]{1,0:T(8,128)S(1)}, f32[128,2048]{1,0:T(8,128)S(1)}, u32[]{:S(2)}, u32[]{:S(2)}) collective-permute-start(f32[128,2048]{1,0:T(8,128)S(1)} %get-tuple-element.88), channel_id=1, source_target_pairs={{0,1},{1,4},{4,5},{5,8},{8,9},{9,12},{12,13},{13,16},{16,17},{17,2... | collective-permute-start | bytes 3145736 | tf_op jit(solution)/shard_map/ppermute | solution.py:722
  152.3 48.8 %collective-permute-start.12 = (bf16[256,2048]{1,0:T(8,128)(2,1)S(1)}, bf16[256,2048]{1,0:T(8,128)(2,1)S(1)}, u32[]{:S(2)}, u32[]{:S(2)}) collective-permute-start(bf16[256,2048]{1,0:T(8,128)(2,1)S(1)} %get-tuple-element.92), channel_id=1, source_target_pairs={{0,2},{2,0},{1,3},{3,1},{4,6},{6,4},{5,7},{7,5},{8,10},{10,8},{9,1... | collective-permute-start | bytes 3145736 | tf_op jit(solution)/shard_map/ppermute | solution.py:797
  154.1 48.1 %collective-permute-start.11 = (f32[128,2048]{1,0:T(8,128)S(1)}, f32[128,2048]{1,0:T(8,128)S(1)}, u32[]{:S(2)}, u32[]{:S(2)}) collective-permute-start(f32[128,2048]{1,0:T(8,128)S(1)} %get-tuple-element.89), channel_id=1, source_target_pairs={{1,0},{4,1},{5,4},{8,5},{9,8},{12,9},{13,12},{16,13},{17,16},{20,1... | collective-permute-start | bytes 3145736 | tf_op jit(solution)/shard_map/ppermute | solution.py:722
  155.4 44.6 %collective-permute-start.13 = (bf16[256,2048]{1,0:T(8,128)(2,1)S(1)}, bf16[256,2048]{1,0:T(8,128)(2,1)S(1)}, u32[]{:S(2)}, u32[]{:S(2)}) collective-permute-start(bf16[256,2048]{1,0:T(8,128)(2,1)S(1)} %get-tuple-element.93), channel_id=1, source_target_pairs={{0,2},{2,0},{1,3},{3,1},{4,6},{6,4},{5,7},{7,5},{8,10},{10,8},{9,1... | collective-permute-start | bytes 3145736 | tf_op jit(solution)/shard_map/ppermute | solution.py:797
where the time goes:
time: 204 us
  Pallas kernels  124 us (61%)
  waiting for transfers between devices  52.8 us (26%)
  starting transfers between devices  25.2 us (12%)
    pallas_call x4, Pallas kernels, gradients(): call(body, [SCALARS] * 3 + [HERE] * (len(shared) + 5) + ([ANYWHERE] * 2 i...  51.9 us
    ppermute x4, waiting for transfers between devices, on_device(): arrived.append([lax.ppermute(rows, 'tensor', turn) for turn in turns])  26.2 us
    ppermute x4, waiting for transfers between devices, on_device(): lax.ppermute(term, 'tensor', turn)  26.2 us
    pallas_call x4, Pallas kernels, project_rest(): call(body, [HERE] * (2 + count) + ([ANYWHERE] * 2 if loads else [HERE]),...  20.5 us
    pallas_call x1, Pallas kernels, own_terms(): call(body, [HERE] * 2 + [ANYWHERE] * 2, HERE, jax.ShapeDtypeStruct((rows,...  16.3 us
    pallas_call x1, Pallas kernels, project_own(): call(body, [HERE] * 3 + [ANYWHERE] * 2, [HERE] * (len(shapes) + 2), shape...  16.1 us
    ppermute x6, starting transfers between devices, shifted(): lax.ppermute(value, ROWS, [(source, source + steps) for source in range(f...  14.5 us
    pallas_call x3, Pallas kernels, row_stats(): call(body, [SCALARS] * 3 + [HERE] * len(shared) + [HERE] * (len(flat) + l...  11.5 us
  transfers between devices with their start and end apart: 16, of which 5 were waited for; matrix products, arithmetic and copies ran while one was open for 0% of the time, Pallas kernels for 48%

commit v1 on v0

--- a/solution.py
+++ b/solution.py
@@ -191,15 +191,17 @@
     return [(out[2 * i], out[2 * i + 1]) for i in range(count)], out[-2], out[-1]
 
 
-def project_rest(partial, arrived, key_weight, value_weight, held, group):
+def project_rest(partial, arrived, key_weight, value_weight, held, group, base=0, height=None, into=None):
     rows, columns = partial[0].shape
+    height = height or rows
+    earlier = [] if into is None else list(into)
     depth = arrived[0].shape[1]
     count = len(arrived)
     weights = Weights(key_weight, True, group)
     loads = held is None
 
     def body(key_part, value_part, *refs):
-        pieces, refs = refs[:count], refs[count:]
+        pieces, refs = refs[:count], refs[count + len(earlier) :]
         if loads:
             both, outs, (buffer, sems) = refs[:2], refs[2:4], refs[4:]
             owners = sources(group)[1:]
@@ -217,23 +219,24 @@
                     total = total + jnp.dot(
                         pieces[at][...], buffer[at, which, j], preferred_element_type=F32
                     )
-                outs[which][:, here] = total.astype(BF16)
+                outs[which][base : base + rows, here] = total.astype(BF16)
             return carry
 
         lax.fori_loop(0, weights.steps, step, 0)
 
-    shapes = [jax.ShapeDtypeStruct((rows, columns), BF16)] * 2
+    shapes = [jax.ShapeDtypeStruct((height, columns), BF16)] * 2
     if loads:
         shapes.append(jax.ShapeDtypeStruct(weights.buffer_shape(count), BF16))
     out = call(
         body,
-        [HERE] * (2 + count) + ([ANYWHERE] * 2 if loads else [HERE]),
+        [HERE] * (2 + count + len(earlier)) + ([ANYWHERE] * 2 if loads else [HERE]),
         [HERE] * len(shapes),
         shapes,
         [weights.semaphores(count)] if loads else [],
         4 * rows * depth * columns * count,
         4 * depth * columns * count if loads else 2 * rows * columns,
-    )(*partial, *arrived, *((key_weight, value_weight) if loads else (held,)))
+        {2 + count + i: i for i in range(len(earlier))},
+    )(*partial, *arrived, *earlier, *((key_weight, value_weight) if loads else (held,)))
     return (out[0], out[1]), (out[2] if loads else held)
 
 
@@ -246,8 +249,9 @@
 
 
 class Tiles:
-    def __init__(self, tokens, first, last, halo):
+    def __init__(self, tokens, first, last, halo, origin=None):
         self.first, self.last, self.tokens = first, last, tokens
+        self.origin = first if origin is None else origin
         low, high = (-1, tokens + 1) if halo else (0, tokens)
         touched = [
             t for t in range(low, high) if any(reaches(t, f) for f in range(first, last))
@@ -310,7 +314,7 @@
 def head_tiles(tiles, tokens, key_ref, value_ref, head):
     lanes = lanes_at(head, DH)
     for group, first, last in tiles.groups:
-        rows = slice((first - tiles.first) * BLOCK, (last - tiles.first) * BLOCK)
+        rows = slice((first - tiles.origin) * BLOCK, (last - tiles.origin) * BLOCK)
         keys, values = key_ref[rows, lanes], value_ref[rows, lanes]
         query_rows = tokens.rows(group, head, False)
         grad_rows = tokens.rows(group, head, True)
@@ -332,12 +336,15 @@
     return top, total, weighted
 
 
-def tile_stats(bands, tiles_list, tokens, kv_refs, head, rate):
+def tile_stats(bands, tiles_list, tokens, kv_refs, head, rate, kept):
     found = {}
     for tiles, (key_ref, value_ref) in zip(tiles_list, kv_refs):
         for group, first, last, _, _, _, scores, slopes in head_tiles(
             tiles, tokens, key_ref, value_ref, head
         ):
+            if kept:
+                kept[0][head] = scores
+                kept[1][head] = slopes
             for position, t in enumerate(group):
                 for f in range(first, last):
                     allowed = bands.allowed(t, f)
@@ -372,7 +379,7 @@
 
 
 def row_stats(
-    band, tiles_list, kvs, queries, grads, below, above, earlier, last, rate
+    band, tiles_list, kvs, queries, grads, below, above, earlier, last, keep, rate
 ):
     own_count = queries.shape[0] // BLOCK
     columns = queries.shape[1]
@@ -391,12 +398,13 @@
         kv_refs = [refs[2 * i : 2 * i + 2] for i in range(count)]
         rest = refs[2 * count :]
         out_ref = rest[len(extra)]
+        kept = rest[-2:] if keep else ()
         even = lax.rem(lax.axis_index(ROWS), 2) == 0
 
         def step(pair, carry):
             for k in range(per):
                 head = pair * per + k
-                stats = tile_stats(bands, tiles_list, tokens, kv_refs, head, rate)
+                stats = tile_stats(bands, tiles_list, tokens, kv_refs, head, rate, kept)
                 results = []
                 for t in range(-1, own_count + 1):
                     mine = [stats[t]] if t in stats else []
@@ -409,7 +417,7 @@
                 )
                 if last:
                     lower, upper = results[:6], results[-6:]
-                    for ref, flag in zip(rest[len(extra) + 1 :], (even, jnp.logical_not(even))):
+                    for ref, flag in zip(rest[len(extra) + 1 : len(extra) + 3], (even, jnp.logical_not(even))):
                         picked = [jnp.where(flag, u, d) for u, d in zip(upper, lower)]
                         ref[head] = jnp.concatenate(picked + blank * 2, axis=0)
             return carry
@@ -421,6 +429,9 @@
     shapes = [jax.ShapeDtypeStruct((heads, depth, BLOCK), F32)]
     if last:
         shapes += [jax.ShapeDtypeStruct((heads, 8, BLOCK), F32)] * 2
+    if keep:
+        ((group, first, end),) = tiles_list[0].groups
+        shapes += [jax.ShapeDtypeStruct((heads, (end - first) * BLOCK, len(group) * BLOCK), F32)] * 2
     return call(
         body,
         [SCALARS] * 3
@@ -455,6 +466,7 @@
     value_weight,
     held,
     deferred,
+    kept,
     totals,
     rate,
     scale,
@@ -474,6 +486,7 @@
     sources_in = [key_weight, value_weight] if loads else [held]
     defer = not halo_touched
     extra = [] if defer else list(deferred)
+    known = [array for _, *arrays in kept for array in arrays]
     earlier = [] if totals is None else list(totals)
     base = tiles.first * BLOCK
     ahead = min(4, weights.steps)
@@ -484,7 +497,8 @@
         refs = refs[len(shared) :]
         key_ref, value_ref, stat_ref, even_ref, odd_ref = refs[:5]
         both, refs = refs[5 : 5 + len(sources_in)], refs[5 + len(sources_in) :]
-        extra_refs, refs = refs[: len(extra)], refs[len(extra) + len(earlier) :]
+        extra_refs, refs = refs[: len(extra)], refs[len(extra) :]
+        known_refs, refs = refs[: len(known)], refs[len(known) + len(earlier) :]
         if loads:
             buffer, sems, refs = refs[-2], refs[-1], refs[:-2]
             owners = targets(group)[1:]
@@ -520,9 +534,18 @@
                 )
                 for t in range(own_count):
                     query_sum[t] = query_part[t * BLOCK : (t + 1) * BLOCK]
-            for group_tokens, first, last, keys, query_rows, grad_rows, scores, slopes in head_tiles(
-                tiles, tokens, key_ref, value_ref, head
-            ):
+            for group_tokens, first, last in tiles.groups:
+                cut = slice((first - tiles.origin) * BLOCK, (last - tiles.origin) * BLOCK)
+                query_rows = tokens.rows(group_tokens, head, False)
+                grad_rows = tokens.rows(group_tokens, head, True)
+                if known:
+                    scores = [known_refs[2 * i][head] for i in range(len(kept))]
+                    slopes = [known_refs[2 * i + 1][head] for i in range(len(kept))]
+                    scores, slopes = jnp.concatenate(scores), jnp.concatenate(slopes)
+                else:
+                    keys, values = key_ref[cut, lanes], value_ref[cut, lanes]
+                    scores = lax.dot_general(keys, query_rows, NT, preferred_element_type=F32)
+                    slopes = lax.dot_general(values, grad_rows, NT, preferred_element_type=F32)
                 low, slope_low = [], []
                 for f in range(first, last):
                     low_row, slope_row = [], []
@@ -559,7 +582,8 @@
                 value_out[cut, lanes] = value_sum[at].astype(BF16)
             if not defer:
                 for t in range(own_count):
-                    own_out[t * BLOCK : (t + 1) * BLOCK, lanes] = query_sum[t]
+                    part = query_sum[t] if t in query_sum else jnp.zeros((BLOCK, DH), F32)
+                    own_out[t * BLOCK : (t + 1) * BLOCK, lanes] = part
                 for out_ref, t in zip(halo_outs, halo_touched):
                     out_ref[:, lanes] = query_sum[t]
 
@@ -610,14 +634,17 @@
         [SCALARS] * 3
         + [HERE] * (len(shared) + 5)
         + ([ANYWHERE] * 2 if loads else [HERE])
-        + [HERE] * (len(extra) + len(earlier)),
+        + [HERE] * (len(extra) + len(known) + len(earlier)),
         [HERE] * len(shapes),
         shapes,
         [weights.semaphores(group - 1)] if loads else [],
         20 * frames * 2 * BLOCK * columns + 4 * frames * columns * features * (group - 1),
         8 * frames * columns,
-        {8 + len(shared) + len(sources_in) + len(extra) + i: i for i in range(len(earlier))},
-    )(*band, *shared, *kv, stats, *swaps, *sources_in, *extra, *earlier)
+        {
+            8 + len(shared) + len(sources_in) + len(extra) + len(known) + i: i
+            for i in range(len(earlier))
+        },
+    )(*band, *shared, *kv, stats, *swaps, *sources_in, *extra, *known, *earlier)
     halo = dict(zip(halo_touched, out[2 + group :]))
     return out[:2], out[2], out[3 : 2 + group], halo, out[-1] if loads else held
 
@@ -758,52 +785,61 @@
     above = shifted(edge_down, -1)
     band = (shifted(band_sent, 1), band_blocks, shifted(band_sent, -1))
 
-    kvs, held = [], None
-    for part, pieces in zip(partial, arrived):
-        kv, held = project_rest(part, pieces, key_weight, value_weight, held, group)
-        kvs.append(kv)
-
-    tiles = [Tiles(own_count, first, last, i < 2) for i, (first, last) in enumerate(cuts)]
-    shared = (queries, out_grad, below, above)
-    (stats,) = row_stats(band, tiles[:2], kvs[:2], *shared, None, False, rate)
-    (stats,) = row_stats(band, tiles[2:3], kvs[2:3], *shared, stats, False, rate)
-    stats, first_swap, second_swap = row_stats(
-        band, tiles[3:], kvs[3:], *shared, stats, True, rate
+    def rest(i, held, **place):
+        return project_rest(partial[i], arrived[i], key_weight, value_weight, held, group, **place)
+
+    def statistics(*where, **what):
+        return row_stats(band, *where, queries, out_grad, below, above, *what.values(), rate)
+
+    low_kv, held = rest(0, None)
+    high_kv, held = rest(1, held)
+    low_tiles, high_tiles = [Tiles(own_count, first, last, True) for first, last in cuts[:2]]
+    inner = [Tiles(own_count, first, last, False, edge) for first, last in cuts[2:]]
+    inner_tiles = Tiles(own_count, edge, frame_blocks - edge, False)
+    (stats,) = statistics([low_tiles, high_tiles], [low_kv, high_kv], earlier=None, last=False, keep=False)
+    height = (frame_blocks - 2 * edge) * BLOCK
+    kv, held = rest(2, held, height=height)
+    stats, *first_kept = statistics(inner[:1], [kv], earlier=stats, last=False, keep=True)
+    kv, stats = lax.optimization_barrier((kv, stats))
+    inner_kv, held = rest(3, held, base=(middle - edge) * BLOCK, height=height, into=kv)
+    stats, first_swap, second_swap, *second_kept = statistics(
+        inner[1:], [inner_kv], earlier=stats, last=True, keep=True
     )
+    kept = [(edge, *first_kept), (middle, *second_kept)]
     swaps = (swapped(first_swap, 0), swapped(second_swap, 1))
 
-    out = [None] * 4
-    sent = [None] * 4
-    totals = away = None
-    for i in (2, 3, 0, 1):
-        deferred = (kvs[2 + i][0], out[2 + i][1]) if i < 2 else None
-        out[i] = gradients(
-            band,
-            tiles[i],
-            kvs[i],
-            *shared,
-            stats,
-            swaps,
-            key_weight,
-            value_weight,
-            away,
-            deferred,
-            totals,
-            rate,
-            scale,
-            group,
+    chunks = [(inner_tiles, inner_kv), (low_tiles, low_kv), (high_tiles, high_kv)]
+    shared = (queries, out_grad, below, above, stats, swaps, key_weight, value_weight)
+    out, sent = [], []
+    totals = away = deferred = None
+    for i, (tiles, kv) in enumerate(chunks):
+        out.append(
+            gradients(
+                band,
+                tiles,
+                kv,
+                *shared,
+                away,
+                deferred,
+                () if i else kept,
+                totals,
+                rate,
+                scale,
+                group,
+            )
         )
         totals, away = out[i][0], out[i][4]
-        sent[i] = [lax.ppermute(term, "tensor", turn) for term, turn in zip(out[i][2], turns)]
-
-    from_below = shifted(out[1][3][own_count], 1)
-    from_above = shifted(out[0][3][-1], -1)
+        deferred = () if i else (inner_kv[0], out[0][1])
+        sent.append([lax.ppermute(term, "tensor", turn) for term, turn in zip(out[i][2], turns)])
+
+    from_below = shifted(out[2][3][own_count], 1)
+    from_above = shifted(out[1][3][-1], -1)
     own = own_terms(totals, key_weight, value_weight, group)
-    query_grad = finish_queries(out[0][1], out[1][1], from_below, from_above)
+    query_grad = finish_queries(out[1][1], out[2][1], from_below, from_above)
 
     encoder_grad = None
-    for i in (2, 3, 0, 1):
-        encoder_grad = add_rows(encoder_grad, own, sent[i], row_cuts[i][0])
+    for i, (tiles, _) in enumerate(chunks):
+        encoder_grad = add_rows(encoder_grad, own, sent[i], tiles.first * BLOCK)
     return (query_grad, encoder_grad)
 
 

time: 204 us -> 219 us (1.074)
  waiting for transfers between devices: 52.8 us -> 78.4 us
  Pallas kernels: 124 us -> 112 us
  starting transfers between devices: 25.2 us -> 27.4 us
    ppermute x4 -> x3, waiting for transfers between devices: 26.2 us -> 49.2 us  [on_device(): lax.ppermute(term, 'tensor', turn)]
    pallas_call x4 -> x3, Pallas kernels: 51.9 us -> 40.4 us  [gradients(): call(body, [SCALARS] * 3 + [HERE] * (len(shared) + 5) + ([ANYWHERE] * 2 i...]
    ppermute x4, waiting for transfers between devices: 26.2 us -> 29.1 us  [on_device(): arrived.append([lax.ppermute(rows, 'tensor', turn) for turn in turns])]
    ppermute x2, starting transfers between devices: 0.92 us -> 3.4 us  [swapped(): return lax.ppermute(value, ROWS, pairs)]
  transfers between devices with their start and end apart: 16 -> 15, of which waited for: 5 -> 5; matrix products, arithmetic and copies ran while one was open for 0% -> 0% of each run, Pallas kernels for 48% -> 29%
where the time goes in v1:
time: 219 us
  Pallas kernels  112 us (51%)
  waiting for transfers between devices  78.4 us (36%)
  starting transfers between devices  27.4 us (13%)
    ppermute x3, waiting for transfers between devices, on_device(): lax.ppermute(term, 'tensor', turn)  49.2 us
    pallas_call x3, Pallas kernels, gradients(): call(body, [SCALARS] * 3 + [HERE] * (len(shared) + 5) + ([ANYWHERE] * 2 i...  40.4 us
    ppermute x4, waiting for transfers between devices, on_device(): arrived.append([lax.ppermute(rows, 'tensor', turn) for turn in turns])  29.1 us
    pallas_call x4, Pallas kernels, project_rest(): call(body, [HERE] * (2 + count + len(earlier)) + ([ANYWHERE] * 2 if loads...  20.5 us
    pallas_call x1, Pallas kernels, own_terms(): call(body, [HERE] * 2 + [ANYWHERE] * 2, HERE, jax.ShapeDtypeStruct((rows,...  16.3 us
    pallas_call x1, Pallas kernels, project_own(): call(body, [HERE] * 3 + [ANYWHERE] * 2, [HERE] * (len(shapes) + 2), shape...  16.1 us
    ppermute x6, starting transfers between devices, shifted(): lax.ppermute(value, ROWS, [(source, source + steps) for source in range(f...  13.3 us
    pallas_call x3, Pallas kernels, row_stats(): call(body, [SCALARS] * 3 + [HERE] * len(shared) + [HERE] * (len(flat) + l...  11.5 us
  transfers between devices with their start and end apart: 15, of which 5 were waited for; matrix products, arithmetic and copies ran while one was open for 0% of the time, Pallas kernels for 29%

profile of v1, /device:TPU:0, one launch (start us, length us, event | category | flops | bytes accessed | tf_op | source)
XLA Modules:
  0.0 219.1 jit_solution(4085827784271647801)
XLA Ops:
  0.6 0.0 copy-start.2
  0.6 0.0 copy-start.1
  0.7 0.0 copy-start
  0.7 1.4 shard_map.78
  2.1 3.0 %collective-permute-start.4 = (bf16[256,2048]{1,0:T(8,128)(2,1)S(1)}, bf16[256,2048]{1,0:T(8,128)(2,1)S(1)}, u32[]{:S(2)}, u32[]{:S(2)}) collective-permute-start(bf16[256,2048]{1,0:T(8,128)(2,1)S(1)} %shard_map.78), channel_id=1, source_target_pairs={{0,2},{2,0},{1,3},{3,1},{4,6},{6,4},{5,7},{7,5},{8,10},{10,8},{9,1... | collective-permute-start | bytes 3145736 | tf_op jit(solution)/shard_map/ppermute | solution.py:778
  5.1 1.5 shard_map.80
  6.6 0.5 collective-permute-start.7
  7.1 0.0 copy-done.2
  7.1 0.0 copy-done.1
  7.1 0.0 copy-done
  7.1 16.1 %shard_map.77 = (f32[256,2048]{1,0:T(8,128)S(1)}, f32[256,2048]{1,0:T(8,128)S(1)}, f32[256,2048]{1,0:T(8,128)S(1)}, f32[256,2048]{1,0:T(8,128)S(1)}, f32[128,204...) custom-call(bf16[768,2048]{1,0:T(8,128)(2,1)S(1)} %copy-done.2, ...), custom_call_target="tpu_custom_call" | custom-call | flops 12884901888 | bytes 19922944 | tf_op jit(solution)/shard_map/pallas_call | solution.py:182
  23.2 1.5 collective-permute-start.2
  24.7 1.3 collective-permute-start.3
  26.0 1.5 collective-permute-start.5
  27.5 1.6 collective-permute-done.4.refs_0_
  29.1 2.0 collective-permute-start.6
  31.1 0.0 copy-start.3
  31.1 7.6 %shard_map.79 = (bf16[256,2048]{1,0:T(8,128)(2,1)S(1)}, bf16[256,2048]{1,0:T(8,128)(2,1)S(1)}, bf16[1,2,8,2048,256]{4,3,2,1,0:T(8,128)(2,1)S(1)}) custom-call(f32[256,2048]{1,0:T(8,128)S(1)} %get-tuple-element.58.key_part, f32[256,2048]{1,0:T(8,128)S(1)} %get-tuple-element.59.value_part, bf16[256,2048]{1,0:T(8,128)(2,1)S(1)} %collective-permute-done.4.refs_0_, ...), custom_call_target="tpu_custom_call" | custom-call | flops 4294967296 | bytes 16777216 | tf_op jit(solution)/shard_map/pallas_call | solution.py:230
  38.7 12.9 %collective-permute-done.7.refs_0_ = bf16[256,2048]{1,0:T(8,128)(2,1)S(1)} collective-permute-done((bf16[256,2048]{1,0:T(8,128)(2,1)S(1)}, bf16[256,2048]{1,0:T(8,128)(2,1)S(1)}, u32[]{:S(2)}, u32[]{:S(2)}) %collective-permute-start.7) | collective-permute-done | bytes 1048608 | tf_op jit(solution)/shard_map/ppermute | solution.py:778
  51.6 0.0 copy-done.3
  51.6 1.3 collective-permute-start.1
  52.9 5.7 %shard_map.82 = (bf16[256,2048]{1,0:T(8,128)(2,1)S(1)}, bf16[256,2048]{1,0:T(8,128)(2,1)S(1)}) custom-call(f32[256,2048]{1,0:T(8,128)S(1)} %get-tuple-element.71.key_part, f32[256,2048]{1,0:T(8,128)S(1)} %get-tuple-element.72.value_part, bf16[256,2048]{1,0:T(8,128)(2,1)S(1)} %collective-permute-done.7.refs_0_, ...), custom_call_target="tpu_custom_call" | custom-call | flops 4294967296 | bytes 1048576 | tf_op jit(solution)/shard_map/pallas_call | solution.py:230
  58.6 14.6 %collective-permute-done.6.refs_0_ = bf16[128,2048]{1,0:T(8,128)(2,1)S(1)} collective-permute-done((bf16[128,2048]{1,0:T(8,128)(2,1)S(1)}, bf16[128,2048]{1,0:T(8,128)(2,1)S(1)}, u32[]{:S(2)}, u32[]{:S(2)}) %collective-permute-start.6) | collective-permute-done | bytes 524320 | tf_op jit(solution)/shard_map/ppermute | solution.py:778
  73.2 1.3 collective-permute-start
  74.5 3.6 %shard_map.81 = (bf16[256,2048]{1,0:T(8,128)(2,1)S(1)}, bf16[256,2048]{1,0:T(8,128)(2,1)S(1)}) custom-call(f32[128,2048]{1,0:T(8,128)S(1)} %get-tuple-element.65.key_part, f32[128,2048]{1,0:T(8,128)S(1)} %get-tuple-element.66.value_part, bf16[128,2048]{1,0:T(8,128)(2,1)S(1)} %collective-permute-done.6.refs_0_, ...), custom_call_target="tpu_custom_call" | custom-call | flops 2147483648 | bytes 524288 | tf_op jit(solution)/shard_map/pallas_call | solution.py:230
  78.1 0.0 collective-permute-done.1.refs_2_
  78.1 0.0 collective-permute-done.refs_0_
  78.1 0.0 collective-permute-done.2.refs_5_
  78.1 0.0 collective-permute-done.3.refs_6_
  78.1 6.8 %shard_map.83.refs_7_ = f32[16,16,128]{2,1,0:T(8,128)S(1)} custom-call(s32[2,2]{1,0:T(2,128)S(1)} %collective-permute-done.refs_0_, s32[2,2]{1,0:T(2,128)S(1)} %copy-done.3, s32[2,2]{1,0:T(2,128)S(1)} %collective-permute-done.1.refs_2_, bf16[256,2048]{1,0:T(8,128)(2,1)S(1)} %copy-done, bf16[256,2048]{1,0:T(8,128)(2,1)S(1)} %copy-done.1, ...), custom_call_target="tpu_custom_call" | custom-call | flops 2147483648 | bytes 8388608 | tf_op jit(solution)/shard_map/pallas_call | solution.py:435
  84.9 2.3 %shard_map.84 = (f32[16,16,128]{2,1,0:T(8,128)S(1)}, f32[16,128,256]{2,1,0:T(8,128)S(1)}, f32[16,128,256]{2,1,0:T(8,128)S(1)}) custom-call(s32[2,2]{1,0:T(2,128)S(1)} %collective-permute-done.refs_0_, s32[2,2]{1,0:T(2,128)S(1)} %copy-done.3, s32[2,2]{1,0:T(2,128)S(1)} %collective-permute-done.1.refs_2_, bf16[256,2048]{1,0:T(8,128)(2,1)S(1)} %copy-done, ...), custom_call_target="tpu_custom_call" | custom-call | flops 1073741824 | bytes 6291456 | tf_op jit(solution)/shard_map/pallas_call | solution.py:435
  87.2 0.0 collective-permute-done.5.refs_0_
  87.2 3.7 %shard_map.85 = (bf16[256,2048]{1,0:T(8,128)(2,1)S(1)}, bf16[256,2048]{1,0:T(8,128)(2,1)S(1)}) custom-call(f32[128,2048]{1,0:T(8,128)S(1)} %get-tuple-element.62.key_part, f32[128,2048]{1,0:T(8,128)S(1)} %get-tuple-element.63.value_part, bf16[128,2048]{1,0:T(8,128)(2,1)S(1)} %collective-permute-done.5.refs_0_, ...), custom_call_target="tpu_custom_call", output_to_operand_aliasing={{0}: (3, {}), {1}: (4, {})} | custom-call | flops 2147483648 | bytes 524288 | tf_op jit(solution)/shard_map/pallas_call | solution.py:230
  90.9 2.4 %shard_map.86 = (f32[16,16,128]{2,1,0:T(8,128)S(1)}, f32[16,8,128]{2,1,0:T(8,128)S(1)}, f32[16,8,128]{2,1,0:T(8,128)S(1)}, f32[16,128,256]{2,1,0:T(8,128)S(1)}, f32[16,128,256]{2,1,0:T(8,128)S(1)}) custom-call(s32[2,2]{1,0:T(2,128)S(1)} %collective-permute-done.refs_0_, s32[2,2]{1,0:T(2,128)S(1)} %copy-done.3, s32[2,2]{1,0:T(2,128)S(1)} %collective-permute-done.1.refs_2_, ...), custom_call_target="tpu_custom_call" | custom-call | flops 1073741824 | bytes 6291456 | tf_op jit(solution)/shard_map/pallas_call | solution.py:435
  93.3 2.6 %collective-permute-start.8 = (f32[16,8,128]{2,1,0:T(8,128)S(1)}, f32[16,8,128]{2,1,0:T(8,128)S(1)}, u32[]{:S(2)}, u32[]{:S(2)}) collective-permute-start(f32[16,8,128]{2,1,0:T(8,128)S(1)} %get-tuple-element.83), channel_id=1, source_target_pairs={{0,1},{1,0},{4,5},{5,4},{8,9},{9,8},{12,13},{13,12},{16,17},{17,16... | collective-permute-start | bytes 196616 | tf_op jit(solution)/shard_map/ppermute | solution.py:756
  95.9 0.8 collective-permute-start.9
  96.7 0.1 collective-permute-done.8.refs_8_.refs_10_
  96.8 0.0 collective-permute-done.9.refs_9_.refs_11_
  96.8 10.1 %shard_map.87 = (bf16[768,2048]{1,0:T(8,128)(2,1)S(1)}, bf16[768,2048]{1,0:T(8,128)(2,1)S(1)}, bf16[16,256,256]{2,1,0:T(8,128)(2,1)S(1)}, bf16[256,2048]{1,0:T(8,128)(2,1)S(1)}, bf16[1,2,8,256,2048]{4,3,2,1,0:T(8,128)(2,1)S(1)}) custom-call(s32[2,2]{1,0:T(2,128)S(1)} %collective-permute-done.refs_0_, s32[2,2]{1,0:T(2,128)S(1)} %copy-done.3, ...), custom_call_target="tpu_custom_call" | custom-call | flops 6979321856 | bytes 4194304 | tf_op jit(solution)/shard_map/pallas_call | solution.py:632
  106.9 16.2 %shard_map.88 = (bf16[768,2048]{1,0:T(8,128)(2,1)S(1)}, bf16[768,2048]{1,0:T(8,128)(2,1)S(1)}, f32[256,2048]{1,0:T(8,128)S(1)}, bf16[256,2048]{1,0:T(8,128)(2,1)S(1)}, f32[128,2048]{1,0:T(8,128)S(1)}) custom-call(s32[2,2]{1,0:T(2,128)S(1)} %collective-permute-done.refs_0_, s32[2,2]{1,0:T(2,128)S(1)} %copy-done.3, ...), custom_call_target="tpu_custom_call", output_to_operand_aliasing={{0}: (15, {}), {1}: (16, {})} | custom-call | flops 6979321856 | bytes 4194304 | tf_op jit(solution)/shard_map/pallas_call | solution.py:632
  123.1 14.0 %shard_map.89 = (bf16[768,2048]{1,0:T(8,128)(2,1)S(1)}, bf16[768,2048]{1,0:T(8,128)(2,1)S(1)}, f32[256,2048]{1,0:T(8,128)S(1)}, bf16[256,2048]{1,0:T(8,128)(2,1)S(1)}, f32[128,2048]{1,0:T(8,128)S(1)}) custom-call(s32[2,2]{1,0:T(2,128)S(1)} %collective-permute-done.refs_0_, s32[2,2]{1,0:T(2,128)S(1)} %copy-done.3, ...), custom_call_target="tpu_custom_call", output_to_operand_aliasing={{0}: (13, {}), {1}: (14, {})} | custom-call | flops 6979321856 | bytes 4194304 | tf_op jit(solution)/shard_map/pallas_call | solution.py:632
  137.1 6.7 %collective-permute-start.10 = (f32[128,2048]{1,0:T(8,128)S(1)}, f32[128,2048]{1,0:T(8,128)S(1)}, u32[]{:S(2)}, u32[]{:S(2)}) collective-permute-start(f32[128,2048]{1,0:T(8,128)S(1)} %get-tuple-element.97), channel_id=1, source_target_pairs={{0,1},{1,4},{4,5},{5,8},{8,9},{9,12},{12,13},{13,16},{16,17},{17,2... | collective-permute-start | bytes 3145736 | tf_op jit(solution)/shard_map/ppermute | solution.py:749
  143.8 1.6 collective-permute-start.12
  145.4 1.3 collective-permute-start.11
  146.7 0.6 collective-permute-start.13
  147.3 1.5 collective-permute-start.14
  148.8 16.3 %shard_map.91.own_ref = bf16[768,2048]{1,0:T(8,128)(2,1)S(1)} custom-call(bf16[768,2048]{1,0:T(8,128)(2,1)S(1)} %get-tuple-element.99.key_grad_ref, bf16[768,2048]{1,0:T(8,128)(2,1)S(1)} %get-tuple-element.100.value_grad_ref, bf16[4096,2048]{1,0:T(8,128)(2,1)} %key_ref.3, bf16[4096,2048]{1,0:T(8,128)(2,1)} %value_ref.3), custom_call_target="tpu_custom_call" | custom-call | flops 12884901888 | bytes 16777216 | tf_op jit(solution)/shard_map/pallas_call | solution.py:668
  165.1 49.2 %collective-permute-done.14.refs_0_ = bf16[256,2048]{1,0:T(8,128)(2,1)S(1)} collective-permute-done((bf16[256,2048]{1,0:T(8,128)(2,1)S(1)}, bf16[256,2048]{1,0:T(8,128)(2,1)S(1)}, u32[]{:S(2)}, u32[]{:S(2)}) %collective-permute-start.14) | collective-permute-done | bytes 1048608 | tf_op jit(solution)/shard_map/ppermute | solution.py:833
  214.3 1.1 shard_map.92.refs_1_
  215.4 0.0 collective-permute-done.13.refs_0_
  215.4 1.1 shard_map.93.refs_1_
  216.4 0.0 collective-permute-done.12.refs_0_
  216.4 1.1 shard_map.94
  217.5 0.0 collective-permute-done.10.below_ref
  217.5 0.0 collective-permute-done.11.above_ref
  217.5 1.4 shard_map.90
Async XLA Ops:
  0.6 6.5 %copy-start.2 = (bf16[768,2048]{1,0:T(8,128)(2,1)S(1)}, bf16[768,2048]{1,0:T(8,128)(2,1)}, u32[]{:S(2)}) copy-start(bf16[768,2048]{1,0:T(8,128)(2,1)} %states_ref.5) | copy-start | bytes 9437188
  0.6 6.5 %copy-start.1 = (bf16[256,2048]{1,0:T(8,128)(2,1)S(1)}, bf16[256,2048]{1,0:T(8,128)(2,1)}, u32[]{:S(2)}) copy-start(bf16[256,2048]{1,0:T(8,128)(2,1)} %refs_4_.11) | copy-start | bytes 3145732
  0.7 6.5 %copy-start = (bf16[256,2048]{1,0:T(8,128)(2,1)S(1)}, bf16[256,2048]{1,0:T(8,128)(2,1)}, u32[]{:S(2)}) copy-start(bf16[256,2048]{1,0:T(8,128)(2,1)} %refs_3_.11) | copy-start | bytes 3145732
  2.1 27.0 %collective-permute-start.4 = (bf16[256,2048]{1,0:T(8,128)(2,1)S(1)}, bf16[256,2048]{1,0:T(8,128)(2,1)S(1)}, u32[]{:S(2)}, u32[]{:S(2)}) collective-permute-start(bf16[256,2048]{1,0:T(8,128)(2,1)S(1)} %shard_map.78), channel_id=1, source_target_pairs={{0,2},{2,0},{1,3},{3,1},{4,6},{6,4},{5,7},{7,5},{8,10},{10,8},{9,1... | collective-permute-start | bytes 3145736 | tf_op jit(solution)/shard_map/ppermute | solution.py:778
  6.6 44.9 %collective-permute-start.7 = (bf16[256,2048]{1,0:T(8,128)(2,1)S(1)}, bf16[256,2048]{1,0:T(8,128)(2,1)S(1)}, u32[]{:S(2)}, u32[]{:S(2)}) collective-permute-start(bf16[256,2048]{1,0:T(8,128)(2,1)S(1)} %get-tuple-element.73), channel_id=1, source_target_pairs={{0,2},{2,0},{1,3},{3,1},{4,6},{6,4},{5,7},{7,5},{8,10},{10,8},{9,1... | collective-permute-start | bytes 3145736 | tf_op jit(solution)/shard_map/ppermute | solution.py:778
  23.2 54.9 %collective-permute-start.2 = (bf16[128,4096]{1,0:T(8,128)(2,1)S(1)}, bf16[128,4096]{1,0:T(8,128)(2,1)S(1)}, u32[]{:S(2)}, u32[]{:S(2)}) collective-permute-start(bf16[128,4096]{1,0:T(8,128)(2,1)S(1)} %get-tuple-element.56), channel_id=1, source_target_pairs={{0,1},{1,4},{4,5},{5,8},{8,9},{9,12},{12,13},{13,16},{16,17},{17,2... | collective-permute-start | bytes 3145736 | tf_op jit(solution)/shard_map/ppermute | solution.py:749
  24.7 53.4 %collective-permute-start.3 = (bf16[128,4096]{1,0:T(8,128)(2,1)S(1)}, bf16[128,4096]{1,0:T(8,128)(2,1)S(1)}, u32[]{:S(2)}, u32[]{:S(2)}) collective-permute-start(bf16[128,4096]{1,0:T(8,128)(2,1)S(1)} %get-tuple-element.57), channel_id=1, source_target_pairs={{1,0},{4,1},{5,4},{8,5},{9,8},{12,9},{13,12},{16,13},{17,16},{20,1... | collective-permute-start | bytes 3145736 | tf_op jit(solution)/shard_map/ppermute | solution.py:749
  26.0 61.2 %collective-permute-start.5 = (bf16[128,2048]{1,0:T(8,128)(2,1)S(1)}, bf16[128,2048]{1,0:T(8,128)(2,1)S(1)}, u32[]{:S(2)}, u32[]{:S(2)}) collective-permute-start(bf16[128,2048]{1,0:T(8,128)(2,1)S(1)} %get-tuple-element.64), channel_id=1, source_target_pairs={{0,2},{2,0},{1,3},{3,1},{4,6},{6,4},{5,7},{7,5},{8,10},{10,8},{9,1... | collective-permute-start | bytes 1572872 | tf_op jit(solution)/shard_map/ppermute | solution.py:778
  29.1 44.1 %collective-permute-start.6 = (bf16[128,2048]{1,0:T(8,128)(2,1)S(1)}, bf16[128,2048]{1,0:T(8,128)(2,1)S(1)}, u32[]{:S(2)}, u32[]{:S(2)}) collective-permute-start(bf16[128,2048]{1,0:T(8,128)(2,1)S(1)} %get-tuple-element.67), channel_id=1, source_target_pairs={{0,2},{2,0},{1,3},{3,1},{4,6},{6,4},{5,7},{7,5},{8,10},{10,8},{9,1... | collective-permute-start | bytes 1572872 | tf_op jit(solution)/shard_map/ppermute | solution.py:778
  31.1 20.5 %copy-start.3 = (s32[2,2]{1,0:T(2,128)S(1)}, s32[2,2]{1,0:T(2,128)}, u32[]{:S(2)}) copy-start(s32[2,2]{1,0:T(2,128)} %refs_1_.13) | copy-start | bytes 52
  51.6 26.5 %collective-permute-start.1 = (s32[2,2]{1,0:T(2,128)S(1)}, s32[2,2]{1,0:T(2,128)S(1)}, u32[]{:S(2)}, u32[]{:S(2)}) collective-permute-start(s32[2,2]{1,0:T(2,128)S(1)} %copy-done.3), channel_id=1, source_target_pairs={{1,0},{4,1},{5,4},{8,5},{9,8},{12,9},{13,12},{16,13},{17,16},{20,1... | collective-permute-start | bytes 56 | tf_op jit(solution)/shard_map/ppermute | solution.py:749
  73.2 4.9 %collective-permute-start = (s32[2,2]{1,0:T(2,128)S(1)}, s32[2,2]{1,0:T(2,128)S(1)}, u32[]{:S(2)}, u32[]{:S(2)}) collective-permute-start(s32[2,2]{1,0:T(2,128)S(1)} %copy-done.3), channel_id=1, source_target_pairs={{0,1},{1,4},{4,5},{5,8},{8,9},{9,12},{12,13},{13,16},{16,17},{17,2... | collective-permute-start | bytes 56 | tf_op jit(solution)/shard_map/ppermute | solution.py:749
  93.3 3.5 %collective-permute-start.8 = (f32[16,8,128]{2,1,0:T(8,128)S(1)}, f32[16,8,128]{2,1,0:T(8,128)S(1)}, u32[]{:S(2)}, u32[]{:S(2)}) collective-permute-start(f32[16,8,128]{2,1,0:T(8,128)S(1)} %get-tuple-element.83), channel_id=1, source_target_pairs={{0,1},{1,0},{4,5},{5,4},{8,9},{9,8},{12,13},{13,12},{16,17},{17,16... | collective-permute-start | bytes 196616 | tf_op jit(solution)/shard_map/ppermute | solution.py:756
  95.9 0.9 collective-permute-start.9
  137.1 80.4 %collective-permute-start.10 = (f32[128,2048]{1,0:T(8,128)S(1)}, f32[128,2048]{1,0:T(8,128)S(1)}, u32[]{:S(2)}, u32[]{:S(2)}) collective-permute-start(f32[128,2048]{1,0:T(8,128)S(1)} %get-tuple-element.97), channel_id=1, source_target_pairs={{0,1},{1,4},{4,5},{5,8},{8,9},{9,12},{12,13},{13,16},{16,17},{17,2... | collective-permute-start | bytes 3145736 | tf_op jit(solution)/shard_map/ppermute | solution.py:749
  143.8 72.6 %collective-permute-start.12 = (bf16[256,2048]{1,0:T(8,128)(2,1)S(1)}, bf16[256,2048]{1,0:T(8,128)(2,1)S(1)}, u32[]{:S(2)}, u32[]{:S(2)}) collective-permute-start(bf16[256,2048]{1,0:T(8,128)(2,1)S(1)} %get-tuple-element.101), channel_id=1, source_target_pairs={{0,2},{2,0},{1,3},{3,1},{4,6},{6,4},{5,7},{7,5},{8,10},{10,8},{9,1... | collective-permute-start | bytes 3145736 | tf_op jit(solution)/shard_map/ppermute | solution.py:833
  145.4 72.1 %collective-permute-start.11 = (f32[128,2048]{1,0:T(8,128)S(1)}, f32[128,2048]{1,0:T(8,128)S(1)}, u32[]{:S(2)}, u32[]{:S(2)}) collective-permute-start(f32[128,2048]{1,0:T(8,128)S(1)} %get-tuple-element.98), channel_id=1, source_target_pairs={{1,0},{4,1},{5,4},{8,5},{9,8},{12,9},{13,12},{16,13},{17,16},{20,1... | collective-permute-start | bytes 3145736 | tf_op jit(solution)/shard_map/ppermute | solution.py:749
  146.7 68.7 %collective-permute-start.13 = (bf16[256,2048]{1,0:T(8,128)(2,1)S(1)}, bf16[256,2048]{1,0:T(8,128)(2,1)S(1)}, u32[]{:S(2)}, u32[]{:S(2)}) collective-permute-start(bf16[256,2048]{1,0:T(8,128)(2,1)S(1)} %get-tuple-element.102), channel_id=1, source_target_pairs={{0,2},{2,0},{1,3},{3,1},{4,6},{6,4},{5,7},{7,5},{8,10},{10,8},{9,1... | collective-permute-start | bytes 3145736 | tf_op jit(solution)/shard_map/ppermute | solution.py:833
  147.3 67.0 %collective-permute-start.14 = (bf16[256,2048]{1,0:T(8,128)(2,1)S(1)}, bf16[256,2048]{1,0:T(8,128)(2,1)S(1)}, u32[]{:S(2)}, u32[]{:S(2)}) collective-permute-start(bf16[256,2048]{1,0:T(8,128)(2,1)S(1)} %get-tuple-element.103), channel_id=1, source_target_pairs={{0,2},{2,0},{1,3},{3,1},{4,6},{6,4},{5,7},{7,5},{8,10},{10,8},{9,1... | collective-permute-start | bytes 3145736 | tf_op jit(solution)/shard_map/ppermute | solution.py:833

commit v2 on v1

--- a/solution.py
+++ b/solution.py
@@ -15,8 +15,8 @@
 HALO_BLK = 2
 NEG = -1e30
 WINDOW = 3
-PER_STATS = 4
-PER_GRADIENTS = 4
+PER_STATS = 8
+PER_GRADIENTS = 8
 ROWS = ("seq", "section")
 NT = (((1,), (1,)), ((), ()))
 TN = (((0,), (0,)), ((), ()))
@@ -144,24 +144,42 @@
     )(pltpu.with_memory_space_constraint(states, pltpu.HBM))
 
 
-def project_own(states, queries, grads, key_weight, value_weight, cuts, group):
+def take_edges(queries, grads):
+    tokens, columns = queries.shape
+
+    def body(query_ref, grad_ref, up_ref, down_ref, sems):
+        copies = []
+        for i, (first, out_ref) in enumerate(((tokens - BLOCK, up_ref), (0, down_ref))):
+            for at, ref in enumerate((query_ref, grad_ref)):
+                copies.append(
+                    pltpu.make_async_copy(
+                        ref.at[pl.ds(first, BLOCK), :],
+                        out_ref.at[:, pl.ds(at * columns, columns)],
+                        sems.at[2 * i + at],
+                    )
+                )
+                copies[-1].start()
+        for copy in copies:
+            copy.wait()
+
+    edge = jax.ShapeDtypeStruct((BLOCK, 2 * columns), BF16)
+    return call(
+        body, [ANYWHERE] * 2, [HERE] * 2, [edge, edge], [pltpu.SemaphoreType.DMA((4,))], 0, 16 * BLOCK * columns
+    )(*[pltpu.with_memory_space_constraint(a, pltpu.HBM) for a in (queries, grads)])
+
+
+def project_own(states, key_weight, value_weight, cuts, group):
     rows, depth = states.shape
     columns = key_weight.shape[1]
-    tokens = queries.shape[0]
     weights = Weights(key_weight, True, group)
     count = len(cuts)
 
-    def body(states_ref, query_ref, grad_ref, key_ref, value_ref, *refs):
+    def body(states_ref, key_ref, value_ref, *refs):
         outs = refs[: 2 * count]
-        up_ref, down_ref = refs[2 * count : 2 * count + 2]
-        buffer, sems = refs[2 * count + 2 :]
+        buffer, sems = refs[2 * count :]
         owners = sources(group)[:1]
         both = (key_ref, value_ref)
         weights.start(both, buffer, sems, owners, WINDOW)
-        for at, ref in enumerate((query_ref, grad_ref)):
-            lanes = slice(at * columns, (at + 1) * columns)
-            up_ref[:, lanes] = ref[tokens - BLOCK :, :]
-            down_ref[:, lanes] = ref[:BLOCK, :]
 
         def step(j, carry):
             weights.advance(both, buffer, sems, owners, j)
@@ -178,17 +196,16 @@
     shapes = []
     for first, last in cuts:
         shapes += [jax.ShapeDtypeStruct((last - first, columns), F32)] * 2
-    edge = jax.ShapeDtypeStruct((BLOCK, 2 * columns), BF16)
     out = call(
         body,
-        [HERE] * 3 + [ANYWHERE] * 2,
-        [HERE] * (len(shapes) + 2),
-        shapes + [edge, edge],
+        [HERE] + [ANYWHERE] * 2,
+        [HERE] * len(shapes),
+        shapes,
         [weights.scratch(1), weights.semaphores(1)],
         4 * rows * depth * columns,
         2 * rows * depth + 4 * depth * columns,
-    )(states, queries, grads, key_weight, value_weight)
-    return [(out[2 * i], out[2 * i + 1]) for i in range(count)], out[-2], out[-1]
+    )(states, key_weight, value_weight)
+    return [(out[2 * i], out[2 * i + 1]) for i in range(count)]
 
 
 def project_rest(partial, arrived, key_weight, value_weight, held, group, base=0, height=None, into=None):
@@ -379,7 +396,7 @@
 
 
 def row_stats(
-    band, tiles_list, kvs, queries, grads, below, above, earlier, last, keep, rate
+    band, tiles_list, kvs, queries, grads, below, above, earlier, send, keep, rate
 ):
     own_count = queries.shape[0] // BLOCK
     columns = queries.shape[1]
@@ -406,20 +423,22 @@
                 head = pair * per + k
                 stats = tile_stats(bands, tiles_list, tokens, kv_refs, head, rate, kept)
                 results = []
+                blank = jnp.zeros((1, BLOCK), F32)
                 for t in range(-1, own_count + 1):
                     mine = [stats[t]] if t in stats else []
                     if extra:
                         mine.append(read_stats(rest[0], head, 3 * (t + 1)))
+                    if not mine:
+                        mine = [(blank, blank, blank)]
                     results += mine[0] if len(mine) == 1 else fold(mine, rate)
-                blank = [jnp.zeros((1, BLOCK), F32)]
                 out_ref[head] = jnp.concatenate(
-                    results + blank * (depth - len(results)), axis=0
+                    results + [blank] * (depth - len(results)), axis=0
                 )
-                if last:
-                    lower, upper = results[:6], results[-6:]
+                if send:
+                    upper, lower = [results[3 * (t + 1) : 3 * (t + 2)] for t in send]
                     for ref, flag in zip(rest[len(extra) + 1 : len(extra) + 3], (even, jnp.logical_not(even))):
                         picked = [jnp.where(flag, u, d) for u, d in zip(upper, lower)]
-                        ref[head] = jnp.concatenate(picked + blank * 2, axis=0)
+                        ref[head] = jnp.concatenate(picked + [blank] * 5, axis=0)
             return carry
 
         lax.fori_loop(0, heads // per, step, 0)
@@ -427,7 +446,7 @@
     frames = sum(kv[0].shape[0] for kv in kvs)
     flat = [array for kv in kvs for array in kv]
     shapes = [jax.ShapeDtypeStruct((heads, depth, BLOCK), F32)]
-    if last:
+    if send:
         shapes += [jax.ShapeDtypeStruct((heads, 8, BLOCK), F32)] * 2
     if keep:
         ((group, first, end),) = tiles_list[0].groups
@@ -495,8 +514,9 @@
         bands, refs = Bands(refs[:3], own_count), refs[3:]
         tokens = Tokens(own_count, columns, refs[: len(shared)])
         refs = refs[len(shared) :]
-        key_ref, value_ref, stat_ref, even_ref, odd_ref = refs[:5]
-        both, refs = refs[5 : 5 + len(sources_in)], refs[5 + len(sources_in) :]
+        key_ref, value_ref, stat_ref = refs[:3]
+        swap_refs, refs = refs[3 : 3 + len(swaps)], refs[3 + len(swaps) :]
+        both, refs = refs[: len(sources_in)], refs[len(sources_in) :]
         extra_refs, refs = refs[: len(extra)], refs[len(extra) :]
         known_refs, refs = refs[: len(known)], refs[len(known) + len(earlier) :]
         if loads:
@@ -515,13 +535,11 @@
             rows = {}
             for t in touched:
                 parts = [read_stats(stat_ref, head, 3 * (t + 1))]
+                even_ref, odd_ref = swap_refs[:2] if 0 <= t < own_count else swap_refs[2:]
+                first, second = read_stats(even_ref, head, 0), read_stats(odd_ref, head, 0)
                 if t <= 0:
-                    row = 3 * (t + 1)
-                    first, second = read_stats(odd_ref, head, row), read_stats(even_ref, head, row)
-                    parts.append([jnp.where(even, a, b) for a, b in zip(first, second)])
+                    parts.append([jnp.where(even, b, a) for a, b in zip(first, second)])
                 if t >= own_count - 1:
-                    row = 3 * (t - own_count + 1)
-                    first, second = read_stats(even_ref, head, row), read_stats(odd_ref, head, row)
                     parts.append([jnp.where(even, a, b) for a, b in zip(first, second)])
                 top, total, weighted = fold(parts, rate)
                 rows[t] = (top * rate + jnp.log2(total), weighted / total)
@@ -632,7 +650,7 @@
     out = call(
         body,
         [SCALARS] * 3
-        + [HERE] * (len(shared) + 5)
+        + [HERE] * (len(shared) + 3 + len(swaps))
         + ([ANYWHERE] * 2 if loads else [HERE])
         + [HERE] * (len(extra) + len(known) + len(earlier)),
         [HERE] * len(shapes),
@@ -641,7 +659,7 @@
         20 * frames * 2 * BLOCK * columns + 4 * frames * columns * features * (group - 1),
         8 * frames * columns,
         {
-            8 + len(shared) + len(sources_in) + len(extra) + len(known) + i: i
+            6 + len(swaps) + len(shared) + len(sources_in) + len(extra) + len(known) + i: i
             for i in range(len(earlier))
         },
     )(*band, *shared, *kv, stats, *swaps, *sources_in, *extra, *known, *earlier)
@@ -777,13 +795,12 @@
     for rows in take_rows(encoder_states, row_cuts[:1]) + take_rows(encoder_states, row_cuts[1:]):
         arrived.append([lax.ppermute(rows, "tensor", turn) for turn in turns])
 
-    partial, edge_up, edge_down = project_own(
-        encoder_states, queries, out_grad, key_weight, value_weight, row_cuts, group
-    )
-    edge_up, edge_down, band_sent = lax.optimization_barrier((edge_up, edge_down, band_blocks))
+    edge_up, edge_down = take_edges(queries, out_grad)
     below = shifted(edge_up, 1)
     above = shifted(edge_down, -1)
-    band = (shifted(band_sent, 1), band_blocks, shifted(band_sent, -1))
+    band = (shifted(band_blocks, 1), band_blocks, shifted(band_blocks, -1))
+
+    partial = project_own(encoder_states, key_weight, value_weight, row_cuts, group)
 
     def rest(i, held, **place):
         return project_rest(partial[i], arrived[i], key_weight, value_weight, held, group, **place)
@@ -791,25 +808,30 @@
     def statistics(*where, **what):
         return row_stats(band, *where, queries, out_grad, below, above, *what.values(), rate)
 
-    low_kv, held = rest(0, None)
-    high_kv, held = rest(1, held)
+    def exchange(arrays):
+        return tuple(swapped(array, first) for first, array in enumerate(arrays))
+
     low_tiles, high_tiles = [Tiles(own_count, first, last, True) for first, last in cuts[:2]]
     inner = [Tiles(own_count, first, last, False, edge) for first, last in cuts[2:]]
     inner_tiles = Tiles(own_count, edge, frame_blocks - edge, False)
-    (stats,) = statistics([low_tiles, high_tiles], [low_kv, high_kv], earlier=None, last=False, keep=False)
+    low_kv, held = rest(0, None)
+    (stats,) = statistics([low_tiles], [low_kv], earlier=None, send=None, keep=False)
+    high_kv, held = rest(1, held)
+    stats, *outer = statistics([high_tiles], [high_kv], earlier=stats, send=(own_count, -1), keep=False)
+    early = exchange(outer)
     height = (frame_blocks - 2 * edge) * BLOCK
     kv, held = rest(2, held, height=height)
-    stats, *first_kept = statistics(inner[:1], [kv], earlier=stats, last=False, keep=True)
+    stats, *first_kept = statistics(inner[:1], [kv], earlier=stats, send=None, keep=True)
     kv, stats = lax.optimization_barrier((kv, stats))
     inner_kv, held = rest(3, held, base=(middle - edge) * BLOCK, height=height, into=kv)
-    stats, first_swap, second_swap, *second_kept = statistics(
-        inner[1:], [inner_kv], earlier=stats, last=True, keep=True
+    stats, first_own, second_own, *second_kept = statistics(
+        inner[1:], [inner_kv], earlier=stats, send=(own_count - 1, 0), keep=True
     )
+    late = exchange((first_own, second_own))
     kept = [(edge, *first_kept), (middle, *second_kept)]
-    swaps = (swapped(first_swap, 0), swapped(second_swap, 1))
 
     chunks = [(inner_tiles, inner_kv), (low_tiles, low_kv), (high_tiles, high_kv)]
-    shared = (queries, out_grad, below, above, stats, swaps, key_weight, value_weight)
+    shared = (queries, out_grad, below, above, stats)
     out, sent = [], []
     totals = away = deferred = None
     for i, (tiles, kv) in enumerate(chunks):
@@ -819,6 +841,9 @@
                 tiles,
                 kv,
                 *shared,
+                early + late if i else early,
+                key_weight,
+                value_weight,
                 away,
                 deferred,
                 () if i else kept,
@@ -829,7 +854,7 @@
             )
         )
         totals, away = out[i][0], out[i][4]
-        deferred = () if i else (inner_kv[0], out[0][1])
+        deferred = (inner_kv[0], out[0][1]) if i == 1 else ()
         sent.append([lax.ppermute(term, "tensor", turn) for term, turn in zip(out[i][2], turns)])
 
     from_below = shifted(out[2][3][own_count], 1)

time: 219 us -> 191 us (0.87)
  waiting for transfers between devices: 78.4 us -> 41.5 us
  starting transfers between devices: 27.4 us -> 32.3 us
  Pallas kernels: 112 us -> 115 us
    ppermute x3, waiting for transfers between devices: 49.2 us -> 27 us  [on_device(): lax.ppermute(term, 'tensor', turn)]
    ppermute x4, waiting for transfers between devices: 29.1 us -> 13.7 us  [on_device(): arrived.append([lax.ppermute(rows, 'tensor', turn) for turn in turns])]
    ppermute x2 -> x4, starting transfers between devices: 3.4 us -> 6.58 us  [swapped(): return lax.ppermute(value, ROWS, pairs)]
    pallas_call x4 -> x5, Pallas kernels: 56.4 us -> 58.9 us  [the longest x3 41.3 us: gradients(): call(body, [SCALARS] * 3 + [HERE] * (len(shared) + 3 + len(swaps)) + ([AN...]
    pallas_call x3 -> x4, Pallas kernels: 11.5 us -> 11.9 us  [row_stats(): call(body, [SCALARS] * 3 + [HERE] * len(shared) + [HERE] * (len(flat) + l...]
  transfers between devices with their start and end apart: 15 -> 17, of which waited for: 5 -> 4; matrix products, arithmetic and copies ran while one was open for 0% -> 0% of each run, Pallas kernels for 29% -> 59%
where the time goes in v2:
time: 191 us
  Pallas kernels  115 us (60%)
  waiting for transfers between devices  41.5 us (22%)
  starting transfers between devices  32.3 us (17%)
    pallas_call x3, Pallas kernels, gradients(): call(body, [SCALARS] * 3 + [HERE] * (len(shared) + 3 + len(swaps)) + ([AN...  41.3 us
    ppermute x3, waiting for transfers between devices, on_device(): lax.ppermute(term, 'tensor', turn)  27 us
    pallas_call x4, Pallas kernels, project_rest(): call(body, [HERE] * (2 + count + len(earlier)) + ([ANYWHERE] * 2 if loads...  20.5 us
    pallas_call x1, Pallas kernels, own_terms(): call(body, [HERE] * 2 + [ANYWHERE] * 2, HERE, jax.ShapeDtypeStruct((rows,...  16.3 us
    pallas_call x1, Pallas kernels, project_own(): call(body, [HERE] + [ANYWHERE] * 2, [HERE] * len(shapes), shapes, [weight...  16.1 us
    ppermute x6, starting transfers between devices, shifted(): lax.ppermute(value, ROWS, [(source, source + steps) for source in range(f...  15.1 us
    ppermute x4, waiting for transfers between devices, on_device(): arrived.append([lax.ppermute(rows, 'tensor', turn) for turn in turns])  13.7 us
    pallas_call x4, Pallas kernels, row_stats(): call(body, [SCALARS] * 3 + [HERE] * len(shared) + [HERE] * (len(flat) + l...  11.9 us
  transfers between devices with their start and end apart: 17, of which 4 were waited for; matrix products, arithmetic and copies ran while one was open for 0% of the time, Pallas kernels for 59%

profile of v2, /device:TPU:0, one launch (start us, length us, event | category | flops | bytes accessed | tf_op | source)
XLA Modules:
  0.0 190.9 jit_solution(16910298056839049118)
XLA Ops:
  0.6 1.3 collective-permute-start.1
  1.9 1.2 shard_map.79
  3.2 0.0 copy-start.2
  3.2 3.0 %collective-permute-start.4 = (bf16[256,2048]{1,0:T(8,128)(2,1)S(1)}, bf16[256,2048]{1,0:T(8,128)(2,1)S(1)}, u32[]{:S(2)}, u32[]{:S(2)}) collective-permute-start(bf16[256,2048]{1,0:T(8,128)(2,1)S(1)} %shard_map.79), channel_id=1, source_target_pairs={{0,2},{2,0},{1,3},{3,1},{4,6},{6,4},{5,7},{7,5},{8,10},{10,8},{9,1... | collective-permute-start | bytes 3145736 | tf_op jit(solution)/shard_map/ppermute | solution.py:796
  6.2 1.5 shard_map.81
  7.8 0.2 collective-permute-start.7
  8.0 1.5 shard_map.77
  9.6 2.8 %collective-permute-start.2 = (bf16[128,4096]{1,0:T(8,128)(2,1)S(1)}, bf16[128,4096]{1,0:T(8,128)(2,1)S(1)}, u32[]{:S(2)}, u32[]{:S(2)}) collective-permute-start(bf16[128,4096]{1,0:T(8,128)(2,1)S(1)} %get-tuple-element.53), channel_id=1, source_target_pairs={{0,1},{1,4},{4,5},{5,8},{8,9},{9,12},{12,13},{13,16},{16,17},{17,2... | collective-permute-start | bytes 3145736 | tf_op jit(solution)/shard_map/ppermute | solution.py:767
  12.4 1.3 collective-permute-start.3
  13.7 0.0 copy-done.2
  13.7 16.1 %shard_map.78 = (f32[256,2048]{1,0:T(8,128)S(1)}, f32[256,2048]{1,0:T(8,128)S(1)}, f32[256,2048]{1,0:T(8,128)S(1)}, f32[256,2048]{1,0:T(8,128)S(1)}, f32[128,204...) custom-call(bf16[768,2048]{1,0:T(8,128)(2,1)S(1)} %copy-done.2, ...), custom_call_target="tpu_custom_call" | custom-call | flops 12884901888 | bytes 19922944 | tf_op jit(solution)/shard_map/pallas_call | solution.py:199
  29.8 0.0 collective-permute-done.4.refs_0_
  29.8 2.3 %collective-permute-start.5 = (bf16[128,2048]{1,0:T(8,128)(2,1)S(1)}, bf16[128,2048]{1,0:T(8,128)(2,1)S(1)}, u32[]{:S(2)}, u32[]{:S(2)}) collective-permute-start(bf16[128,2048]{1,0:T(8,128)(2,1)S(1)} %get-tuple-element.61), channel_id=1, source_target_pairs={{0,2},{2,0},{1,3},{3,1},{4,6},{6,4},{5,7},{7,5},{8,10},{10,8},{9,1... | collective-permute-start | bytes 1572872 | tf_op jit(solution)/shard_map/ppermute | solution.py:796
  32.1 7.5 %shard_map.80 = (bf16[256,2048]{1,0:T(8,128)(2,1)S(1)}, bf16[256,2048]{1,0:T(8,128)(2,1)S(1)}, bf16[1,2,8,2048,256]{4,3,2,1,0:T(8,128)(2,1)S(1)}) custom-call(f32[256,2048]{1,0:T(8,128)S(1)} %get-tuple-element.55.key_part, f32[256,2048]{1,0:T(8,128)S(1)} %get-tuple-element.56.value_part, bf16[256,2048]{1,0:T(8,128)(2,1)S(1)} %collective-permute-done.4.refs_0_, ...), custom_call_target="tpu_custom_call" | custom-call | flops 4294967296 | bytes 16777216 | tf_op jit(solution)/shard_map/pallas_call | solution.py:247
  39.6 12.7 %collective-permute-done.7.refs_0_ = bf16[256,2048]{1,0:T(8,128)(2,1)S(1)} collective-permute-done((bf16[256,2048]{1,0:T(8,128)(2,1)S(1)}, bf16[256,2048]{1,0:T(8,128)(2,1)S(1)}, u32[]{:S(2)}, u32[]{:S(2)}) %collective-permute-start.7) | collective-permute-done | bytes 1048608 | tf_op jit(solution)/shard_map/ppermute | solution.py:796
  52.3 2.3 %collective-permute-start.6 = (bf16[128,2048]{1,0:T(8,128)(2,1)S(1)}, bf16[128,2048]{1,0:T(8,128)(2,1)S(1)}, u32[]{:S(2)}, u32[]{:S(2)}) collective-permute-start(bf16[128,2048]{1,0:T(8,128)(2,1)S(1)} %get-tuple-element.64), channel_id=1, source_target_pairs={{0,2},{2,0},{1,3},{3,1},{4,6},{6,4},{5,7},{7,5},{8,10},{10,8},{9,1... | collective-permute-start | bytes 1572872 | tf_op jit(solution)/shard_map/ppermute | solution.py:796
  54.6 5.7 %shard_map.83 = (bf16[256,2048]{1,0:T(8,128)(2,1)S(1)}, bf16[256,2048]{1,0:T(8,128)(2,1)S(1)}) custom-call(f32[256,2048]{1,0:T(8,128)S(1)} %get-tuple-element.68.key_part, f32[256,2048]{1,0:T(8,128)S(1)} %get-tuple-element.69.value_part, bf16[256,2048]{1,0:T(8,128)(2,1)S(1)} %collective-permute-done.7.refs_0_, ...), custom_call_target="tpu_custom_call" | custom-call | flops 4294967296 | bytes 1048576 | tf_op jit(solution)/shard_map/pallas_call | solution.py:247
  60.3 0.0 collective-permute-done.1.refs_2_
  60.3 0.0 copy-done.7
  60.3 2.1 %collective-permute-start = (s32[2,2]{1,0:T(2,128)S(1)}, s32[2,2]{1,0:T(2,128)S(1)}, u32[]{:S(2)}, u32[]{:S(2)}) collective-permute-start(s32[2,2]{1,0:T(2,128)S(1)} %copy-done.7), channel_id=1, source_target_pairs={{0,1},{1,4},{4,5},{5,8},{8,9},{9,12},{12,13},{13,16},{16,17},{17,2... | collective-permute-start | bytes 56 | tf_op jit(solution)/shard_map/ppermute | solution.py:767
  62.3 0.8 collective-permute-done.refs_0_
  63.1 0.0 collective-permute-done.2.refs_5_
  63.2 0.0 collective-permute-done.3.refs_6_
  63.2 0.0 copy-done
  63.2 0.0 copy-done.1
  63.2 3.7 %shard_map.84.refs_9_ = f32[16,16,128]{2,1,0:T(8,128)S(1)} custom-call(s32[2,2]{1,0:T(2,128)S(1)} %collective-permute-done.refs_0_, s32[2,2]{1,0:T(2,128)S(1)} %copy-done.7, s32[2,2]{1,0:T(2,128)S(1)} %collective-permute-done.1.refs_2_, bf16[256,2048]{1,0:T(8,128)(2,1)S(1)} %copy-done, bf16[256,2048]{1,0:T(8,128)(2,1)S(1)} %copy-done.1, ...), custom_call_target="tpu_custom_call" | custom-call | flops 1073741824 | bytes 6291456 | tf_op jit(solution)/shard_map/pallas_call | solution.py:454
  66.8 4.0 %shard_map.85 = (f32[16,16,128]{2,1,0:T(8,128)S(1)}, f32[16,8,128]{2,1,0:T(8,128)S(1)}, f32[16,8,128]{2,1,0:T(8,128)S(1)}) custom-call(s32[2,2]{1,0:T(2,128)S(1)} %collective-permute-done.refs_0_, s32[2,2]{1,0:T(2,128)S(1)} %copy-done.7, s32[2,2]{1,0:T(2,128)S(1)} %collective-permute-done.1.refs_2_, bf16[256,2048]{1,0:T(8,128)(2,1)S(1)} %copy-done, ...), custom_call_target="tpu_custom_call" | custom-call | flops 1073741824 | bytes 6291456 | tf_op jit(solution)/shard_map/pallas_call | solution.py:454
  70.9 2.3 %collective-permute-start.8 = (f32[16,8,128]{2,1,0:T(8,128)S(1)}, f32[16,8,128]{2,1,0:T(8,128)S(1)}, u32[]{:S(2)}, u32[]{:S(2)}) collective-permute-start(f32[16,8,128]{2,1,0:T(8,128)S(1)} %get-tuple-element.81), channel_id=1, source_target_pairs={{0,1},{1,0},{4,5},{5,4},{8,9},{9,8},{12,13},{13,12},{16,17},{17,16... | collective-permute-start | bytes 196616 | tf_op jit(solution)/shard_map/ppermute | solution.py:774
  73.1 0.7 collective-permute-start.9
  73.8 0.9 collective-permute-done.6.refs_0_
  74.7 3.7 %shard_map.82 = (bf16[256,2048]{1,0:T(8,128)(2,1)S(1)}, bf16[256,2048]{1,0:T(8,128)(2,1)S(1)}) custom-call(f32[128,2048]{1,0:T(8,128)S(1)} %get-tuple-element.62.key_part, f32[128,2048]{1,0:T(8,128)S(1)} %get-tuple-element.63.value_part, bf16[128,2048]{1,0:T(8,128)(2,1)S(1)} %collective-permute-done.6.refs_0_, ...), custom_call_target="tpu_custom_call" | custom-call | flops 2147483648 | bytes 524288 | tf_op jit(solution)/shard_map/pallas_call | solution.py:247
  78.4 2.1 %shard_map.86 = (f32[16,16,128]{2,1,0:T(8,128)S(1)}, f32[16,128,256]{2,1,0:T(8,128)S(1)}, f32[16,128,256]{2,1,0:T(8,128)S(1)}) custom-call(s32[2,2]{1,0:T(2,128)S(1)} %collective-permute-done.refs_0_, s32[2,2]{1,0:T(2,128)S(1)} %copy-done.7, s32[2,2]{1,0:T(2,128)S(1)} %collective-permute-done.1.refs_2_, bf16[256,2048]{1,0:T(8,128)(2,1)S(1)} %copy-done, ...), custom_call_target="tpu_custom_call" | custom-call | flops 1073741824 | bytes 6291456 | tf_op jit(solution)/shard_map/pallas_call | solution.py:454
  80.5 0.0 copy-start.3
  80.5 1.3 copy-done.3
  81.8 0.0 collective-permute-done.5.refs_0_
  81.8 3.7 %shard_map.87 = (bf16[256,2048]{1,0:T(8,128)(2,1)S(1)}, bf16[256,2048]{1,0:T(8,128)(2,1)S(1)}) custom-call(f32[128,2048]{1,0:T(8,128)S(1)} %get-tuple-element.59.key_part, f32[128,2048]{1,0:T(8,128)S(1)} %get-tuple-element.60.value_part, bf16[128,2048]{1,0:T(8,128)(2,1)S(1)} %collective-permute-done.5.refs_0_, ...), custom_call_target="tpu_custom_call", output_to_operand_aliasing={{0}: (3, {}), {1}: (4, {})} | custom-call | flops 2147483648 | bytes 524288 | tf_op jit(solution)/shard_map/pallas_call | solution.py:247
  85.5 0.0 copy-done.5
  85.5 0.0 copy-start.4
  85.5 0.0 copy-start.6
  85.5 2.1 %shard_map.88 = (f32[16,16,128]{2,1,0:T(8,128)S(1)}, f32[16,8,128]{2,1,0:T(8,128)S(1)}, f32[16,8,128]{2,1,0:T(8,128)S(1)}, f32[16,128,256]{2,1,0:T(8,128)S(1)}, f32[16,128,256]{2,1,0:T(8,128)S(1)}) custom-call(s32[2,2]{1,0:T(2,128)S(1)} %collective-permute-done.refs_0_, s32[2,2]{1,0:T(2,128)S(1)} %copy-done.7, s32[2,2]{1,0:T(2,128)S(1)} %collective-permute-done.1.refs_2_, ...), custom_call_target="tpu_custom_call" | custom-call | flops 1073741824 | bytes 6291456 | tf_op jit(solution)/shard_map/pallas_call | solution.py:454
  87.7 2.8 %collective-permute-start.10 = (f32[16,8,128]{2,1,0:T(8,128)S(1)}, f32[16,8,128]{2,1,0:T(8,128)S(1)}, u32[]{:S(2)}, u32[]{:S(2)}) collective-permute-start(f32[16,8,128]{2,1,0:T(8,128)S(1)} %get-tuple-element.83), channel_id=1, source_target_pairs={{0,1},{1,0},{4,5},{5,4},{8,9},{9,8},{12,13},{13,12},{16,17},{17,16... | collective-permute-start | bytes 196616 | tf_op jit(solution)/shard_map/ppermute | solution.py:774
  90.5 0.8 collective-permute-start.11
  91.4 0.0 collective-permute-done.8.refs_8_.refs_10_
  91.4 0.0 collective-permute-done.9.refs_9_.refs_11_
  91.4 10.2 %shard_map.89 = (bf16[768,2048]{1,0:T(8,128)(2,1)S(1)}, bf16[768,2048]{1,0:T(8,128)(2,1)S(1)}, bf16[16,256,256]{2,1,0:T(8,128)(2,1)S(1)}, bf16[256,2048]{1,0:T(8,128)(2,1)}, bf16[1,2,8,256,2048]{4,3,2,1,0:T(8,128)(2,1)S(1)}) custom-call(s32[2,2]{1,0:T(2,128)S(1)} %collective-permute-done.refs_0_, s32[2,2]{1,0:T(2,128)S(1)} %copy-done.7, ...), custom_call_target="tpu_custom_call" | custom-call | flops 6979321856 | bytes 4194304 | tf_op jit(solution)/shard_map/pallas_call | solution.py:650
  101.6 0.6 collective-permute-start.16
  102.2 0.0 collective-permute-done.10.refs_12_
  102.2 0.0 collective-permute-done.11.refs_13_
  102.2 14.5 %shard_map.90 = (bf16[768,2048]{1,0:T(8,128)(2,1)S(1)}, bf16[768,2048]{1,0:T(8,128)(2,1)S(1)}, f32[256,2048]{1,0:T(8,128)S(1)}, bf16[256,2048]{1,0:T(8,128)(2,1)}, f32[128,2048]{1,0:T(8,128)S(1)}) custom-call(s32[2,2]{1,0:T(2,128)S(1)} %collective-permute-done.refs_0_, s32[2,2]{1,0:T(2,128)S(1)} %copy-done.7, ...), custom_call_target="tpu_custom_call", output_to_operand_aliasing={{0}: (15, {}), {1}: (16, {})} | custom-call | flops 6979321856 | bytes 4194304 | tf_op jit(solution)/shard_map/pallas_call | solution.py:650
  116.7 16.6 %shard_map.91 = (bf16[768,2048]{1,0:T(8,128)(2,1)S(1)}, bf16[768,2048]{1,0:T(8,128)(2,1)S(1)}, f32[256,2048]{1,0:T(8,128)S(1)}, bf16[256,2048]{1,0:T(8,128)(2,1)}, f32[128,2048]{1,0:T(8,128)}) custom-call(s32[2,2]{1,0:T(2,128)S(1)} %collective-permute-done.refs_0_, s32[2,2]{1,0:T(2,128)S(1)} %copy-done.7, ...), custom_call_target="tpu_custom_call", output_to_operand_aliasing={{0}: (17, {}), {1}: (18, {})} | custom-call | flops 6979321856 | bytes 4194304 | tf_op jit(solution)/shard_map/pallas_call | solution.py:650
  133.3 6.1 %collective-permute-start.12 = (f32[128,2048]{1,0:T(8,128)}, f32[128,2048]{1,0:T(8,128)S(1)}, u32[]{:S(2)}, u32[]{:S(2)}) collective-permute-start(f32[128,2048]{1,0:T(8,128)} %get-tuple-element.97), channel_id=1, source_target_pairs={{0,1},{1,4},{4,5},{5,8},{8,9},{9,12},{12,13},{13,16},{16,17},{17,2... | collective-permute-start | bytes 3145736 | tf_op jit(solution)/shard_map/ppermute | solution.py:767
  139.4 1.6 collective-permute-start.14
  141.0 1.5 collective-permute-start.13
  142.5 0.6 collective-permute-start.15
  143.1 16.3 %shard_map.93.own_ref = bf16[768,2048]{1,0:T(8,128)(2,1)S(1)} custom-call(bf16[768,2048]{1,0:T(8,128)(2,1)S(1)} %get-tuple-element.99.key_grad_ref, bf16[768,2048]{1,0:T(8,128)(2,1)S(1)} %get-tuple-element.100.value_grad_ref, bf16[4096,2048]{1,0:T(8,128)(2,1)} %key_ref.3, bf16[4096,2048]{1,0:T(8,128)(2,1)} %value_ref.3), custom_call_target="tpu_custom_call" | custom-call | flops 12884901888 | bytes 16777216 | tf_op jit(solution)/shard_map/pallas_call | solution.py:686
  159.4 0.0 collective-permute-done.16.refs_0_
  159.4 1.1 shard_map.94.refs_1_
  160.5 27.0 %collective-permute-done.15.refs_0_ = bf16[256,2048]{1,0:T(8,128)(2,1)S(1)} collective-permute-done((bf16[256,2048]{1,0:T(8,128)(2,1)}, bf16[256,2048]{1,0:T(8,128)(2,1)S(1)}, u32[]{:S(2)}, u32[]{:S(2)}) %collective-permute-start.15) | collective-permute-done | bytes 1048608 | tf_op jit(solution)/shard_map/ppermute | solution.py:858
  187.5 1.1 shard_map.95.refs_1_
  188.5 0.0 collective-permute-done.14.refs_0_
  188.5 1.1 shard_map.96
  189.6 0.0 collective-permute-done.12.below_ref
  189.6 0.0 collective-permute-done.13.above_ref
  189.6 1.1 shard_map.92
  (6 shorter events, 0.0 us)
Async XLA Ops:
  0.6 59.6 %collective-permute-start.1 = (s32[2,2]{1,0:T(2,128)}, s32[2,2]{1,0:T(2,128)S(1)}, u32[]{:S(2)}, u32[]{:S(2)}) collective-permute-start(s32[2,2]{1,0:T(2,128)} %refs_1_.15), channel_id=1, source_target_pairs={{1,0},{4,1},{5,4},{8,5},{9,8},{12,9},{13,12},{16,13},{17,16},{20,1... | collective-permute-start | bytes 56 | tf_op jit(solution)/shard_map/ppermute | solution.py:767
  3.2 10.5 %copy-start.2 = (bf16[768,2048]{1,0:T(8,128)(2,1)S(1)}, bf16[768,2048]{1,0:T(8,128)(2,1)}, u32[]{:S(2)}) copy-start(bf16[768,2048]{1,0:T(8,128)(2,1)} %states_ref.5) | copy-start | bytes 9437188
  3.2 26.6 %collective-permute-start.4 = (bf16[256,2048]{1,0:T(8,128)(2,1)S(1)}, bf16[256,2048]{1,0:T(8,128)(2,1)S(1)}, u32[]{:S(2)}, u32[]{:S(2)}) collective-permute-start(bf16[256,2048]{1,0:T(8,128)(2,1)S(1)} %shard_map.79), channel_id=1, source_target_pairs={{0,2},{2,0},{1,3},{3,1},{4,6},{6,4},{5,7},{7,5},{8,10},{10,8},{9,1... | collective-permute-start | bytes 3145736 | tf_op jit(solution)/shard_map/ppermute | solution.py:796
  7.8 44.5 %collective-permute-start.7 = (bf16[256,2048]{1,0:T(8,128)(2,1)S(1)}, bf16[256,2048]{1,0:T(8,128)(2,1)S(1)}, u32[]{:S(2)}, u32[]{:S(2)}) collective-permute-start(bf16[256,2048]{1,0:T(8,128)(2,1)S(1)} %get-tuple-element.70), channel_id=1, source_target_pairs={{0,2},{2,0},{1,3},{3,1},{4,6},{6,4},{5,7},{7,5},{8,10},{10,8},{9,1... | collective-permute-start | bytes 3145736 | tf_op jit(solution)/shard_map/ppermute | solution.py:796
  9.6 53.6 %collective-permute-start.2 = (bf16[128,4096]{1,0:T(8,128)(2,1)S(1)}, bf16[128,4096]{1,0:T(8,128)(2,1)S(1)}, u32[]{:S(2)}, u32[]{:S(2)}) collective-permute-start(bf16[128,4096]{1,0:T(8,128)(2,1)S(1)} %get-tuple-element.53), channel_id=1, source_target_pairs={{0,1},{1,4},{4,5},{5,8},{8,9},{9,12},{12,13},{13,16},{16,17},{17,2... | collective-permute-start | bytes 3145736 | tf_op jit(solution)/shard_map/ppermute | solution.py:767
  12.4 50.8 %collective-permute-start.3 = (bf16[128,4096]{1,0:T(8,128)(2,1)S(1)}, bf16[128,4096]{1,0:T(8,128)(2,1)S(1)}, u32[]{:S(2)}, u32[]{:S(2)}) collective-permute-start(bf16[128,4096]{1,0:T(8,128)(2,1)S(1)} %get-tuple-element.54), channel_id=1, source_target_pairs={{1,0},{4,1},{5,4},{8,5},{9,8},{12,9},{13,12},{16,13},{17,16},{20,1... | collective-permute-start | bytes 3145736 | tf_op jit(solution)/shard_map/ppermute | solution.py:767
  29.8 52.0 %collective-permute-start.5 = (bf16[128,2048]{1,0:T(8,128)(2,1)S(1)}, bf16[128,2048]{1,0:T(8,128)(2,1)S(1)}, u32[]{:S(2)}, u32[]{:S(2)}) collective-permute-start(bf16[128,2048]{1,0:T(8,128)(2,1)S(1)} %get-tuple-element.61), channel_id=1, source_target_pairs={{0,2},{2,0},{1,3},{3,1},{4,6},{6,4},{5,7},{7,5},{8,10},{10,8},{9,1... | collective-permute-start | bytes 1572872 | tf_op jit(solution)/shard_map/ppermute | solution.py:796
  52.3 22.5 %collective-permute-start.6 = (bf16[128,2048]{1,0:T(8,128)(2,1)S(1)}, bf16[128,2048]{1,0:T(8,128)(2,1)S(1)}, u32[]{:S(2)}, u32[]{:S(2)}) collective-permute-start(bf16[128,2048]{1,0:T(8,128)(2,1)S(1)} %get-tuple-element.64), channel_id=1, source_target_pairs={{0,2},{2,0},{1,3},{3,1},{4,6},{6,4},{5,7},{7,5},{8,10},{10,8},{9,1... | collective-permute-start | bytes 1572872 | tf_op jit(solution)/shard_map/ppermute | solution.py:796
  54.6 5.7 %copy-start.7 = (s32[2,2]{1,0:T(2,128)S(1)}, s32[2,2]{1,0:T(2,128)}, u32[]{:S(2)}) copy-start(s32[2,2]{1,0:T(2,128)} %refs_1_.15) | copy-start | bytes 52
  54.6 8.6 %copy-start = (bf16[256,2048]{1,0:T(8,128)(2,1)S(1)}, bf16[256,2048]{1,0:T(8,128)(2,1)}, u32[]{:S(2)}) copy-start(bf16[256,2048]{1,0:T(8,128)(2,1)} %refs_3_.13) | copy-start | bytes 3145732
  54.6 8.6 %copy-start.1 = (bf16[256,2048]{1,0:T(8,128)(2,1)S(1)}, bf16[256,2048]{1,0:T(8,128)(2,1)}, u32[]{:S(2)}) copy-start(bf16[256,2048]{1,0:T(8,128)(2,1)} %refs_4_.13) | copy-start | bytes 3145732
  60.3 2.9 %collective-permute-start = (s32[2,2]{1,0:T(2,128)S(1)}, s32[2,2]{1,0:T(2,128)S(1)}, u32[]{:S(2)}, u32[]{:S(2)}) collective-permute-start(s32[2,2]{1,0:T(2,128)S(1)} %copy-done.7), channel_id=1, source_target_pairs={{0,1},{1,4},{4,5},{5,8},{8,9},{9,12},{12,13},{13,16},{16,17},{17,2... | collective-permute-start | bytes 56 | tf_op jit(solution)/shard_map/ppermute | solution.py:767
  70.9 20.5 %collective-permute-start.8 = (f32[16,8,128]{2,1,0:T(8,128)S(1)}, f32[16,8,128]{2,1,0:T(8,128)S(1)}, u32[]{:S(2)}, u32[]{:S(2)}) collective-permute-start(f32[16,8,128]{2,1,0:T(8,128)S(1)} %get-tuple-element.81), channel_id=1, source_target_pairs={{0,1},{1,0},{4,5},{5,4},{8,9},{9,8},{12,13},{13,12},{16,17},{17,16... | collective-permute-start | bytes 196616 | tf_op jit(solution)/shard_map/ppermute | solution.py:774
  73.1 18.2 %collective-permute-start.9 = (f32[16,8,128]{2,1,0:T(8,128)S(1)}, f32[16,8,128]{2,1,0:T(8,128)S(1)}, u32[]{:S(2)}, u32[]{:S(2)}) collective-permute-start(f32[16,8,128]{2,1,0:T(8,128)S(1)} %get-tuple-element.82), channel_id=1, source_target_pairs={{1,4},{4,1},{5,8},{8,5},{9,12},{12,9},{13,16},{16,13},{17,20},{20,... | collective-permute-start | bytes 196616 | tf_op jit(solution)/shard_map/ppermute | solution.py:774
  80.5 1.3 copy-start.3
  81.8 3.7 %copy-start.5 = (f32[16,128,256]{2,1,0:T(8,128)}, f32[16,128,256]{2,1,0:T(8,128)S(1)}, u32[]{:S(2)}) copy-start(f32[16,128,256]{2,1,0:T(8,128)S(1)} %get-tuple-element.86.refs_13_) | copy-start | bytes 6291460
  85.5 5.9 %copy-start.4 = (f32[16,128,256]{2,1,0:T(8,128)S(1)}, f32[16,128,256]{2,1,0:T(8,128)}, u32[]{:S(2)}) copy-start(f32[16,128,256]{2,1,0:T(8,128)} %copy-done.3) | copy-start | bytes 6291460
  85.5 5.9 %copy-start.6 = (f32[16,128,256]{2,1,0:T(8,128)S(1)}, f32[16,128,256]{2,1,0:T(8,128)}, u32[]{:S(2)}) copy-start(f32[16,128,256]{2,1,0:T(8,128)} %copy-done.5) | copy-start | bytes 6291460
  87.7 14.5 %collective-permute-start.10 = (f32[16,8,128]{2,1,0:T(8,128)S(1)}, f32[16,8,128]{2,1,0:T(8,128)S(1)}, u32[]{:S(2)}, u32[]{:S(2)}) collective-permute-start(f32[16,8,128]{2,1,0:T(8,128)S(1)} %get-tuple-element.83), channel_id=1, source_target_pairs={{0,1},{1,0},{4,5},{5,4},{8,9},{9,8},{12,13},{13,12},{16,17},{17,16... | collective-permute-start | bytes 196616 | tf_op jit(solution)/shard_map/ppermute | solution.py:774
  90.5 11.7 %collective-permute-start.11 = (f32[16,8,128]{2,1,0:T(8,128)S(1)}, f32[16,8,128]{2,1,0:T(8,128)S(1)}, u32[]{:S(2)}, u32[]{:S(2)}) collective-permute-start(f32[16,8,128]{2,1,0:T(8,128)S(1)} %get-tuple-element.84), channel_id=1, source_target_pairs={{1,4},{4,1},{5,8},{8,5},{9,12},{12,9},{13,16},{16,13},{17,20},{20,... | collective-permute-start | bytes 196616 | tf_op jit(solution)/shard_map/ppermute | solution.py:774
  101.6 57.8 %collective-permute-start.16 = (bf16[256,2048]{1,0:T(8,128)(2,1)}, bf16[256,2048]{1,0:T(8,128)(2,1)S(1)}, u32[]{:S(2)}, u32[]{:S(2)}) collective-permute-start(bf16[256,2048]{1,0:T(8,128)(2,1)} %get-tuple-element.103), channel_id=1, source_target_pairs={{0,2},{2,0},{1,3},{3,1},{4,6},{6,4},{5,7},{7,5},{8,10},{10,8},{9,1... | collective-permute-start | bytes 3145736 | tf_op jit(solution)/shard_map/ppermute | solution.py:858
  133.3 56.3 %collective-permute-start.12 = (f32[128,2048]{1,0:T(8,128)}, f32[128,2048]{1,0:T(8,128)S(1)}, u32[]{:S(2)}, u32[]{:S(2)}) collective-permute-start(f32[128,2048]{1,0:T(8,128)} %get-tuple-element.97), channel_id=1, source_target_pairs={{0,1},{1,4},{4,5},{5,8},{8,9},{9,12},{12,13},{13,16},{16,17},{17,2... | collective-permute-start | bytes 3145736 | tf_op jit(solution)/shard_map/ppermute | solution.py:767
  139.4 49.1 %collective-permute-start.14 = (bf16[256,2048]{1,0:T(8,128)(2,1)}, bf16[256,2048]{1,0:T(8,128)(2,1)S(1)}, u32[]{:S(2)}, u32[]{:S(2)}) collective-permute-start(bf16[256,2048]{1,0:T(8,128)(2,1)} %get-tuple-element.101), channel_id=1, source_target_pairs={{0,2},{2,0},{1,3},{3,1},{4,6},{6,4},{5,7},{7,5},{8,10},{10,8},{9,1... | collective-permute-start | bytes 3145736 | tf_op jit(solution)/shard_map/ppermute | solution.py:858
  141.0 48.6 %collective-permute-start.13 = (f32[128,2048]{1,0:T(8,128)S(1)}, f32[128,2048]{1,0:T(8,128)S(1)}, u32[]{:S(2)}, u32[]{:S(2)}) collective-permute-start(f32[128,2048]{1,0:T(8,128)S(1)} %get-tuple-element.98), channel_id=1, source_target_pairs={{1,0},{4,1},{5,4},{8,5},{9,8},{12,9},{13,12},{16,13},{17,16},{20,1... | collective-permute-start | bytes 3145736 | tf_op jit(solution)/shard_map/ppermute | solution.py:767
  142.5 45.0 %collective-permute-start.15 = (bf16[256,2048]{1,0:T(8,128)(2,1)}, bf16[256,2048]{1,0:T(8,128)(2,1)S(1)}, u32[]{:S(2)}, u32[]{:S(2)}) collective-permute-start(bf16[256,2048]{1,0:T(8,128)(2,1)} %get-tuple-element.102), channel_id=1, source_target_pairs={{0,2},{2,0},{1,3},{3,1},{4,6},{6,4},{5,7},{7,5},{8,10},{10,8},{9,1... | collective-permute-start | bytes 3145736 | tf_op jit(solution)/shard_map/ppermute | solution.py:858

commit v3 on v2

--- a/solution.py
+++ b/solution.py
@@ -16,7 +16,9 @@
 NEG = -1e30
 WINDOW = 3
 PER_STATS = 8
+PER_LAST = 16
 PER_GRADIENTS = 8
+UNROLL = 4
 ROWS = ("seq", "section")
 NT = (((1,), (1,)), ((), ()))
 TN = (((0,), (0,)), ((), ()))
@@ -55,7 +57,7 @@
 
 
 class Weights:
-    def __init__(self, key_weight, by_columns, group):
+    def __init__(self, key_weight, by_columns, group, span=None):
         rows, columns = key_weight.shape
         self.features = rows // group
         self.by_columns = by_columns
@@ -64,9 +66,11 @@
             self.steps = columns // self.step
             self.block = (self.features, self.step)
         else:
-            self.step = min(256, self.features)
+            self.step = min(256, max(self.features // 4, BLOCK))
             self.steps = self.features // self.step
             self.block = (self.step, columns)
+        self.first, last = span or (0, self.steps)
+        self.steps = last - self.first
 
     def buffer_shape(self, count):
         return (count, 2, self.steps) + self.block
@@ -80,9 +84,11 @@
     def copy(self, refs, buffer, sems, owner, at, which, step):
         if self.by_columns:
             first = pl.multiple_of(owner * self.features, self.features)
-            source = refs[which].at[pl.ds(first, self.features), lanes_at(step, self.step)]
+            source = refs[which].at[
+                pl.ds(first, self.features), lanes_at(step + self.first, self.step)
+            ]
         else:
-            first = pl.multiple_of(owner * self.features + step * self.step, self.step)
+            first = pl.multiple_of(owner * self.features + (step + self.first) * self.step, self.step)
             source = refs[which].at[pl.ds(first, self.step), :]
         return pltpu.make_async_copy(
             source, buffer.at[at, which, step], sems.at[at, which, step]
@@ -120,19 +126,20 @@
     return [lax.rem(me + k, group) for k in range(group)]
 
 
-def take_rows(states, cuts):
+def take_parts(states, cuts):
     def body(states_ref, *refs):
         outs, sems = refs[:-1], refs[-1]
         copies = []
-        for i, (first, last) in enumerate(cuts):
-            copies.append(
-                pltpu.make_async_copy(states_ref.at[pl.ds(first, last - first), :], outs[i], sems.at[i])
-            )
+        for i, (first, last, left, right) in enumerate(cuts):
+            part = states_ref.at[pl.ds(first, last - first), pl.ds(left, right - left)]
+            copies.append(pltpu.make_async_copy(part, outs[i], sems.at[i]))
             copies[-1].start()
         for copy in copies:
             copy.wait()
 
-    shapes = [jax.ShapeDtypeStruct((last - first, states.shape[1]), BF16) for first, last in cuts]
+    shapes = [
+        jax.ShapeDtypeStruct((last - first, right - left), BF16) for first, last, left, right in cuts
+    ]
     return call(
         body,
         [ANYWHERE],
@@ -208,23 +215,31 @@
     return [(out[2 * i], out[2 * i + 1]) for i in range(count)]
 
 
-def project_rest(partial, arrived, key_weight, value_weight, held, group, base=0, height=None, into=None):
+def project_rest(
+    partial, arrived, key_weight, value_weight, held, group, left=0, final=True, away=None, base=0, height=None, into=None
+):
     rows, columns = partial[0].shape
     height = height or rows
     earlier = [] if into is None else list(into)
     depth = arrived[0].shape[1]
     count = len(arrived)
     weights = Weights(key_weight, True, group)
+    later = Weights(key_weight, False, group, away) if away else None
     loads = held is None
+    used = [key_weight, value_weight] if loads or away else []
 
     def body(key_part, value_part, *refs):
         pieces, refs = refs[:count], refs[count + len(earlier) :]
+        both, refs = refs[: len(used)], refs[len(used) :]
+        owners = sources(group)[1:]
+        others = targets(group)[1:]
         if loads:
-            both, outs, (buffer, sems) = refs[:2], refs[2:4], refs[4:]
-            owners = sources(group)[1:]
+            outs, (buffer, sems) = refs[:2], refs[2:]
             weights.start(both, buffer, sems, owners, WINDOW)
         else:
-            buffer, outs = refs[0], refs[1:]
+            buffer, outs, rest = refs[0], refs[1:3], refs[3:]
+        if away:
+            later.start(both, *rest, others)
 
         def step(j, carry):
             if loads:
@@ -234,27 +249,43 @@
                 total = part_ref[:, here]
                 for at in range(count):
                     total = total + jnp.dot(
-                        pieces[at][...], buffer[at, which, j], preferred_element_type=F32
+                        pieces[at][...],
+                        buffer[at, which, j, left : left + depth, :],
+                        preferred_element_type=F32,
                     )
-                outs[which][base : base + rows, here] = total.astype(BF16)
+                outs[which][base : base + rows, here] = total.astype(outs[which].dtype)
             return carry
 
-        lax.fori_loop(0, weights.steps, step, 0)
-
-    shapes = [jax.ShapeDtypeStruct((height, columns), BF16)] * 2
+        lax.fori_loop(0, weights.steps, step, 0, unroll=1 if loads or rows > BLOCK else UNROLL)
+        if away:
+            for j in range(later.steps):
+                later.wait(both, *rest, others, j)
+
+    shapes = [jax.ShapeDtypeStruct((height, columns), BF16 if final else F32)] * 2
     if loads:
         shapes.append(jax.ShapeDtypeStruct(weights.buffer_shape(count), BF16))
+    if away:
+        shapes.append(jax.ShapeDtypeStruct(later.buffer_shape(count), BF16))
+    semaphores = [weights.semaphores(count)] if loads else [later.semaphores(count)] if away else []
+    aliases = {2 + count + i: i for i in range(len(earlier))} if final else {0: 0, 1: 1}
     out = call(
         body,
-        [HERE] * (2 + count + len(earlier)) + ([ANYWHERE] * 2 if loads else [HERE]),
+        [HERE] * (2 + count + len(earlier)) + [ANYWHERE] * len(used) + [HERE] * (0 if loads else 1),
         [HERE] * len(shapes),
         shapes,
-        [weights.semaphores(count)] if loads else [],
+        semaphores,
         4 * rows * depth * columns * count,
         4 * depth * columns * count if loads else 2 * rows * columns,
-        {2 + count + i: i for i in range(len(earlier))},
-    )(*partial, *arrived, *earlier, *((key_weight, value_weight) if loads else (held,)))
-    return (out[0], out[1]), (out[2] if loads else held)
+        aliases,
+    )(*partial, *arrived, *earlier, *used, *(() if loads else (held,)))
+    return (out[0], out[1]), out[2] if loads or away else None
+
+
+def away_spans(key_weight, group):
+    total = Weights(key_weight, False, group).steps
+    first = total // 4
+    second = first + (total - first) // 2
+    return [(0, first), (first, second), (second, total)]
 
 
 def certain(token, frame):
@@ -401,7 +432,7 @@
     own_count = queries.shape[0] // BLOCK
     columns = queries.shape[1]
     heads = columns // DH
-    per = min(PER_STATS, heads)
+    per = min(PER_LAST if send and earlier is not None and keep else PER_STATS, heads)
     depth = stat_depth(own_count)
     count = len(kvs)
     halo = any(t < 0 or t >= own_count for tiles in tiles_list for t in tiles.touched)
@@ -464,11 +495,23 @@
     )(*band, *shared, *flat, *extra)
 
 
-def term_block(buffer, at, step, key_ref, value_ref, rows, out_ref):
+def term_block(buffer, at, step, key_ref, value_ref, rows, out_ref, place):
     term = lax.dot_general(
         key_ref[rows, :], buffer[at, 0, step], NT, preferred_element_type=F32
     ) + lax.dot_general(value_ref[rows, :], buffer[at, 1, step], NT, preferred_element_type=F32)
-    out_ref[:, lanes_at(step, buffer.shape[3])] = term.astype(BF16)
+    out_ref[:, lanes_at(place, buffer.shape[3])] = term.astype(BF16)
+
+
+def terms_of(buffer, begin, end, key_ref, value_ref, rows, outs, offset, before=None):
+    def step(j, carry):
+        if before is not None:
+            before(j)
+        for at, out_ref in enumerate(outs):
+            term_block(buffer, at, j, key_ref, value_ref, rows, out_ref, j - begin + offset)
+        return carry
+
+    lax.fori_loop(begin, end, step, 0)
+    return offset + end - begin
 
 
 def gradients(
@@ -481,12 +524,13 @@
     above,
     stats,
     swaps,
-    key_weight,
-    value_weight,
     held,
     deferred,
     kept,
     totals,
+    load,
+    key_weight,
+    value_weight,
     rate,
     scale,
     group,
@@ -499,16 +543,15 @@
     touched = tiles.touched
     halo_touched = [t for t in touched if not 0 <= t < own_count]
     shared = (queries, grads) + ((below, above) if halo_touched else ())
-    weights = Weights(key_weight, False, group)
-    steps, features = weights.steps, weights.features
-    loads = held is None
-    sources_in = [key_weight, value_weight] if loads else [held]
+    features = sum(buffer.shape[2] for buffer in held) * held[0].shape[3]
+    features += held[0].shape[3] if load else 0
+    later = Weights(key_weight, False, group, load) if load else None
+    used = [key_weight, value_weight] if load else []
     defer = not halo_touched
     extra = [] if defer else list(deferred)
     known = [array for _, *arrays in kept for array in arrays]
     earlier = [] if totals is None else list(totals)
     base = tiles.first * BLOCK
-    ahead = min(4, weights.steps)
 
     def body(*refs):
         bands, refs = Bands(refs[:3], own_count), refs[3:]
@@ -516,15 +559,14 @@
         refs = refs[len(shared) :]
         key_ref, value_ref, stat_ref = refs[:3]
         swap_refs, refs = refs[3 : 3 + len(swaps)], refs[3 + len(swaps) :]
-        both, refs = refs[: len(sources_in)], refs[len(sources_in) :]
+        buffers, refs = refs[: len(held)], refs[len(held) :]
+        both, refs = refs[: len(used)], refs[len(used) :]
         extra_refs, refs = refs[: len(extra)], refs[len(extra) :]
         known_refs, refs = refs[: len(known)], refs[len(known) + len(earlier) :]
-        if loads:
-            buffer, sems, refs = refs[-2], refs[-1], refs[:-2]
+        if load:
+            *refs, held_out, sems = refs
             owners = targets(group)[1:]
-            weights.start(both, buffer, sems, owners, ahead)
-        else:
-            buffer = both[0]
+            later.start(both, held_out, sems, owners)
         key_out, value_out, own_out = refs[:3]
         term_outs = refs[3 : 2 + group]
         halo_outs = refs[2 + group :]
@@ -608,33 +650,18 @@
         def step(pair, carry):
             for k in range(per):
                 one(pair * per + k)
-            if loads:
-
-                @pl.when(pair + ahead < steps)
-                def _():
-                    weights.wait(both, buffer, sems, owners, pair)
-                    weights.start_step(both, buffer, sems, owners, pair + ahead)
-
             return carry
 
         lax.fori_loop(0, heads // per, step, 0)
-        done = min(heads // per, steps - ahead)
-        if loads:
-            for j in range(done + ahead, steps):
-                weights.start_step(both, buffer, sems, owners, j)
-
-        def term_step(j, carry):
-            if loads:
-
-                @pl.when(j >= done)
-                def _():
-                    weights.wait(both, buffer, sems, owners, j)
-
-            for at, out_ref in enumerate(term_outs):
-                term_block(buffer, at, j, key_out, value_out, slice(base, base + frames), out_ref)
-            return carry
-
-        lax.fori_loop(0, steps, term_step, 0)
+
+        place, rows = 0, slice(base, base + frames)
+        for buffer in buffers:
+            place = terms_of(buffer, 0, buffer.shape[2], key_out, value_out, rows, term_outs, place)
+        if load:
+            later.wait(both, held_out, sems, owners, 0)
+            terms_of(held_out, 0, 1, key_out, value_out, rows, term_outs, place)
+            for j in range(1, later.steps):
+                later.wait(both, held_out, sems, owners, j)
 
     shapes = (
         [jax.ShapeDtypeStruct((RATIO * own_count * BLOCK, columns), BF16)] * 2
@@ -645,26 +672,57 @@
         ]
         + [jax.ShapeDtypeStruct((frames, features), BF16)] * (group - 1)
         + [jax.ShapeDtypeStruct((BLOCK, columns), F32)] * len(halo_touched)
-        + ([jax.ShapeDtypeStruct(weights.buffer_shape(group - 1), BF16)] if loads else [])
+        + ([jax.ShapeDtypeStruct(later.buffer_shape(group - 1), BF16)] if load else [])
     )
     out = call(
         body,
         [SCALARS] * 3
         + [HERE] * (len(shared) + 3 + len(swaps))
-        + ([ANYWHERE] * 2 if loads else [HERE])
+        + [HERE] * len(held)
+        + [ANYWHERE] * len(used)
         + [HERE] * (len(extra) + len(known) + len(earlier)),
         [HERE] * len(shapes),
         shapes,
-        [weights.semaphores(group - 1)] if loads else [],
+        [later.semaphores(group - 1)] if load else [],
         20 * frames * 2 * BLOCK * columns + 4 * frames * columns * features * (group - 1),
         8 * frames * columns,
         {
-            6 + len(swaps) + len(shared) + len(sources_in) + len(extra) + len(known) + i: i
+            6 + len(held) + len(used) + len(swaps) + len(shared) + len(extra) + len(known) + i: i
             for i in range(len(earlier))
         },
-    )(*band, *shared, *kv, stats, *swaps, *sources_in, *extra, *known, *earlier)
+    )(*band, *shared, *kv, stats, *swaps, *held, *used, *extra, *known, *earlier)
     halo = dict(zip(halo_touched, out[2 + group :]))
-    return out[:2], out[2], out[3 : 2 + group], halo, out[-1] if loads else held
+    return out[:2], out[2], out[3 : 2 + group], halo, out[-1] if load else None
+
+
+def more_terms(totals, first, frames, held, span, key_weight, value_weight, group):
+    columns = totals[0].shape[1]
+    later = Weights(key_weight, False, group, span)
+    features = (held.shape[2] - 1 + later.steps) * later.step
+    shapes = [jax.ShapeDtypeStruct((frames, features), BF16)] * (group - 1)
+    shapes.append(jax.ShapeDtypeStruct(later.buffer_shape(group - 1), BF16))
+
+    def body(key_ref, value_ref, buffer, key_weight_ref, value_weight_ref, *refs):
+        *outs, held_out, sems = refs
+        both, owners = (key_weight_ref, value_weight_ref), targets(group)[1:]
+        later.start(both, held_out, sems, owners)
+        rows = slice(first, first + frames)
+
+        def before(j):
+            later.wait(both, held_out, sems, owners, j)
+
+        place = terms_of(buffer, 1, held.shape[2], key_ref, value_ref, rows, outs, 0)
+        terms_of(held_out, 0, later.steps, key_ref, value_ref, rows, outs, place, before)
+
+    return call(
+        body,
+        [HERE] * 3 + [ANYWHERE] * 2,
+        [HERE] * len(shapes),
+        shapes,
+        [later.semaphores(group - 1)],
+        4 * frames * columns * features * (group - 1),
+        4 * frames * columns,
+    )(*totals, held, key_weight, value_weight)
 
 
 def own_terms(totals, key_weight, value_weight, group):
@@ -678,7 +736,7 @@
 
         def step(j, carry):
             weights.advance(both, buffer, sems, owners, j)
-            term_block(buffer, 0, j, key_grad_ref, value_grad_ref, slice(0, rows), out_ref)
+            term_block(buffer, 0, j, key_grad_ref, value_grad_ref, slice(0, rows), out_ref, j)
             return carry
 
         lax.fori_loop(0, weights.steps, step, 0)
@@ -725,40 +783,52 @@
     )(low, high, from_below, from_above)
 
 
-def add_rows(target, own, arrived, first):
-    rows, features = arrived[0].shape
+def add_rows(target, own, arrived):
+    features = own.shape[1]
     tall = BLOCK // 2
-    steps = rows // tall
-    count = len(arrived)
+    flat = [array for _, turns in arrived for turn in turns for array in turn]
+    sizes = [turns[0][0].shape[0] // tall for _, turns in arrived]
 
     def body(own_ref, *refs):
-        terms = refs[:count]
         out_ref, buffer, sems = refs[-3:]
         copies = []
-        for i in range(steps):
-            value = own_ref[first + i * tall : first + (i + 1) * tall, :].astype(F32)
-            for ref in terms:
-                value = value + ref[i * tall : (i + 1) * tall, :].astype(F32)
-            buffer[i] = value.astype(BF16)
-            copy = pltpu.make_async_copy(
-                buffer.at[i], out_ref.at[pl.ds(first + i * tall, tall), :], sems.at[i]
-            )
-            copy.start()
-            copies.append(copy)
+        at = slot = 0
+        for (first, turns), steps in zip(arrived, sizes):
+            terms = []
+            for turn in turns:
+                terms.append(refs[at : at + len(turn)])
+                at += len(turn)
+            for i in range(steps):
+                rows = slice(first + i * tall, first + (i + 1) * tall)
+                left = 0
+                for side in range(len(turns[0])):
+                    right = left + terms[0][side].shape[1]
+                    value = own_ref[rows, left:right].astype(F32)
+                    for turn in terms:
+                        value = value + turn[side][i * tall : (i + 1) * tall, :].astype(F32)
+                    buffer[slot, :, left:right] = value.astype(BF16)
+                    left = right
+                copy = pltpu.make_async_copy(
+                    buffer.at[slot], out_ref.at[pl.ds(first + i * tall, tall), :], sems.at[slot]
+                )
+                copy.start()
+                copies.append(copy)
+                slot += 1
         for copy in copies:
             copy.wait()
 
     extra = [] if target is None else [target]
+    slots = sum(sizes)
     return call(
         body,
-        [HERE] * (1 + count) + [ANYWHERE] * len(extra),
+        [HERE] * (1 + len(flat)) + [ANYWHERE] * len(extra),
         ANYWHERE,
         pltpu.HBM(own.shape, own.dtype),
-        [pltpu.VMEM((steps, tall, features), BF16), pltpu.SemaphoreType.DMA((steps,))],
-        rows * features * count,
-        2 * rows * features * (count + 2),
-        {1 + count: 0} if extra else None,
-    )(own, *arrived, *extra)
+        [pltpu.VMEM((slots, tall, features), BF16), pltpu.SemaphoreType.DMA((slots,))],
+        slots * tall * features,
+        6 * slots * tall * features,
+        {1 + len(flat): 0} if extra else None,
+    )(own, *flat, *extra)
 
 
 def shifted(value, steps):
@@ -791,8 +861,12 @@
     key_weight, value_weight = [
         pltpu.with_memory_space_constraint(w, pltpu.HBM) for w in (key_weight, value_weight)
     ]
+    depth = encoder_states.shape[1]
+    split = max(depth // 2 // BLOCK, 1) * BLOCK
+    parts = [(first, last, 0, depth) for first, last in row_cuts[:-1]]
+    parts += [(*row_cuts[-1], 0, split), (*row_cuts[-1], split, depth)]
     arrived = []
-    for rows in take_rows(encoder_states, row_cuts[:1]) + take_rows(encoder_states, row_cuts[1:]):
+    for rows in take_parts(encoder_states, parts[:1]) + take_parts(encoder_states, parts[1:]):
         arrived.append([lax.ppermute(rows, "tensor", turn) for turn in turns])
 
     edge_up, edge_down = take_edges(queries, out_grad)
@@ -802,8 +876,8 @@
 
     partial = project_own(encoder_states, key_weight, value_weight, row_cuts, group)
 
-    def rest(i, held, **place):
-        return project_rest(partial[i], arrived[i], key_weight, value_weight, held, group, **place)
+    def rest(i, part, held, **place):
+        return project_rest(part, arrived[i], key_weight, value_weight, held, group, **place)
 
     def statistics(*where, **what):
         return row_stats(band, *where, queries, out_grad, below, above, *what.values(), rate)
@@ -814,16 +888,20 @@
     low_tiles, high_tiles = [Tiles(own_count, first, last, True) for first, last in cuts[:2]]
     inner = [Tiles(own_count, first, last, False, edge) for first, last in cuts[2:]]
     inner_tiles = Tiles(own_count, edge, frame_blocks - edge, False)
-    low_kv, held = rest(0, None)
+    low_kv, held = rest(0, partial[0], None)
     (stats,) = statistics([low_tiles], [low_kv], earlier=None, send=None, keep=False)
-    high_kv, held = rest(1, held)
+    high_kv, _ = rest(1, partial[1], held)
     stats, *outer = statistics([high_tiles], [high_kv], earlier=stats, send=(own_count, -1), keep=False)
     early = exchange(outer)
     height = (frame_blocks - 2 * edge) * BLOCK
-    kv, held = rest(2, held, height=height)
+    kv, _ = rest(2, partial[2], held, height=height)
     stats, *first_kept = statistics(inner[:1], [kv], earlier=stats, send=None, keep=True)
     kv, stats = lax.optimization_barrier((kv, stats))
-    inner_kv, held = rest(3, held, base=(middle - edge) * BLOCK, height=height, into=kv)
+    spans = away_spans(key_weight, group)
+    part, first_held = rest(3, partial[3], held, final=False, away=spans[0])
+    inner_kv, _ = rest(
+        4, part, held, left=split, base=(middle - edge) * BLOCK, height=height, into=kv
+    )
     stats, first_own, second_own, *second_kept = statistics(
         inner[1:], [inner_kv], earlier=stats, send=(own_count - 1, 0), keep=True
     )
@@ -833,7 +911,9 @@
     chunks = [(inner_tiles, inner_kv), (low_tiles, low_kv), (high_tiles, high_kv)]
     shared = (queries, out_grad, below, above, stats)
     out, sent = [], []
-    totals = away = deferred = None
+    totals = None
+    deferred = ()
+    away = [first_held]
     for i, (tiles, kv) in enumerate(chunks):
         out.append(
             gradients(
@@ -842,29 +922,44 @@
                 kv,
                 *shared,
                 early + late if i else early,
-                key_weight,
-                value_weight,
                 away,
                 deferred,
                 () if i else kept,
                 totals,
+                None if i else spans[1],
+                key_weight,
+                value_weight,
                 rate,
                 scale,
                 group,
             )
         )
-        totals, away = out[i][0], out[i][4]
+        totals = out[i][0]
         deferred = (inner_kv[0], out[0][1]) if i == 1 else ()
-        sent.append([lax.ppermute(term, "tensor", turn) for term, turn in zip(out[i][2], turns)])
+        sent.append([[lax.ppermute(term, "tensor", turn)] for term, turn in zip(out[i][2], turns)])
+        if i == 0:
+            *more, last_held = more_terms(
+                totals,
+                tiles.first * BLOCK,
+                kv[0].shape[0],
+                out[0][4],
+                spans[2],
+                key_weight,
+                value_weight,
+                group,
+            )
+            away = [first_held, out[0][4], last_held]
+            for turn_sent, term, turn in zip(sent[0], more, turns):
+                turn_sent.append(lax.ppermute(term, "tensor", turn))
 
     from_below = shifted(out[2][3][own_count], 1)
     from_above = shifted(out[1][3][-1], -1)
     own = own_terms(totals, key_weight, value_weight, group)
     query_grad = finish_queries(out[1][1], out[2][1], from_below, from_above)
 
-    encoder_grad = None
-    for i, (tiles, _) in enumerate(chunks):
-        encoder_grad = add_rows(encoder_grad, own, sent[i], tiles.first * BLOCK)
+    back = [(tiles.first * BLOCK, turns_sent) for (tiles, _), turns_sent in zip(chunks, sent)]
+    encoder_grad = add_rows(None, own, back[:-1])
+    encoder_grad = add_rows(encoder_grad, own, back[-1:])
     return (query_grad, encoder_grad)
 
 

time: 191 us -> 184 us (0.963)
  Pallas kernels: 115 us -> 110 us
  starting transfers between devices: 32.3 us -> 30.1 us
    pallas_call x12 -> x13, Pallas kernels: 67.7 us -> 63.7 us  [the longest x3 34.2 us: gradients(): call(body, [SCALARS] * 3 + [HERE] * (len(shared) + 3 + len(swaps)) + [HER...]
    ppermute x4, starting transfers between devices: 6.58 us -> 2.87 us  [swapped(): return lax.ppermute(value, ROWS, pairs)]
    ppermute x4 -> x5, starting transfers between devices: 7.86 us -> 6.55 us  [on_device(): arrived.append([lax.ppermute(rows, 'tensor', turn) for turn in turns])]
    ppermute x4 -> x5, waiting for transfers between devices: 13.7 us -> 13.8 us  [on_device(): arrived.append([lax.ppermute(rows, 'tensor', turn) for turn in turns])]
  transfers between devices with their start and end apart: 17 -> 19, of which waited for: 4 -> 3; matrix products, arithmetic and copies ran while one was open for 0% -> 0% of each run, Pallas kernels for 59% -> 59%
where the time goes in v3:
time: 184 us
  Pallas kernels  110 us (60%)
  waiting for transfers between devices  42.2 us (23%)
  starting transfers between devices  30.1 us (16%)
    pallas_call x3, Pallas kernels, gradients(): call(body, [SCALARS] * 3 + [HERE] * (len(shared) + 3 + len(swaps)) + [HER...  34.2 us
    ppermute x3, waiting for transfers between devices, on_device(): lax.ppermute(term, 'tensor', turn)  28.4 us
    pallas_call x5, Pallas kernels, project_rest(): call(body, [HERE] * (2 + count + len(earlier)) + [ANYWHERE] * len(used) +...  20.2 us
    pallas_call x1, Pallas kernels, own_terms(): call(body, [HERE] * 2 + [ANYWHERE] * 2, HERE, jax.ShapeDtypeStruct((rows,...  16.3 us
    ppermute x6, starting transfers between devices, shifted(): lax.ppermute(value, ROWS, [(source, source + steps) for source in range(f...  16.2 us
    pallas_call x1, Pallas kernels, project_own(): call(body, [HERE] + [ANYWHERE] * 2, [HERE] * len(shapes), shapes, [weight...  16.1 us
    ppermute x5, waiting for transfers between devices, on_device(): arrived.append([lax.ppermute(rows, 'tensor', turn) for turn in turns])  13.8 us
    pallas_call x4, Pallas kernels, row_stats(): call(body, [SCALARS] * 3 + [HERE] * len(shared) + [HERE] * (len(flat) + l...  11.6 us
  transfers between devices with their start and end apart: 19, of which 3 were waited for; matrix products, arithmetic and copies ran while one was open for 0% of the time, Pallas kernels for 59%

profile of v3, /device:TPU:0, one launch (start us, length us, event | category | flops | bytes accessed | tf_op | source)
XLA Modules:
  0.0 183.9 jit_solution(9562583383597671937)
XLA Ops:
  0.6 1.3 collective-permute-start.1
  1.9 1.2 shard_map.79
  3.2 0.0 copy-start.6
  3.2 3.0 %collective-permute-start.4 = (bf16[256,2048]{1,0:T(8,128)(2,1)S(1)}, bf16[256,2048]{1,0:T(8,128)(2,1)S(1)}, u32[]{:S(2)}, u32[]{:S(2)}) collective-permute-start(bf16[256,2048]{1,0:T(8,128)(2,1)S(1)} %shard_map.79), channel_id=1, source_target_pairs={{0,2},{2,0},{1,3},{3,1},{4,6},{6,4},{5,7},{7,5},{8,10},{10,8},{9,1... | collective-permute-start | bytes 3145736 | tf_op jit(solution)/shard_map/ppermute | solution.py:870
  6.2 1.5 shard_map.81
  7.8 0.2 collective-permute-start.8
  8.0 1.5 shard_map.77
  9.5 2.8 %collective-permute-start.2 = (bf16[128,4096]{1,0:T(8,128)(2,1)S(1)}, bf16[128,4096]{1,0:T(8,128)(2,1)S(1)}, u32[]{:S(2)}, u32[]{:S(2)}) collective-permute-start(bf16[128,4096]{1,0:T(8,128)(2,1)S(1)} %get-tuple-element.59), channel_id=1, source_target_pairs={{0,1},{1,4},{4,5},{5,8},{8,9},{9,12},{12,13},{13,16},{16,17},{17,2... | collective-permute-start | bytes 3145736 | tf_op jit(solution)/shard_map/ppermute | solution.py:837
  12.4 0.0 copy-start.13
  12.4 1.3 collective-permute-start.3
  13.7 16.1 %shard_map.78 = (f32[256,2048]{1,0:T(8,128)S(1)}, f32[256,2048]{1,0:T(8,128)S(1)}, f32[256,2048]{1,0:T(8,128)S(1)}, f32[256,2048]{1,0:T(8,128)S(1)}, f32[128,204...) custom-call(bf16[768,2048]{1,0:T(8,128)(2,1)S(1)} %copy-done.6, ...), custom_call_target="tpu_custom_call" | custom-call | flops 12884901888 | bytes 19922944 | tf_op jit(solution)/shard_map/pallas_call | solution.py:206
  29.8 0.0 collective-permute-done.4.refs_0_
  29.8 0.0 copy-done.13
  29.8 4.5 %collective-permute-start = (s32[2,2]{1,0:T(2,128)S(1)}, s32[2,2]{1,0:T(2,128)S(1)}, u32[]{:S(2)}, u32[]{:S(2)}) collective-permute-start(s32[2,2]{1,0:T(2,128)S(1)} %copy-done.13), channel_id=1, source_target_pairs={{0,1},{1,4},{4,5},{5,8},{8,9},{9,12},{12,13},{13,16},{16,17},{17,2... | collective-permute-start | bytes 56 | tf_op jit(solution)/shard_map/ppermute | solution.py:837
  34.3 0.0 copy-start
  34.4 0.0 copy-start.1
  34.4 8.1 %shard_map.80 = (bf16[256,2048]{1,0:T(8,128)(2,1)S(1)}, bf16[256,2048]{1,0:T(8,128)(2,1)S(1)}, bf16[1,2,8,2048,256]{4,3,2,1,0:T(8,128)(2,1)S(1)}) custom-call(f32[256,2048]{1,0:T(8,128)S(1)} %get-tuple-element.61.key_part, f32[256,2048]{1,0:T(8,128)S(1)} %get-tuple-element.62.value_part, bf16[256,2048]{1,0:T(8,128)(2,1)S(1)} %collective-permute-done.4.refs_0_, ...), custom_call_target="tpu_custom_call" | custom-call | flops 4294967296 | bytes 16777216 | tf_op jit(solution)/shard_map/pallas_call | solution.py:271
  42.5 0.0 collective-permute-done.1.refs_2_
  42.5 1.3 collective-permute-start.5
  43.7 0.0 collective-permute-done.refs_0_
  43.7 0.8 collective-permute-start.6
  44.6 0.0 collective-permute-done.2.refs_5_
  44.6 1.2 collective-permute-start.7
  45.8 0.0 collective-permute-done.3.refs_6_
  45.8 3.7 %shard_map.85.refs_9_ = f32[16,16,128]{2,1,0:T(8,128)S(1)} custom-call(s32[2,2]{1,0:T(2,128)S(1)} %collective-permute-done.refs_0_, s32[2,2]{1,0:T(2,128)S(1)} %copy-done.13, s32[2,2]{1,0:T(2,128)S(1)} %collective-permute-done.1.refs_2_, bf16[256,2048]{1,0:T(8,128)(2,1)S(1)} %copy-done, bf16[256,2048]{1,0:T(8,128)(2,1)S(1)} %copy-done.1, ...), custom_call_target="tpu_custom_call" | custom-call | flops 1073741824 | bytes 6291456 | tf_op jit(solution)/shard_map/pallas_call | solution.py:485
  49.5 2.8 %collective-permute-done.8.refs_0_ = bf16[256,2048]{1,0:T(8,128)(2,1)S(1)} collective-permute-done((bf16[256,2048]{1,0:T(8,128)(2,1)S(1)}, bf16[256,2048]{1,0:T(8,128)(2,1)S(1)}, u32[]{:S(2)}, u32[]{:S(2)}) %collective-permute-start.8) | collective-permute-done | bytes 1048608 | tf_op jit(solution)/shard_map/ppermute | solution.py:870
  52.3 5.7 %shard_map.84 = (bf16[256,2048]{1,0:T(8,128)(2,1)S(1)}, bf16[256,2048]{1,0:T(8,128)(2,1)S(1)}) custom-call(f32[256,2048]{1,0:T(8,128)S(1)} %get-tuple-element.77.key_part, f32[256,2048]{1,0:T(8,128)S(1)} %get-tuple-element.78.value_part, bf16[256,2048]{1,0:T(8,128)(2,1)S(1)} %collective-permute-done.8.refs_0_, ...), custom_call_target="tpu_custom_call" | custom-call | flops 4294967296 | bytes 1048576 | tf_op jit(solution)/shard_map/pallas_call | solution.py:271
  58.0 4.0 %shard_map.86 = (f32[16,16,128]{2,1,0:T(8,128)S(1)}, f32[16,8,128]{2,1,0:T(8,128)S(1)}, f32[16,8,128]{2,1,0:T(8,128)S(1)}) custom-call(s32[2,2]{1,0:T(2,128)S(1)} %collective-permute-done.refs_0_, s32[2,2]{1,0:T(2,128)S(1)} %copy-done.13, s32[2,2]{1,0:T(2,128)S(1)} %collective-permute-done.1.refs_2_, bf16[256,2048]{1,0:T(8,128)(2,1)S(1)} %copy-done, ...), custom_call_target="tpu_custom_call" | custom-call | flops 1073741824 | bytes 6291456 | tf_op jit(solution)/shard_map/pallas_call | solution.py:485
  62.1 1.1 collective-permute-start.9
  63.1 0.7 collective-permute-start.10
  63.8 11.0 %collective-permute-done.7.refs_0_ = bf16[128,2048]{1,0:T(8,128)(2,1)S(1)} collective-permute-done((bf16[128,2048]{1,0:T(8,128)(2,1)S(1)}, bf16[128,2048]{1,0:T(8,128)(2,1)S(1)}, u32[]{:S(2)}, u32[]{:S(2)}) %collective-permute-start.7) | collective-permute-done | bytes 524320 | tf_op jit(solution)/shard_map/ppermute | solution.py:870
  74.7 2.7 %shard_map.83 = (bf16[256,2048]{1,0:T(8,128)(2,1)S(1)}, bf16[256,2048]{1,0:T(8,128)(2,1)S(1)}) custom-call(f32[128,2048]{1,0:T(8,128)S(1)} %get-tuple-element.72.key_part, f32[128,2048]{1,0:T(8,128)S(1)} %get-tuple-element.73.value_part, bf16[128,2048]{1,0:T(8,128)(2,1)S(1)} %collective-permute-done.7.refs_0_, ...), custom_call_target="tpu_custom_call" | custom-call | flops 2147483648 | bytes 524288 | tf_op jit(solution)/shard_map/pallas_call | solution.py:271
  77.4 2.1 %shard_map.87 = (f32[16,16,128]{2,1,0:T(8,128)S(1)}, f32[16,128,256]{2,1,0:T(8,128)S(1)}, f32[16,128,256]{2,1,0:T(8,128)S(1)}) custom-call(s32[2,2]{1,0:T(2,128)S(1)} %collective-permute-done.refs_0_, s32[2,2]{1,0:T(2,128)S(1)} %copy-done.13, s32[2,2]{1,0:T(2,128)S(1)} %collective-permute-done.1.refs_2_, bf16[256,2048]{1,0:T(8,128)(2,1)S(1)} %copy-done, ...), custom_call_target="tpu_custom_call" | custom-call | flops 1073741824 | bytes 6291456 | tf_op jit(solution)/shard_map/pallas_call | solution.py:485
  79.5 0.0 collective-permute-done.5.refs_0_
  79.5 2.2 %shard_map.82 = (f32[128,2048]{1,0:T(8,128)S(1)}, f32[128,2048]{1,0:T(8,128)S(1)}, bf16[1,2,2,256,2048]{4,3,2,1,0:T(8,128)(2,1)S(1)}) custom-call(f32[128,2048]{1,0:T(8,128)S(1)} %get-tuple-element.65.key_part, f32[128,2048]{1,0:T(8,128)S(1)} %get-tuple-element.66.value_part, ...), custom_call_target="tpu_custom_call", output_to_operand_aliasing={{0}: (0, {}), {1}: (1, {})} | custom-call | flops 1073741824 | bytes 524288 | tf_op jit(solution)/shard_map/pallas_call | solution.py:271
  81.8 0.0 collective-permute-done.6.refs_0_
  81.8 1.5 shard_map.88
  83.3 1.8 shard_map.89
  85.1 0.3 collective-permute-start.11
  85.4 0.8 collective-permute-start.12
  86.3 0.0 collective-permute-done.9.refs_8_.refs_10_
  86.3 0.0 collective-permute-done.10.refs_9_.refs_11_
  86.3 4.8 %shard_map.90 = (bf16[768,2048]{1,0:T(8,128)(2,1)S(1)}, bf16[768,2048]{1,0:T(8,128)(2,1)S(1)}, bf16[16,256,256]{2,1,0:T(8,128)(2,1)S(1)}, bf16[256,768]{1,0:T(8,128)(2,1)S(1)}, bf16[1,2,3,256,2048]{4,3,2,1,0:T(8,128)(2,1)S(1)}) custom-call(s32[2,2]{1,0:T(2,128)S(1)} %collective-permute-done.refs_0_, s32[2,2]{1,0:T(2,128)S(1)} %copy-done.13, ...), custom_call_target="tpu_custom_call" | custom-call | flops 4294967296 | bytes 4194304 | tf_op jit(solution)/shard_map/pallas_call | solution.py:677
  91.1 2.2 %collective-permute-start.16 = (bf16[256,768]{1,0:T(8,128)(2,1)S(1)}, bf16[256,768]{1,0:T(8,128)(2,1)S(1)}, u32[]{:S(2)}, u32[]{:S(2)}) collective-permute-start(bf16[256,768]{1,0:T(8,128)(2,1)S(1)} %get-tuple-element.113), channel_id=1, source_target_pairs={{0,2},{2,0},{1,3},{3,1},{4,6},{6,4},{5,7},{7,5},{8,10},{10,8},{9,1... | collective-permute-start | bytes 1179656 | tf_op jit(solution)/shard_map/ppermute | solution.py:939
  93.3 4.0 %shard_map.91 = (bf16[256,1280]{1,0:T(8,128)(2,1)S(1)}, bf16[1,2,3,256,2048]{4,3,2,1,0:T(8,128)(2,1)S(1)}) custom-call(bf16[768,2048]{1,0:T(8,128)(2,1)S(1)} %get-tuple-element.100.key_ref.refs_17_, bf16[768,2048]{1,0:T(8,128)(2,1)S(1)} %get-tuple-element.101.value_ref.refs_18_, bf16[1,2,3,256,2048]{4,3,2,1,0:T(8,128)(2,1)S(1)} %get-tuple-element.99.buffer.refs_15_, ...), custom_call_target="tpu_custom_call" | custom-call | flops 2684354560 | bytes 2097152 | tf_op jit(solution)/shard_map/pallas_call | solution.py:717
  97.3 0.1 collective-permute-start.17
  97.4 0.0 collective-permute-done.11.refs_12_
  97.4 0.0 collective-permute-done.12.refs_13_
  97.5 13.6 %shard_map.92 = (bf16[768,2048]{1,0:T(8,128)(2,1)S(1)}, bf16[768,2048]{1,0:T(8,128)(2,1)S(1)}, f32[256,2048]{1,0:T(8,128)S(1)}, bf16[256,2048]{1,0:T(8,128)(2,1)S(1)}, f32[128,2048]{1,0:T(8,128)S(1)}) custom-call(s32[2,2]{1,0:T(2,128)S(1)} %collective-permute-done.refs_0_, s32[2,2]{1,0:T(2,128)S(1)} %copy-done.13, ...), custom_call_target="tpu_custom_call", output_to_operand_aliasing={{0}: (17, {}), {1}: (18, {})} | custom-call | flops 6979321856 | bytes 4194304 | tf_op jit(solution)/shard_map/pallas_call | solution.py:677
  111.1 15.8 %shard_map.93 = (bf16[768,2048]{1,0:T(8,128)(2,1)S(1)}, bf16[768,2048]{1,0:T(8,128)(2,1)S(1)}, f32[256,2048]{1,0:T(8,128)S(1)}, bf16[256,2048]{1,0:T(8,128)(2,1)S(1)}, f32[128,2048]{1,0:T(8,128)S(1)}) custom-call(s32[2,2]{1,0:T(2,128)S(1)} %collective-permute-done.refs_0_, s32[2,2]{1,0:T(2,128)S(1)} %copy-done.13, ...), custom_call_target="tpu_custom_call", output_to_operand_aliasing={{0}: (19, {}), {1}: (20, {})} | custom-call | flops 6979321856 | bytes 4194304 | tf_op jit(solution)/shard_map/pallas_call | solution.py:677
  126.9 5.0 %collective-permute-start.13 = (f32[128,2048]{1,0:T(8,128)S(1)}, f32[128,2048]{1,0:T(8,128)S(1)}, u32[]{:S(2)}, u32[]{:S(2)}) collective-permute-start(f32[128,2048]{1,0:T(8,128)S(1)} %get-tuple-element.108), channel_id=1, source_target_pairs={{0,1},{1,4},{4,5},{5,8},{8,9},{9,12},{12,13},{13,16},{16,17},{17,2... | collective-permute-start | bytes 3145736 | tf_op jit(solution)/shard_map/ppermute | solution.py:837
  131.9 1.6 collective-permute-start.15
  133.5 1.3 collective-permute-start.14
  134.8 0.0 collective-permute-done.16.refs_0_
  134.8 0.6 collective-permute-start.18
  135.4 16.3 %shard_map.95.own_ref = bf16[768,2048]{1,0:T(8,128)(2,1)S(1)} custom-call(bf16[768,2048]{1,0:T(8,128)(2,1)S(1)} %get-tuple-element.110.key_grad_ref, bf16[768,2048]{1,0:T(8,128)(2,1)S(1)} %get-tuple-element.111.value_grad_ref, bf16[4096,2048]{1,0:T(8,128)(2,1)} %key_ref.3, bf16[4096,2048]{1,0:T(8,128)(2,1)} %value_ref.3), custom_call_target="tpu_custom_call" | custom-call | flops 12884901888 | bytes 16777216 | tf_op jit(solution)/shard_map/pallas_call | solution.py:744
  151.7 0.0 collective-permute-done.17.refs_1_
  151.7 28.4 %collective-permute-done.18.refs_2_ = bf16[256,2048]{1,0:T(8,128)(2,1)S(1)} collective-permute-done((bf16[256,2048]{1,0:T(8,128)(2,1)S(1)}, bf16[256,2048]{1,0:T(8,128)(2,1)S(1)}, u32[]{:S(2)}, u32[]{:S(2)}) %collective-permute-start.18) | collective-permute-done | bytes 1048608 | tf_op jit(solution)/shard_map/ppermute | solution.py:939
  180.1 1.4 shard_map.96.refs_1_
  181.5 0.0 collective-permute-done.15.refs_0_
  181.5 1.1 shard_map.97
  182.6 0.0 collective-permute-done.13.below_ref
  182.6 0.0 collective-permute-done.14.above_ref
  182.6 1.1 shard_map.94
  (23 shorter events, 0.0 us)
Async XLA Ops:
  0.6 41.8 %collective-permute-start.1 = (s32[2,2]{1,0:T(2,128)}, s32[2,2]{1,0:T(2,128)S(1)}, u32[]{:S(2)}, u32[]{:S(2)}) collective-permute-start(s32[2,2]{1,0:T(2,128)} %refs_1_.17), channel_id=1, source_target_pairs={{1,0},{4,1},{5,4},{8,5},{9,8},{12,9},{13,12},{16,13},{17,16},{20,1... | collective-permute-start | bytes 56 | tf_op jit(solution)/shard_map/ppermute | solution.py:837
  3.2 10.5 %copy-start.6 = (bf16[768,2048]{1,0:T(8,128)(2,1)S(1)}, bf16[768,2048]{1,0:T(8,128)(2,1)}, u32[]{:S(2)}) copy-start(bf16[768,2048]{1,0:T(8,128)(2,1)} %states_ref.5) | copy-start | bytes 9437188
  3.2 26.6 %collective-permute-start.4 = (bf16[256,2048]{1,0:T(8,128)(2,1)S(1)}, bf16[256,2048]{1,0:T(8,128)(2,1)S(1)}, u32[]{:S(2)}, u32[]{:S(2)}) collective-permute-start(bf16[256,2048]{1,0:T(8,128)(2,1)S(1)} %shard_map.79), channel_id=1, source_target_pairs={{0,2},{2,0},{1,3},{3,1},{4,6},{6,4},{5,7},{7,5},{8,10},{10,8},{9,1... | collective-permute-start | bytes 3145736 | tf_op jit(solution)/shard_map/ppermute | solution.py:870
  7.8 44.5 %collective-permute-start.8 = (bf16[256,2048]{1,0:T(8,128)(2,1)S(1)}, bf16[256,2048]{1,0:T(8,128)(2,1)S(1)}, u32[]{:S(2)}, u32[]{:S(2)}) collective-permute-start(bf16[256,2048]{1,0:T(8,128)(2,1)S(1)} %get-tuple-element.79), channel_id=1, source_target_pairs={{0,2},{2,0},{1,3},{3,1},{4,6},{6,4},{5,7},{7,5},{8,10},{10,8},{9,1... | collective-permute-start | bytes 3145736 | tf_op jit(solution)/shard_map/ppermute | solution.py:870
  9.5 35.0 %collective-permute-start.2 = (bf16[128,4096]{1,0:T(8,128)(2,1)S(1)}, bf16[128,4096]{1,0:T(8,128)(2,1)S(1)}, u32[]{:S(2)}, u32[]{:S(2)}) collective-permute-start(bf16[128,4096]{1,0:T(8,128)(2,1)S(1)} %get-tuple-element.59), channel_id=1, source_target_pairs={{0,1},{1,4},{4,5},{5,8},{8,9},{9,12},{12,13},{13,16},{16,17},{17,2... | collective-permute-start | bytes 3145736 | tf_op jit(solution)/shard_map/ppermute | solution.py:837
  12.4 17.4 %copy-start.13 = (s32[2,2]{1,0:T(2,128)S(1)}, s32[2,2]{1,0:T(2,128)}, u32[]{:S(2)}) copy-start(s32[2,2]{1,0:T(2,128)} %refs_1_.17) | copy-start | bytes 52
  12.4 33.4 %collective-permute-start.3 = (bf16[128,4096]{1,0:T(8,128)(2,1)S(1)}, bf16[128,4096]{1,0:T(8,128)(2,1)S(1)}, u32[]{:S(2)}, u32[]{:S(2)}) collective-permute-start(bf16[128,4096]{1,0:T(8,128)(2,1)S(1)} %get-tuple-element.60), channel_id=1, source_target_pairs={{1,0},{4,1},{5,4},{8,5},{9,8},{12,9},{13,12},{16,13},{17,16},{20,1... | collective-permute-start | bytes 3145736 | tf_op jit(solution)/shard_map/ppermute | solution.py:837
  29.8 13.9 %collective-permute-start = (s32[2,2]{1,0:T(2,128)S(1)}, s32[2,2]{1,0:T(2,128)S(1)}, u32[]{:S(2)}, u32[]{:S(2)}) collective-permute-start(s32[2,2]{1,0:T(2,128)S(1)} %copy-done.13), channel_id=1, source_target_pairs={{0,1},{1,4},{4,5},{5,8},{8,9},{9,12},{12,13},{13,16},{16,17},{17,2... | collective-permute-start | bytes 56 | tf_op jit(solution)/shard_map/ppermute | solution.py:837
  34.3 11.4 %copy-start = (bf16[256,2048]{1,0:T(8,128)(2,1)S(1)}, bf16[256,2048]{1,0:T(8,128)(2,1)}, u32[]{:S(2)}) copy-start(bf16[256,2048]{1,0:T(8,128)(2,1)} %refs_3_.13) | copy-start | bytes 3145732
  34.4 11.4 %copy-start.1 = (bf16[256,2048]{1,0:T(8,128)(2,1)S(1)}, bf16[256,2048]{1,0:T(8,128)(2,1)}, u32[]{:S(2)}) copy-start(bf16[256,2048]{1,0:T(8,128)(2,1)} %refs_4_.13) | copy-start | bytes 3145732
  42.4 7.0 %copy-start.7 = (bf16[256,2048]{1,0:T(8,128)(2,1)}, bf16[256,2048]{1,0:T(8,128)(2,1)S(1)}, u32[]{:S(2)}) copy-start(bf16[256,2048]{1,0:T(8,128)(2,1)S(1)} %get-tuple-element.64.refs_8_) | copy-start | bytes 3145732
  42.5 37.1 %collective-permute-start.5 = (bf16[128,1024]{1,0:T(8,128)(2,1)S(1)}, bf16[128,1024]{1,0:T(8,128)(2,1)S(1)}, u32[]{:S(2)}, u32[]{:S(2)}) collective-permute-start(bf16[128,1024]{1,0:T(8,128)(2,1)S(1)} %get-tuple-element.67), channel_id=1, source_target_pairs={{0,2},{2,0},{1,3},{3,1},{4,6},{6,4},{5,7},{7,5},{8,10},{10,8},{9,1... | collective-permute-start | bytes 786440 | tf_op jit(solution)/shard_map/ppermute | solution.py:870
  43.7 38.0 %collective-permute-start.6 = (bf16[128,1024]{1,0:T(8,128)(2,1)S(1)}, bf16[128,1024]{1,0:T(8,128)(2,1)S(1)}, u32[]{:S(2)}, u32[]{:S(2)}) collective-permute-start(bf16[128,1024]{1,0:T(8,128)(2,1)S(1)} %get-tuple-element.71), channel_id=1, source_target_pairs={{0,2},{2,0},{1,3},{3,1},{4,6},{6,4},{5,7},{7,5},{8,10},{10,8},{9,1... | collective-permute-start | bytes 786440 | tf_op jit(solution)/shard_map/ppermute | solution.py:870
  44.6 13.4 %copy-start.2 = (bf16[128,4096]{1,0:T(8,128)(2,1)}, bf16[128,4096]{1,0:T(8,128)(2,1)S(1)}, u32[]{:S(2)}) copy-start(bf16[128,4096]{1,0:T(8,128)(2,1)S(1)} %collective-permute-done.2.refs_5_) | copy-start | bytes 3145732
  44.6 30.2 %collective-permute-start.7 = (bf16[128,2048]{1,0:T(8,128)(2,1)S(1)}, bf16[128,2048]{1,0:T(8,128)(2,1)S(1)}, u32[]{:S(2)}, u32[]{:S(2)}) collective-permute-start(bf16[128,2048]{1,0:T(8,128)(2,1)S(1)} %get-tuple-element.74), channel_id=1, source_target_pairs={{0,2},{2,0},{1,3},{3,1},{4,6},{6,4},{5,7},{7,5},{8,10},{10,8},{9,1... | collective-permute-start | bytes 1572872 | tf_op jit(solution)/shard_map/ppermute | solution.py:870
  45.8 12.2 %copy-start.4 = (bf16[128,4096]{1,0:T(8,128)(2,1)}, bf16[128,4096]{1,0:T(8,128)(2,1)S(1)}, u32[]{:S(2)}) copy-start(bf16[128,4096]{1,0:T(8,128)(2,1)S(1)} %collective-permute-done.3.refs_6_) | copy-start | bytes 3145732
  58.0 4.1 %copy-start.9 = (bf16[256,2048]{1,0:T(8,128)(2,1)}, bf16[256,2048]{1,0:T(8,128)(2,1)S(1)}, u32[]{:S(2)}) copy-start(bf16[256,2048]{1,0:T(8,128)(2,1)S(1)} %get-tuple-element.80.refs_7_) | copy-start | bytes 3145732
  58.0 4.1 %copy-start.11 = (bf16[256,2048]{1,0:T(8,128)(2,1)}, bf16[256,2048]{1,0:T(8,128)(2,1)S(1)}, u32[]{:S(2)}) copy-start(bf16[256,2048]{1,0:T(8,128)(2,1)S(1)} %get-tuple-element.81.refs_8_) | copy-start | bytes 3145732
  62.1 24.2 %collective-permute-start.9 = (f32[16,8,128]{2,1,0:T(8,128)S(1)}, f32[16,8,128]{2,1,0:T(8,128)S(1)}, u32[]{:S(2)}, u32[]{:S(2)}) collective-permute-start(f32[16,8,128]{2,1,0:T(8,128)S(1)} %get-tuple-element.90), channel_id=1, source_target_pairs={{0,1},{1,0},{4,5},{5,4},{8,9},{9,8},{12,13},{13,12},{16,17},{17,16... | collective-permute-start | bytes 196616 | tf_op jit(solution)/shard_map/ppermute | solution.py:844
  63.1 23.2 %collective-permute-start.10 = (f32[16,8,128]{2,1,0:T(8,128)S(1)}, f32[16,8,128]{2,1,0:T(8,128)S(1)}, u32[]{:S(2)}, u32[]{:S(2)}) collective-permute-start(f32[16,8,128]{2,1,0:T(8,128)S(1)} %get-tuple-element.91), channel_id=1, source_target_pairs={{1,4},{4,1},{5,8},{8,5},{9,12},{12,9},{13,16},{16,13},{17,20},{20,... | collective-permute-start | bytes 196616 | tf_op jit(solution)/shard_map/ppermute | solution.py:844
  85.1 12.3 %collective-permute-start.11 = (f32[16,8,128]{2,1,0:T(8,128)S(1)}, f32[16,8,128]{2,1,0:T(8,128)S(1)}, u32[]{:S(2)}, u32[]{:S(2)}) collective-permute-start(f32[16,8,128]{2,1,0:T(8,128)S(1)} %get-tuple-element.92), channel_id=1, source_target_pairs={{0,1},{1,0},{4,5},{5,4},{8,9},{9,8},{12,13},{13,12},{16,17},{17,16... | collective-permute-start | bytes 196616 | tf_op jit(solution)/shard_map/ppermute | solution.py:844
  85.4 12.0 %collective-permute-start.12 = (f32[16,8,128]{2,1,0:T(8,128)S(1)}, f32[16,8,128]{2,1,0:T(8,128)S(1)}, u32[]{:S(2)}, u32[]{:S(2)}) collective-permute-start(f32[16,8,128]{2,1,0:T(8,128)S(1)} %get-tuple-element.93), channel_id=1, source_target_pairs={{1,4},{4,1},{5,8},{8,5},{9,12},{12,9},{13,16},{16,13},{17,20},{20,... | collective-permute-start | bytes 196616 | tf_op jit(solution)/shard_map/ppermute | solution.py:844
  91.1 43.7 %collective-permute-start.16 = (bf16[256,768]{1,0:T(8,128)(2,1)S(1)}, bf16[256,768]{1,0:T(8,128)(2,1)S(1)}, u32[]{:S(2)}, u32[]{:S(2)}) collective-permute-start(bf16[256,768]{1,0:T(8,128)(2,1)S(1)} %get-tuple-element.113), channel_id=1, source_target_pairs={{0,2},{2,0},{1,3},{3,1},{4,6},{6,4},{5,7},{7,5},{8,10},{10,8},{9,1... | collective-permute-start | bytes 1179656 | tf_op jit(solution)/shard_map/ppermute | solution.py:939
  93.3 4.1 %copy-start.3 = (bf16[128,4096]{1,0:T(8,128)(2,1)S(1)}, bf16[128,4096]{1,0:T(8,128)(2,1)}, u32[]{:S(2)}) copy-start(bf16[128,4096]{1,0:T(8,128)(2,1)} %copy-done.2) | copy-start | bytes 3145732
  93.3 4.1 %copy-start.5 = (bf16[128,4096]{1,0:T(8,128)(2,1)S(1)}, bf16[128,4096]{1,0:T(8,128)(2,1)}, u32[]{:S(2)}) copy-start(bf16[128,4096]{1,0:T(8,128)(2,1)} %copy-done.4) | copy-start | bytes 3145732
  93.3 4.1 %copy-start.8 = (bf16[256,2048]{1,0:T(8,128)(2,1)S(1)}, bf16[256,2048]{1,0:T(8,128)(2,1)}, u32[]{:S(2)}) copy-start(bf16[256,2048]{1,0:T(8,128)(2,1)} %copy-done.7) | copy-start | bytes 3145732
  97.3 54.4 %collective-permute-start.17 = (bf16[256,1280]{1,0:T(8,128)(2,1)S(1)}, bf16[256,1280]{1,0:T(8,128)(2,1)S(1)}, u32[]{:S(2)}, u32[]{:S(2)}) collective-permute-start(bf16[256,1280]{1,0:T(8,128)(2,1)S(1)} %get-tuple-element.114), channel_id=1, source_target_pairs={{0,2},{2,0},{1,3},{3,1},{4,6},{6,4},{5,7},{7,5},{8,10},{10,8},{9,1... | collective-permute-start | bytes 1966088 | tf_op jit(solution)/shard_map/ppermute | solution.py:953
  97.5 13.6 %copy-start.10 = (bf16[256,2048]{1,0:T(8,128)(2,1)S(1)}, bf16[256,2048]{1,0:T(8,128)(2,1)}, u32[]{:S(2)}) copy-start(bf16[256,2048]{1,0:T(8,128)(2,1)} %copy-done.9) | copy-start | bytes 3145732
  97.5 13.6 %copy-start.12 = (bf16[256,2048]{1,0:T(8,128)(2,1)S(1)}, bf16[256,2048]{1,0:T(8,128)(2,1)}, u32[]{:S(2)}) copy-start(bf16[256,2048]{1,0:T(8,128)(2,1)} %copy-done.11) | copy-start | bytes 3145732
  126.9 55.6 %collective-permute-start.13 = (f32[128,2048]{1,0:T(8,128)S(1)}, f32[128,2048]{1,0:T(8,128)S(1)}, u32[]{:S(2)}, u32[]{:S(2)}) collective-permute-start(f32[128,2048]{1,0:T(8,128)S(1)} %get-tuple-element.108), channel_id=1, source_target_pairs={{0,1},{1,4},{4,5},{5,8},{8,9},{9,12},{12,13},{13,16},{16,17},{17,2... | collective-permute-start | bytes 3145736 | tf_op jit(solution)/shard_map/ppermute | solution.py:837
  131.9 49.6 %collective-permute-start.15 = (bf16[256,2048]{1,0:T(8,128)(2,1)S(1)}, bf16[256,2048]{1,0:T(8,128)(2,1)S(1)}, u32[]{:S(2)}, u32[]{:S(2)}) collective-permute-start(bf16[256,2048]{1,0:T(8,128)(2,1)S(1)} %get-tuple-element.112), channel_id=1, source_target_pairs={{0,2},{2,0},{1,3},{3,1},{4,6},{6,4},{5,7},{7,5},{8,10},{10,8},{9,1... | collective-permute-start | bytes 3145736 | tf_op jit(solution)/shard_map/ppermute | solution.py:939
  133.5 49.1 %collective-permute-start.14 = (f32[128,2048]{1,0:T(8,128)S(1)}, f32[128,2048]{1,0:T(8,128)S(1)}, u32[]{:S(2)}, u32[]{:S(2)}) collective-permute-start(f32[128,2048]{1,0:T(8,128)S(1)} %get-tuple-element.109), channel_id=1, source_target_pairs={{1,0},{4,1},{5,4},{8,5},{9,8},{12,9},{13,12},{16,13},{17,16},{20,1... | collective-permute-start | bytes 3145736 | tf_op jit(solution)/shard_map/ppermute | solution.py:837
  134.8 45.2 %collective-permute-start.18 = (bf16[256,2048]{1,0:T(8,128)(2,1)S(1)}, bf16[256,2048]{1,0:T(8,128)(2,1)S(1)}, u32[]{:S(2)}, u32[]{:S(2)}) collective-permute-start(bf16[256,2048]{1,0:T(8,128)(2,1)S(1)} %get-tuple-element.115), channel_id=1, source_target_pairs={{0,2},{2,0},{1,3},{3,1},{4,6},{6,4},{5,7},{7,5},{8,10},{10,8},{9,1... | collective-permute-start | bytes 3145736 | tf_op jit(solution)/shard_map/ppermute | solution.py:939
